TPU v7x, 128 devices: a whole 4x4x4 slice. The times are simulated.
128 devices in a mesh: heads: 4 (over z), seq: 32 (over x, y, core).
Axes of the slice: x: 4, y: 4, z: 4, core: 2. Of those that a mesh axis runs over, the one named last changes fastest.
Arguments:
- queries: bfloat16 [8, 64, 128, 128], P(None, None, 'heads'), may hold values from -12 to 12
- prefix_keys: bfloat16 [192, 128, 8, 128], P('seq', None, 'heads'), may hold values from -6 to 6
- prefix_values: bfloat16 [192, 128, 8, 128], P('seq', None, 'heads'), may hold values from -6 to 6
- block_use: int32 [8, 192], P(None, 'seq'), may hold values 0 or 1
- private_keys: bfloat16 [8, 8192, 8, 128], P(None, 'seq', 'heads'), may hold values from -6 to 6
- private_values: bfloat16 [8, 8192, 8, 128], P(None, 'seq', 'heads'), may hold values from -6 to 6
- private_lengths: int32 [8], replicated, may hold values from 1 to 8192
- draft_keys: bfloat16 [8, 64, 8, 128], P(None, None, 'heads'), may hold values from -10 to 10
- draft_values: bfloat16 [8, 64, 8, 128], P(None, None, 'heads'), may hold values from -6 to 6
- parents: int32 [8, 64], replicated, may hold values from 0 to 62, as said below
- out_weight: bfloat16 [128, 128, 16384], P('heads', None, 'seq'), may hold values from -0.046875 to 0.046875
Outputs:
- mixed: float32 [8, 64, 16384], P('heads', None, 'seq')
Inputs may be any that keep to these rules, and one draw needn't show every extreme that they name: parents[r, 0] = 0, parents[r, t] < t for t >= 1, and the parent of token 63 is token 62.
All inputs are finite; a program needn't handle non-finite values. No bound on the sum of `block_use` on one device may be relied on, other than what follows from the above.
Results may differ from a plain program's by a relative error of at most 0.0047.
Values may be sent and summed in bfloat16 or wider, within the bound.
A program may use at most 128 MiB of HBM per device.

v0:
```python
import math

import jax
import jax.numpy as jnp
from jax import lax
from jax.sharding import PartitionSpec as P


def ancestry(parents):
    tree_size = parents.shape[-1]
    places = jnp.arange(tree_size, dtype=jnp.int32)
    onestep = (parents[..., None] == places).astype(jnp.float32)
    ident = (places[:, None] == places[None, :]).astype(jnp.float32)
    reach = jnp.maximum(onestep, ident)
    for level in range(max(1, (tree_size - 1).bit_length())):
        reach = jnp.minimum(
            jnp.einsum("rij,rjk->rik", reach, reach, precision=lax.Precision.HIGHEST), 1.0
        )
    return reach


def combine(first, second):
    top = jnp.maximum(first[0], second[0])
    first_factor = jnp.exp(first[0] - top)
    second_factor = jnp.exp(second[0] - top)
    totals = first[1] * first_factor + second[1] * second_factor
    weighted = first[2] * first_factor[..., None] + second[2] * second_factor[..., None]
    return (top, totals, weighted)


def draft_part(row_queries, tree_keys, tree_values, row_reach, scaling):
    requests, rows, heads_dev, head_dim = row_queries.shape
    kv_dev = tree_keys.shape[2]
    group_size = heads_dev // kv_dev
    grouped = row_queries.reshape(requests, rows, kv_dev, group_size, head_dim)
    scores = (
        jnp.einsum("rtkgd,rskd->rtkgs", grouped, tree_keys, preferred_element_type=jnp.float32)
        * scaling
    )
    live = (row_reach > 0.5)[:, :, None, None, :]
    scores = jnp.where(live, scores, -1e30)
    highest = jnp.max(scores, axis=-1)
    weights = jnp.where(live, jnp.exp(scores - highest[..., None]), 0.0)
    totals = jnp.sum(weights, axis=-1)
    weighted = jnp.einsum(
        "rtkgs,rskd->rtkgd",
        weights.astype(jnp.bfloat16),
        tree_values,
        preferred_element_type=jnp.float32,
    )
    return (
        highest.reshape(requests, rows, heads_dev),
        totals.reshape(requests, rows, heads_dev),
        weighted.reshape(requests, rows, heads_dev, head_dim),
    )


def local(
    queries,
    prefix_keys,
    prefix_values,
    block_use,
    private_keys,
    private_values,
    private_lengths,
    draft_keys,
    draft_values,
    parents,
    out_weight,
):
    tree_size = queries.shape[1]
    heads_dev = queries.shape[2]
    head_dim = queries.shape[3]
    kv_dev = prefix_keys.shape[2]
    group_size = heads_dev // kv_dev
    block_count = prefix_keys.shape[0]
    block_len = prefix_keys.shape[1]
    private_dev = private_keys.shape[1]
    scaling = 1.0 / math.sqrt(head_dim)
    shard_index = lax.axis_index("seq")
    prefix_flat_keys = prefix_keys.reshape(block_count * block_len, kv_dev, head_dim)
    prefix_flat_values = prefix_values.reshape(block_count * block_len, kv_dev, head_dim)
    positions = shard_index * private_dev + jnp.arange(private_dev, dtype=jnp.int32)
    reach = ancestry(parents)

    def one_request(item):
        query_rows, use_row, length, own_keys, own_values = item
        grouped = query_rows.reshape(tree_size, kv_dev, group_size, head_dim)
        prefix_live = jnp.repeat(use_row == 1, block_len)
        own_live = positions < length
        prefix_scores = (
            jnp.einsum(
                "tkgd,nkd->tkgn", grouped, prefix_flat_keys, preferred_element_type=jnp.float32
            )
            * scaling
        )
        own_scores = (
            jnp.einsum("tkgd,nkd->tkgn", grouped, own_keys, preferred_element_type=jnp.float32)
            * scaling
        )
        prefix_scores = jnp.where(prefix_live, prefix_scores, -1e30)
        own_scores = jnp.where(own_live, own_scores, -1e30)
        highest = jnp.maximum(jnp.max(prefix_scores, axis=-1), jnp.max(own_scores, axis=-1))
        prefix_weights = jnp.where(prefix_live, jnp.exp(prefix_scores - highest[..., None]), 0.0)
        own_weights = jnp.where(own_live, jnp.exp(own_scores - highest[..., None]), 0.0)
        totals = jnp.sum(prefix_weights, axis=-1) + jnp.sum(own_weights, axis=-1)
        weighted = jnp.einsum(
            "tkgn,nkd->tkgd",
            prefix_weights.astype(jnp.bfloat16),
            prefix_flat_values,
            preferred_element_type=jnp.float32,
        )
        weighted = weighted + jnp.einsum(
            "tkgn,nkd->tkgd",
            own_weights.astype(jnp.bfloat16),
            own_values,
            preferred_element_type=jnp.float32,
        )
        return (
            highest.reshape(tree_size, heads_dev),
            totals.reshape(tree_size, heads_dev),
            weighted.reshape(tree_size, heads_dev, head_dim),
        )

    highest, totals, weighted = lax.map(
        one_request, (queries, block_use, private_lengths, private_keys, private_values)
    )
    top_all = lax.pmax(highest, "seq")
    factor = jnp.exp(highest - top_all)
    summed_totals, summed_weighted = lax.psum(
        (totals * factor, weighted * factor[..., None]), "seq"
    )
    draft = draft_part(queries, draft_keys, draft_values, reach, scaling)
    final_top, final_totals, final_weighted = combine(
        (top_all, summed_totals, summed_weighted), draft
    )
    attention = (final_weighted / final_totals[..., None]).astype(jnp.bfloat16)
    return lax.psum_scatter(
        jnp.einsum("rthd,hde->rte", attention, out_weight, preferred_element_type=jnp.float32),
        "heads",
        scatter_dimension=0,
        tiled=True,
    )


def solution(mesh):
    return jax.shard_map(
        local,
        mesh=mesh,
        in_specs=(
            P(None, None, "heads", None),
            P("seq", None, "heads", None),
            P("seq", None, "heads", None),
            P(None, "seq"),
            P(None, "seq", "heads", None),
            P(None, "seq", "heads", None),
            P(),
            P(None, None, "heads", None),
            P(None, None, "heads", None),
            P(),
            P("heads", None, "seq"),
        ),
        out_specs=P("heads", None, "seq"),
        check_vma=False,
    )
```

profile of v0, /device:TPU:0, one launch (start us, length us, event | category | flops | bytes accessed | tf_op | source)
XLA Modules:
  0.0 472.2 jit_solution(4256542227768642580)
XLA Ops:
  6.5 1.9 copy.100
  8.4 1.8 copy.101
  10.2 184.2 %while.15 = (s32[]{:T(128)}, f32[8,64,32]{1,2,0:T(8,128)}, f32[8,64,32]{1,2,0:T(8,128)}, f32[8,64,32,128]{3,2,1,0:T(8,128)}, s32[8,6]{1,0:T(8,128)}, /*index=5*/...) while((s32[]{:T(128)}, f32[8,64,32]{1,2,0:T(8,128)}, ...), condition=%wide.region_5.6_spmd.clone, body=%wide.region_0.5_spmd.clone.sunk | while | flops 1099166208 | bytes 61590624 | solution.py:125
  10.2 1.2 dynamic_slice.37
  12.8 1.1 constant_dynamic-slice_fusion.7
  14.0 1.1 constant_dynamic-slice_fusion.6
  15.7 4.8 %bitcast_reduce_fusion.4 = (f32[64,2,16]{2,0,1:T(8,128)S(1)}, f32[2,64,16,768]{3,2,1,0:T(8,128)}) fusion(pred[768]{0:T(1024)(128)(4,1)S(1)} %broadcast_bitcast_fusion.2, bf16[768,2,128]{2,0,1:T(8,128)(2,1)} %get-tuple-element.323, bf16[64,2,16,128]{3,2,1,0:T(8,128)(2,1)S(1)} %bitcast.157), kind=kOutput, calls=%fused_computation.2.clone.1 | convolution fusion | flops 407369728 | bytes 7217920 | tf_op jit(solution)/shard_map/while/body/eval_jaxpr/tkgd,nkd->tkgn/dot_general | solution.py:92
  20.5 2.1 fusion.80
  22.7 4.5 fusion.79
  27.4 2.6 fusion.81
  33.2 1.2 dynamic_slice.37
  35.8 1.1 constant_dynamic-slice_fusion.7
  38.7 4.8 %bitcast_reduce_fusion.4 = (f32[64,2,16]{2,0,1:T(8,128)S(1)}, f32[2,64,16,768]{3,2,1,0:T(8,128)}) fusion(pred[768]{0:T(1024)(128)(4,1)S(1)} %broadcast_bitcast_fusion.2, bf16[768,2,128]{2,0,1:T(8,128)(2,1)} %get-tuple-element.323, bf16[64,2,16,128]{3,2,1,0:T(8,128)(2,1)S(1)} %bitcast.157), kind=kOutput, calls=%fused_computation.2.clone.1 | convolution fusion | flops 407369728 | bytes 7217920 | tf_op jit(solution)/shard_map/while/body/eval_jaxpr/tkgd,nkd->tkgn/dot_general | solution.py:92
  43.5 2.1 fusion.80
  45.7 4.5 fusion.79
  50.4 2.6 fusion.81
  56.3 1.2 dynamic_slice.37
  58.9 1.1 constant_dynamic-slice_fusion.7
  61.7 4.8 %bitcast_reduce_fusion.4 = (f32[64,2,16]{2,0,1:T(8,128)S(1)}, f32[2,64,16,768]{3,2,1,0:T(8,128)}) fusion(pred[768]{0:T(1024)(128)(4,1)S(1)} %broadcast_bitcast_fusion.2, bf16[768,2,128]{2,0,1:T(8,128)(2,1)} %get-tuple-element.323, bf16[64,2,16,128]{3,2,1,0:T(8,128)(2,1)S(1)} %bitcast.157), kind=kOutput, calls=%fused_computation.2.clone.1 | convolution fusion | flops 407369728 | bytes 7217920 | tf_op jit(solution)/shard_map/while/body/eval_jaxpr/tkgd,nkd->tkgn/dot_general | solution.py:92
  66.6 2.1 fusion.80
  68.8 4.5 fusion.79
  73.4 2.6 fusion.81
  79.3 1.2 dynamic_slice.37
  81.9 1.1 constant_dynamic-slice_fusion.7
  84.8 4.8 %bitcast_reduce_fusion.4 = (f32[64,2,16]{2,0,1:T(8,128)S(1)}, f32[2,64,16,768]{3,2,1,0:T(8,128)}) fusion(pred[768]{0:T(1024)(128)(4,1)S(1)} %broadcast_bitcast_fusion.2, bf16[768,2,128]{2,0,1:T(8,128)(2,1)} %get-tuple-element.323, bf16[64,2,16,128]{3,2,1,0:T(8,128)(2,1)S(1)} %bitcast.157), kind=kOutput, calls=%fused_computation.2.clone.1 | convolution fusion | flops 407369728 | bytes 7217920 | tf_op jit(solution)/shard_map/while/body/eval_jaxpr/tkgd,nkd->tkgn/dot_general | solution.py:92
  89.6 2.1 fusion.80
  91.8 4.5 fusion.79
  96.5 2.6 fusion.81
  102.3 1.2 dynamic_slice.37
  104.9 1.1 constant_dynamic-slice_fusion.7
  107.8 4.8 %bitcast_reduce_fusion.4 = (f32[64,2,16]{2,0,1:T(8,128)S(1)}, f32[2,64,16,768]{3,2,1,0:T(8,128)}) fusion(pred[768]{0:T(1024)(128)(4,1)S(1)} %broadcast_bitcast_fusion.2, bf16[768,2,128]{2,0,1:T(8,128)(2,1)} %get-tuple-element.323, bf16[64,2,16,128]{3,2,1,0:T(8,128)(2,1)S(1)} %bitcast.157), kind=kOutput, calls=%fused_computation.2.clone.1 | convolution fusion | flops 407369728 | bytes 7217920 | tf_op jit(solution)/shard_map/while/body/eval_jaxpr/tkgd,nkd->tkgn/dot_general | solution.py:92
  112.6 2.1 fusion.80
  114.8 4.5 fusion.79
  119.5 2.6 fusion.81
  125.3 1.2 dynamic_slice.37
  127.9 1.1 constant_dynamic-slice_fusion.7
  130.8 4.8 %bitcast_reduce_fusion.4 = (f32[64,2,16]{2,0,1:T(8,128)S(1)}, f32[2,64,16,768]{3,2,1,0:T(8,128)}) fusion(pred[768]{0:T(1024)(128)(4,1)S(1)} %broadcast_bitcast_fusion.2, bf16[768,2,128]{2,0,1:T(8,128)(2,1)} %get-tuple-element.323, bf16[64,2,16,128]{3,2,1,0:T(8,128)(2,1)S(1)} %bitcast.157), kind=kOutput, calls=%fused_computation.2.clone.1 | convolution fusion | flops 407369728 | bytes 7217920 | tf_op jit(solution)/shard_map/while/body/eval_jaxpr/tkgd,nkd->tkgn/dot_general | solution.py:92
  135.6 2.1 fusion.80
  137.8 4.5 fusion.79
  142.5 2.6 fusion.81
  148.4 1.2 dynamic_slice.37
  151.0 1.1 constant_dynamic-slice_fusion.7
  153.8 4.8 %bitcast_reduce_fusion.4 = (f32[64,2,16]{2,0,1:T(8,128)S(1)}, f32[2,64,16,768]{3,2,1,0:T(8,128)}) fusion(pred[768]{0:T(1024)(128)(4,1)S(1)} %broadcast_bitcast_fusion.2, bf16[768,2,128]{2,0,1:T(8,128)(2,1)} %get-tuple-element.323, bf16[64,2,16,128]{3,2,1,0:T(8,128)(2,1)S(1)} %bitcast.157), kind=kOutput, calls=%fused_computation.2.clone.1 | convolution fusion | flops 407369728 | bytes 7217920 | tf_op jit(solution)/shard_map/while/body/eval_jaxpr/tkgd,nkd->tkgn/dot_general | solution.py:92
  158.7 2.1 fusion.80
  160.9 4.5 fusion.79
  165.5 2.6 fusion.81
  171.4 1.2 dynamic_slice.37
  174.0 1.1 constant_dynamic-slice_fusion.7
  176.8 4.8 %bitcast_reduce_fusion.4 = (f32[64,2,16]{2,0,1:T(8,128)S(1)}, f32[2,64,16,768]{3,2,1,0:T(8,128)}) fusion(pred[768]{0:T(1024)(128)(4,1)S(1)} %broadcast_bitcast_fusion.2, bf16[768,2,128]{2,0,1:T(8,128)(2,1)} %get-tuple-element.323, bf16[64,2,16,128]{3,2,1,0:T(8,128)(2,1)S(1)} %bitcast.157), kind=kOutput, calls=%fused_computation.2.clone.1 | convolution fusion | flops 407369728 | bytes 7217920 | tf_op jit(solution)/shard_map/while/body/eval_jaxpr/tkgd,nkd->tkgn/dot_general | solution.py:92
  181.7 2.1 fusion.80
  183.9 4.5 fusion.79
  188.5 2.6 fusion.81
  194.5 103.6 %all-reduce.4.cloned.1.call-done = f32[8,64,32]{1,2,0:T(8,128)} async-done(((f32[8,64,32]{1,2,0:T(8,128)}), f32[8,64,32]{1,2,0:T(8,128)}) %all-reduce.4.cloned.1.call-update) | async-done | bytes 65552 | tf_op jit(solution)/shard_map/pmax | solution.py:128
  298.1 1.7 fusion.57
  300.0 7.9 %broadcast_multiply_fusion = f32[8,64,32,128]{3,2,1,0:T(8,128)} fusion(f32[8,64,32,128]{3,2,1,0:T(8,128)} %get-tuple-element.69, f32[8,64,32]{2,1,0:T(8,128)S(1)} %copy.104), kind=kLoop, calls=%fused_computation.57 | loop fusion | flops 2097152 | bytes 16842752 | tf_op jit(solution)/shard_map/mul | solution.py:131
  311.2 6.1 %fusion.31 = (f32[8,64,2,16]{1,3,2,0:T(8,128)S(1)}, f32[8,2,64,64,16]{3,2,4,1,0:T(8,128)S(1)}) fusion(pred[8,64,64]{1,2,0:T(8,128)(4,1)S(1)} %copy.105, bf16[8,64,2,16,128]{4,3,2,1,0:T(8,128)(2,1)} %bitcast.159, bf16[8,64,2,128,1]{3,2,1,0,4:T(2,128)(2,1)S(1)} %bitcast.163), kind=kOutput, calls=%fused_computation.49 | convolution fusion | flops 271564800 | bytes 8749056 | tf_op jit(solution)/shard_map/rtkgd,rskd->rtkgs/dot_general | solution.py:37
  317.3 4.6 fusion.32
  321.9 7.2 %copy.109 = bf16[8,64,2,16,64]{4,3,1,2,0:T(8,128)(2,1)} copy(bf16[8,64,2,16,64]{1,4,3,2,0:T(8,128)(2,1)} %get-tuple-element.199) | data formatting | bytes 4194304 | tf_op jit(solution)/shard_map/convert_element_type | solution.py:47
  329.1 3.6 convolution_bitcast_fusion.1
  332.8 4.3 copy.111
  337.1 90.9 %all-reduce.6.cloned.1.call-done = (f32[8,64,32,128]{3,2,1,0:T(8,128)}, f32[8,64,32]{1,2,0:T(8,128)}) async-done(((f32[8,64,32,128]{3,2,1,0:T(8,128)}, f32[8,64,32]{1,2,0:T(8,128)}), (f32[8,64,32,128]{3,2,1,0:T(8,128)}, f32[8,64,32]{1,2,0:T(8,128)})) %all-reduce.6.cloned.1.call-update) | async-done | bytes 8454160 | tf_op jit(solution)/shard_map/psum | solution.py:130
  429.4 9.3 %fusion.30 = bf16[8,64,32,128]{3,2,1,0:T(8,128)(2,1)S(1)} fusion(f32[8,64,2,16,128]{4,3,2,1,0:T(8,128)} %copy.111, f32[8,64,32,128]{3,2,1,0:T(8,128)} %get-tuple-element.183, f32[8,64,32]{2,1,0:T(8,128)S(1)} %copy.113, f32[8,64,32]{2,1,0:T(8,128)S(1)} %copy.112, f32[8,64,32]{2,1,0:T(8,128)S(1)} %copy.108), kind=kLoop, calls=%fused_computation.46 | loop fusion | flops 10485760 | bytes 21168128 | tf_op jit(solution)/shard_map/convert_element_type | solution.py:137
  438.7 3.3 fusion.39
  442.1 23.6 %reduce-scatter.2.cloned.1.call-done = f32[2,64,512]{2,1,0:T(8,128)} async-done(((f32[8,64,512]{2,1,0:T(8,128)}), f32[2,64,512]{2,1,0:T(8,128)}) %reduce-scatter.2.cloned.1.call-update) | async-done | bytes 262160 | tf_op jit(solution)/shard_map/reduce_scatter | solution.py:138
  (231 shorter events, 56.3 us)
Async XLA Ops:
  6.5 322.6 %copy-start = (bf16[8,64,2,128]{3,2,1,0:T(2,128)(2,1)S(1)}, bf16[8,64,2,128]{3,2,1,0:T(2,128)(2,1)}, u32[]{:S(2)}) copy-start(bf16[8,64,2,128]{3,2,1,0:T(2,128)(2,1)} %param.21) | copy-start | bytes 786436
  6.5 291.6 %all-reduce.4.cloned.1.call-start = ((), (), s32[]{:S(2)}) async-start(), calls=%async_computation.1 | async-start | bytes 262144 | tf_op jit(solution)/shard_map/pmax | solution.py:128
  12.0 3.6 copy-start.7
  12.8 7.6 %copy-start.4 = (pred[768]{0:T(1024)(128)(4,1)}, pred[768]{0:T(1024)(128)(4,1)S(1)}, u32[]{:S(2)}) copy-start(pred[768]{0:T(1024)(128)(4,1)S(1)} %broadcast_bitcast_fusion.2) | copy-start | bytes 2308 | tf_op jit(solution)/shard_map/while
  22.6 4.6 copy-start.5
  22.7 4.6 copy-start.1
  27.4 3.4 copy-start.2
  35.0 3.6 copy-start.7
  35.8 7.6 %copy-start.4 = (pred[768]{0:T(1024)(128)(4,1)}, pred[768]{0:T(1024)(128)(4,1)S(1)}, u32[]{:S(2)}) copy-start(pred[768]{0:T(1024)(128)(4,1)S(1)} %broadcast_bitcast_fusion.2) | copy-start | bytes 2308 | tf_op jit(solution)/shard_map/while
  45.6 4.6 copy-start.5
  45.7 4.6 copy-start.1
  50.4 3.4 copy-start.2
  58.1 3.7 copy-start.7
  58.9 7.7 %copy-start.4 = (pred[768]{0:T(1024)(128)(4,1)}, pred[768]{0:T(1024)(128)(4,1)S(1)}, u32[]{:S(2)}) copy-start(pred[768]{0:T(1024)(128)(4,1)S(1)} %broadcast_bitcast_fusion.2) | copy-start | bytes 2308 | tf_op jit(solution)/shard_map/while
  68.7 4.6 copy-start.5
  68.8 4.6 copy-start.1
  73.4 3.4 copy-start.2
  81.1 3.7 copy-start.7
  81.9 7.7 %copy-start.4 = (pred[768]{0:T(1024)(128)(4,1)}, pred[768]{0:T(1024)(128)(4,1)S(1)}, u32[]{:S(2)}) copy-start(pred[768]{0:T(1024)(128)(4,1)S(1)} %broadcast_bitcast_fusion.2) | copy-start | bytes 2308 | tf_op jit(solution)/shard_map/while
  91.7 4.6 copy-start.5
  91.8 4.6 copy-start.1
  96.5 3.4 copy-start.2
  104.1 3.6 copy-start.7
  104.9 7.6 %copy-start.4 = (pred[768]{0:T(1024)(128)(4,1)}, pred[768]{0:T(1024)(128)(4,1)S(1)}, u32[]{:S(2)}) copy-start(pred[768]{0:T(1024)(128)(4,1)S(1)} %broadcast_bitcast_fusion.2) | copy-start | bytes 2308 | tf_op jit(solution)/shard_map/while
  114.8 4.6 copy-start.5
  114.8 4.6 copy-start.1
  119.5 3.4 copy-start.2
  127.1 3.6 copy-start.7
  127.9 7.6 %copy-start.4 = (pred[768]{0:T(1024)(128)(4,1)}, pred[768]{0:T(1024)(128)(4,1)S(1)}, u32[]{:S(2)}) copy-start(pred[768]{0:T(1024)(128)(4,1)S(1)} %broadcast_bitcast_fusion.2) | copy-start | bytes 2308 | tf_op jit(solution)/shard_map/while
  137.8 4.6 copy-start.5
  137.8 4.6 copy-start.1
  142.5 3.4 copy-start.2
  150.2 3.6 copy-start.7
  151.0 7.6 %copy-start.4 = (pred[768]{0:T(1024)(128)(4,1)}, pred[768]{0:T(1024)(128)(4,1)S(1)}, u32[]{:S(2)}) copy-start(pred[768]{0:T(1024)(128)(4,1)S(1)} %broadcast_bitcast_fusion.2) | copy-start | bytes 2308 | tf_op jit(solution)/shard_map/while
  160.8 4.6 copy-start.5
  160.9 4.6 copy-start.1
  165.5 3.4 copy-start.2
  173.2 3.6 copy-start.7
  174.0 7.6 %copy-start.4 = (pred[768]{0:T(1024)(128)(4,1)}, pred[768]{0:T(1024)(128)(4,1)S(1)}, u32[]{:S(2)}) copy-start(pred[768]{0:T(1024)(128)(4,1)S(1)} %broadcast_bitcast_fusion.2) | copy-start | bytes 2308 | tf_op jit(solution)/shard_map/while
  183.8 4.6 copy-start.5
  183.9 4.6 copy-start.1
  188.5 3.4 copy-start.2
  194.4 233.5 %all-reduce.6.cloned.1.call-start = ((), (), s32[]{:S(2)}) async-start(), calls=%async_computation.3 | async-start | bytes 17039360 | tf_op jit(solution)/shard_map/psum | solution.py:130
  307.8 0.7 copy-start.8
  307.8 3.4 copy-start.6
  307.9 157.8 %reduce-scatter.2.cloned.1.call-start = ((), (), s32[]{:S(2)}) async-start(), calls=%async_computation.2 | async-start | bytes 1310720 | tf_op jit(solution)/shard_map/reduce_scatter | solution.py:138
  332.8 95.2 %copy-start.3 = (f32[8,64,32]{1,2,0:T(8,128)S(1)}, f32[8,64,32]{1,2,0:T(8,128)}, u32[]{:S(2)}) copy-start(f32[8,64,32]{1,2,0:T(8,128)} %all-reduce.4.cloned.1.call-done) | copy-start | bytes 196612
  429.4 9.4 %copy-start.9 = (bf16[32,128,512]{2,1,0:T(8,128)(2,1)S(1)}, bf16[32,128,512]{2,1,0:T(8,128)(2,1)}, u32[]{:S(2)}) copy-start(bf16[32,128,512]{2,1,0:T(8,128)(2,1)} %param.23) | copy-start | bytes 12582916
Sparse Core Ops, SparseCore 0:
  194.6 103.5 all-reduce.3
  308.0 119.9 all-reduce.5
  442.2 23.4 reduce-scatter.1
where the time goes:
time: 474 us; the launch traced here: 472 us
  waiting for transfers between devices  218 us (46%)
  other arithmetic  87.8 us (19%)
  matrix products  85.3 us (18%)
  local copies, waits for them, and re-layouts  66.8 us (14%)
  between operations  13.3 us (3%)
    pmax x1, waiting for transfers between devices, local(): top_all = lax.pmax(highest, 'seq')  104 us
    psum x1, waiting for transfers between devices, local(): lax.psum((totals * factor, weighted * factor[..., None]), 'seq')  90.9 us
    dot_general x8, matrix products, one_request(): jnp.einsum('tkgd,nkd->tkgn', grouped, prefix_flat_keys, preferred_element...  38.2 us
    reduce_sum x8, other arithmetic, one_request(): totals = jnp.sum(prefix_weights, axis=-1) + jnp.sum(own_weights, axis=-1)  36 us
    dynamic_slice x24, local copies, waits for them, and re-layouts, local(): lax.map(one_request, (queries, block_use, private_lengths, private_keys,...  27.7 us
    reduce_scatter x1, waiting for transfers between devices, local(): lax.psum_scatter(jnp.einsum('rthd,hde->rte', attention, out_weight, prefe...  23.6 us
    dot_general x8, matrix products, one_request(): jnp.einsum('tkgn,nkd->tkgd', prefix_weights.astype(jnp.bfloat16), prefix_...  20.9 us
    dynamic_update_slice x24, local copies, waits for them, and re-layouts, local(): lax.map(one_request, (queries, block_use, private_lengths, private_keys,...  18.2 us
  transfers between devices with their start and end apart: 3, of which 3 were waited for; matrix products, arithmetic and copies ran while one was open for 6% of the time, Pallas kernels for 0%

commit v1 on v0

--- a/solution.py
+++ b/solution.py
@@ -125,16 +125,40 @@
     highest, totals, weighted = lax.map(
         one_request, (queries, block_use, private_lengths, private_keys, private_values)
     )
-    top_all = lax.pmax(highest, "seq")
-    factor = jnp.exp(highest - top_all)
-    summed_totals, summed_weighted = lax.psum(
-        (totals * factor, weighted * factor[..., None]), "seq"
+    requests = queries.shape[0]
+    seq_size = lax.axis_size("seq")
+    row_count = requests * tree_size
+    chunk = row_count // seq_size
+    sent = weighted.astype(jnp.bfloat16).reshape(seq_size, chunk, heads_dev, head_dim)
+    stats = jnp.stack([highest, totals], 0).reshape(2, seq_size, chunk, heads_dev)
+    stats = jnp.transpose(stats, (1, 0, 2, 3))
+    got = lax.all_to_all(sent, "seq", 0, 0, tiled=True)
+    got_stats = lax.all_to_all(stats, "seq", 0, 0, tiled=True)
+    part_top = got_stats[:, 0]
+    part_totals = got_stats[:, 1]
+    top_all = jnp.max(part_top, axis=0)
+    factor = jnp.exp(part_top - top_all[None])
+    summed_totals = jnp.sum(part_totals * factor, axis=0)
+    summed_weighted = jnp.sum(got.astype(jnp.float32) * factor[..., None], axis=0)
+    row0 = shard_index * chunk
+    request = row0 // tree_size
+    token0 = row0 % tree_size
+    my_queries = lax.dynamic_slice_in_dim(
+        queries.reshape(row_count, heads_dev, head_dim), row0, chunk, 0
+    )[None]
+    my_keys = lax.dynamic_index_in_dim(draft_keys, request, 0, keepdims=True)
+    my_values = lax.dynamic_index_in_dim(draft_values, request, 0, keepdims=True)
+    my_reach = lax.dynamic_slice_in_dim(
+        lax.dynamic_index_in_dim(reach, request, 0, keepdims=True), token0, chunk, 1
     )
-    draft = draft_part(queries, draft_keys, draft_values, reach, scaling)
+    draft = draft_part(my_queries, my_keys, my_values, my_reach, scaling)
+    draft = (draft[0][0], draft[1][0], draft[2][0])
     final_top, final_totals, final_weighted = combine(
         (top_all, summed_totals, summed_weighted), draft
     )
     attention = (final_weighted / final_totals[..., None]).astype(jnp.bfloat16)
+    attention = lax.all_gather(attention, "seq", axis=0, tiled=True)
+    attention = attention.reshape(requests, tree_size, heads_dev, head_dim)
     return lax.psum_scatter(
         jnp.einsum("rthd,hde->rte", attention, out_weight, preferred_element_type=jnp.float32),
         "heads",

time: 474 us -> 355 us (0.75)
  waiting for transfers between devices: 218 us -> 116 us
  other arithmetic: 87.8 us -> 68 us
  blocking collectives: 0 us -> 15.1 us
  matrix products: 85.3 us -> 71.7 us
  starting transfers between devices: 0.27 us -> 5.24 us
    pmax x1 -> x0, waiting for transfers between devices: 104 us -> none  [local(): top_all = lax.pmax(highest, 'seq')]
    psum x1 -> x0, waiting for transfers between devices: 90.9 us -> none  [local(): lax.psum((totals * factor, weighted * factor[..., None]), 'seq')]
    all_gather x0 -> x1, waiting for transfers between devices: none -> 47.4 us  [local(): attention = lax.all_gather(attention, 'seq', axis=0, tiled=True)]
    all_to_all x0 -> x1, waiting for transfers between devices: none -> 45.4 us  [local(): got = lax.all_to_all(sent, 'seq', 0, 0, tiled=True)]
    all_to_all x0 -> x1, blocking collectives: none -> 15.1 us  [local(): got_stats = lax.all_to_all(stats, 'seq', 0, 0, tiled=True)]
    mul x2 -> x0, other arithmetic: 9.58 us -> none  [the longest x1 7.86 us: local(): weighted * factor[..., None]]
    convert_element_type x1, other arithmetic: 9.34 us -> 0.93 us  [local(): attention = (final_weighted / final_totals[..., None]).astype(jnp.bfloat16)]
    dot_general x8, matrix products: 38.2 us -> 30 us  [one_request(): jnp.einsum('tkgd,nkd->tkgn', grouped, prefix_flat_keys, preferred_element...]
  transfers between devices with their start and end apart: 3 -> 3, of which waited for: 3 -> 3; matrix products, arithmetic and copies ran while one was open for 6% -> 2% of each run, Pallas kernels for 0% -> 0%
where the time goes in v1:
time: 355 us; the launch traced here: 353 us
  waiting for transfers between devices  116 us (33%)
  matrix products  71.7 us (20%)
  other arithmetic  68 us (19%)
  local copies, waits for them, and re-layouts  62.4 us (18%)
  blocking collectives  15.1 us (4%)
  between operations  13.7 us (4%)
  starting transfers between devices  5.24 us (1%)
    all_gather x1, waiting for transfers between devices, local(): attention = lax.all_gather(attention, 'seq', axis=0, tiled=True)  47.4 us
    all_to_all x1, waiting for transfers between devices, local(): got = lax.all_to_all(sent, 'seq', 0, 0, tiled=True)  45.4 us
    reduce_sum x8, other arithmetic, one_request(): totals = jnp.sum(prefix_weights, axis=-1) + jnp.sum(own_weights, axis=-1)  34.5 us
    dynamic_slice x24, local copies, waits for them, and re-layouts, local(): lax.map(one_request, (queries, block_use, private_lengths, private_keys,...  32.7 us
    dot_general x8, matrix products, one_request(): jnp.einsum('tkgd,nkd->tkgn', grouped, prefix_flat_keys, preferred_element...  30 us
    reduce_scatter x1, waiting for transfers between devices, local(): lax.psum_scatter(jnp.einsum('rthd,hde->rte', attention, out_weight, prefe...  23.5 us
    dot_general x8, matrix products, one_request(): jnp.einsum('tkgn,nkd->tkgd', prefix_weights.astype(jnp.bfloat16), prefix_...  21.1 us
    convert_element_type x8, other arithmetic, one_request(): own_weights.astype(jnp.bfloat16)  16.7 us
  transfers between devices with their start and end apart: 3, of which 3 were waited for; matrix products, arithmetic and copies ran while one was open for 2% of the time, Pallas kernels for 0%

profile of v1, /device:TPU:0, one launch (start us, length us, event | category | flops | bytes accessed | tf_op | source)
XLA Modules:
  0.0 353.1 jit_solution(10569610488154433797)
XLA Ops:
  7.6 1.8 copy.129
  9.4 178.4 %while.15 = (s32[]{:T(128)}, f32[8,64,32]{1,2,0:T(8,128)}, f32[8,64,32]{1,2,0:T(8,128)}, bf16[8,64,32,128]{3,2,1,0:T(8,128)(2,1)}, s32[8,6]{1,0:T(8,128)}, /*ind...) while((s32[]{:T(128)}, f32[8,64,32]{1,2,0:T(8,128)}, ...), condition=%wide.region_5.6_spmd.clone, body=%wide.region_0.5_spmd.clone.sunk | while | flops 1099428352 | bytes 59493500 | solution.py:125
  9.4 1.2 dynamic_slice.66
  12.0 1.8 constant_dynamic-slice_fusion.10
  13.8 1.1 constant_dynamic-slice_fusion.9
  15.5 3.7 %bitcast_reduce_fusion.5 = (f32[64,2,16]{2,0,1:T(8,128)S(1)}, f32[2,64,16,768]{3,2,1,0:T(8,128)}) fusion(pred[768]{0:T(1024)(128)(4,1)S(1)} %broadcast_bitcast_fusion.2, bf16[768,2,128]{2,0,1:T(8,128)(2,1)S(1)} %get-tuple-element.345, bf16[64,2,16,128]{3,2,1,0:T(8,128)(2,1)S(1)} %bitcast.175), kind=kOutput, calls=%fused_computation.2.clone.1 | convolution fusion | flops 407369728 | bytes 7217920 | tf_op jit(solution)/shard_map/while/body/eval_jaxpr/tkgd,nkd->tkgn/dot_general | solution.py:92
  19.3 2.1 fusion.89
  21.5 4.3 %fusion.88 = f32[64,2,16]{2,0,1:T(8,128)S(1)} fusion(f32[2,64,16,768]{3,2,1,0:T(8,128)} %get-tuple-element.308, f32[64,2,16]{2,0,1:T(8,128)S(1)} %copy.202, pred[768]{0:T(1024)(128)(4,1)} %copy-done.3), kind=kLoop, calls=%fused_computation.7.clone.1 | loop fusion | flops 7862272 | bytes 6308608 | tf_op jit(solution)/shard_map/while/body/eval_jaxpr/reduce_sum | solution.py:106
  26.2 2.6 fusion.90
  31.8 1.2 dynamic_slice.66
  34.3 1.8 constant_dynamic-slice_fusion.10
  36.1 1.1 constant_dynamic-slice_fusion.9
  37.8 3.7 %bitcast_reduce_fusion.5 = (f32[64,2,16]{2,0,1:T(8,128)S(1)}, f32[2,64,16,768]{3,2,1,0:T(8,128)}) fusion(pred[768]{0:T(1024)(128)(4,1)S(1)} %broadcast_bitcast_fusion.2, bf16[768,2,128]{2,0,1:T(8,128)(2,1)S(1)} %get-tuple-element.345, bf16[64,2,16,128]{3,2,1,0:T(8,128)(2,1)S(1)} %bitcast.175), kind=kOutput, calls=%fused_computation.2.clone.1 | convolution fusion | flops 407369728 | bytes 7217920 | tf_op jit(solution)/shard_map/while/body/eval_jaxpr/tkgd,nkd->tkgn/dot_general | solution.py:92
  41.6 2.1 fusion.89
  43.8 4.3 %fusion.88 = f32[64,2,16]{2,0,1:T(8,128)S(1)} fusion(f32[2,64,16,768]{3,2,1,0:T(8,128)} %get-tuple-element.308, f32[64,2,16]{2,0,1:T(8,128)S(1)} %copy.202, pred[768]{0:T(1024)(128)(4,1)} %copy-done.3), kind=kLoop, calls=%fused_computation.7.clone.1 | loop fusion | flops 7862272 | bytes 6308608 | tf_op jit(solution)/shard_map/while/body/eval_jaxpr/reduce_sum | solution.py:106
  48.5 2.6 fusion.90
  54.1 1.2 dynamic_slice.66
  56.6 1.8 constant_dynamic-slice_fusion.10
  58.4 1.1 constant_dynamic-slice_fusion.9
  60.1 3.7 %bitcast_reduce_fusion.5 = (f32[64,2,16]{2,0,1:T(8,128)S(1)}, f32[2,64,16,768]{3,2,1,0:T(8,128)}) fusion(pred[768]{0:T(1024)(128)(4,1)S(1)} %broadcast_bitcast_fusion.2, bf16[768,2,128]{2,0,1:T(8,128)(2,1)S(1)} %get-tuple-element.345, bf16[64,2,16,128]{3,2,1,0:T(8,128)(2,1)S(1)} %bitcast.175), kind=kOutput, calls=%fused_computation.2.clone.1 | convolution fusion | flops 407369728 | bytes 7217920 | tf_op jit(solution)/shard_map/while/body/eval_jaxpr/tkgd,nkd->tkgn/dot_general | solution.py:92
  64.0 2.1 fusion.89
  66.1 4.3 %fusion.88 = f32[64,2,16]{2,0,1:T(8,128)S(1)} fusion(f32[2,64,16,768]{3,2,1,0:T(8,128)} %get-tuple-element.308, f32[64,2,16]{2,0,1:T(8,128)S(1)} %copy.202, pred[768]{0:T(1024)(128)(4,1)} %copy-done.3), kind=kLoop, calls=%fused_computation.7.clone.1 | loop fusion | flops 7862272 | bytes 6308608 | tf_op jit(solution)/shard_map/while/body/eval_jaxpr/reduce_sum | solution.py:106
  70.8 2.6 fusion.90
  76.3 1.2 dynamic_slice.66
  78.9 1.8 constant_dynamic-slice_fusion.10
  80.7 1.1 constant_dynamic-slice_fusion.9
  82.4 3.7 %bitcast_reduce_fusion.5 = (f32[64,2,16]{2,0,1:T(8,128)S(1)}, f32[2,64,16,768]{3,2,1,0:T(8,128)}) fusion(pred[768]{0:T(1024)(128)(4,1)S(1)} %broadcast_bitcast_fusion.2, bf16[768,2,128]{2,0,1:T(8,128)(2,1)S(1)} %get-tuple-element.345, bf16[64,2,16,128]{3,2,1,0:T(8,128)(2,1)S(1)} %bitcast.175), kind=kOutput, calls=%fused_computation.2.clone.1 | convolution fusion | flops 407369728 | bytes 7217920 | tf_op jit(solution)/shard_map/while/body/eval_jaxpr/tkgd,nkd->tkgn/dot_general | solution.py:92
  86.2 2.1 fusion.89
  88.4 4.3 %fusion.88 = f32[64,2,16]{2,0,1:T(8,128)S(1)} fusion(f32[2,64,16,768]{3,2,1,0:T(8,128)} %get-tuple-element.308, f32[64,2,16]{2,0,1:T(8,128)S(1)} %copy.202, pred[768]{0:T(1024)(128)(4,1)} %copy-done.3), kind=kLoop, calls=%fused_computation.7.clone.1 | loop fusion | flops 7862272 | bytes 6308608 | tf_op jit(solution)/shard_map/while/body/eval_jaxpr/reduce_sum | solution.py:106
  93.1 2.6 fusion.90
  98.7 1.2 dynamic_slice.66
  101.2 1.8 constant_dynamic-slice_fusion.10
  103.0 1.1 constant_dynamic-slice_fusion.9
  104.7 3.7 %bitcast_reduce_fusion.5 = (f32[64,2,16]{2,0,1:T(8,128)S(1)}, f32[2,64,16,768]{3,2,1,0:T(8,128)}) fusion(pred[768]{0:T(1024)(128)(4,1)S(1)} %broadcast_bitcast_fusion.2, bf16[768,2,128]{2,0,1:T(8,128)(2,1)S(1)} %get-tuple-element.345, bf16[64,2,16,128]{3,2,1,0:T(8,128)(2,1)S(1)} %bitcast.175), kind=kOutput, calls=%fused_computation.2.clone.1 | convolution fusion | flops 407369728 | bytes 7217920 | tf_op jit(solution)/shard_map/while/body/eval_jaxpr/tkgd,nkd->tkgn/dot_general | solution.py:92
  108.5 2.1 fusion.89
  110.7 4.3 %fusion.88 = f32[64,2,16]{2,0,1:T(8,128)S(1)} fusion(f32[2,64,16,768]{3,2,1,0:T(8,128)} %get-tuple-element.308, f32[64,2,16]{2,0,1:T(8,128)S(1)} %copy.202, pred[768]{0:T(1024)(128)(4,1)} %copy-done.3), kind=kLoop, calls=%fused_computation.7.clone.1 | loop fusion | flops 7862272 | bytes 6308608 | tf_op jit(solution)/shard_map/while/body/eval_jaxpr/reduce_sum | solution.py:106
  115.4 2.6 fusion.90
  121.0 1.2 dynamic_slice.66
  123.5 1.8 constant_dynamic-slice_fusion.10
  125.3 1.1 constant_dynamic-slice_fusion.9
  127.0 3.7 %bitcast_reduce_fusion.5 = (f32[64,2,16]{2,0,1:T(8,128)S(1)}, f32[2,64,16,768]{3,2,1,0:T(8,128)}) fusion(pred[768]{0:T(1024)(128)(4,1)S(1)} %broadcast_bitcast_fusion.2, bf16[768,2,128]{2,0,1:T(8,128)(2,1)S(1)} %get-tuple-element.345, bf16[64,2,16,128]{3,2,1,0:T(8,128)(2,1)S(1)} %bitcast.175), kind=kOutput, calls=%fused_computation.2.clone.1 | convolution fusion | flops 407369728 | bytes 7217920 | tf_op jit(solution)/shard_map/while/body/eval_jaxpr/tkgd,nkd->tkgn/dot_general | solution.py:92
  130.9 2.1 fusion.89
  133.0 4.3 %fusion.88 = f32[64,2,16]{2,0,1:T(8,128)S(1)} fusion(f32[2,64,16,768]{3,2,1,0:T(8,128)} %get-tuple-element.308, f32[64,2,16]{2,0,1:T(8,128)S(1)} %copy.202, pred[768]{0:T(1024)(128)(4,1)} %copy-done.3), kind=kLoop, calls=%fused_computation.7.clone.1 | loop fusion | flops 7862272 | bytes 6308608 | tf_op jit(solution)/shard_map/while/body/eval_jaxpr/reduce_sum | solution.py:106
  137.7 2.6 fusion.90
  143.3 1.2 dynamic_slice.66
  145.9 1.8 constant_dynamic-slice_fusion.10
  147.7 1.1 constant_dynamic-slice_fusion.9
  149.4 3.7 %bitcast_reduce_fusion.5 = (f32[64,2,16]{2,0,1:T(8,128)S(1)}, f32[2,64,16,768]{3,2,1,0:T(8,128)}) fusion(pred[768]{0:T(1024)(128)(4,1)S(1)} %broadcast_bitcast_fusion.2, bf16[768,2,128]{2,0,1:T(8,128)(2,1)S(1)} %get-tuple-element.345, bf16[64,2,16,128]{3,2,1,0:T(8,128)(2,1)S(1)} %bitcast.175), kind=kOutput, calls=%fused_computation.2.clone.1 | convolution fusion | flops 407369728 | bytes 7217920 | tf_op jit(solution)/shard_map/while/body/eval_jaxpr/tkgd,nkd->tkgn/dot_general | solution.py:92
  153.2 2.1 fusion.89
  155.4 4.3 %fusion.88 = f32[64,2,16]{2,0,1:T(8,128)S(1)} fusion(f32[2,64,16,768]{3,2,1,0:T(8,128)} %get-tuple-element.308, f32[64,2,16]{2,0,1:T(8,128)S(1)} %copy.202, pred[768]{0:T(1024)(128)(4,1)} %copy-done.3), kind=kLoop, calls=%fused_computation.7.clone.1 | loop fusion | flops 7862272 | bytes 6308608 | tf_op jit(solution)/shard_map/while/body/eval_jaxpr/reduce_sum | solution.py:106
  160.0 2.6 fusion.90
  165.6 1.2 dynamic_slice.66
  168.2 1.8 constant_dynamic-slice_fusion.10
  171.7 3.7 %bitcast_reduce_fusion.5 = (f32[64,2,16]{2,0,1:T(8,128)S(1)}, f32[2,64,16,768]{3,2,1,0:T(8,128)}) fusion(pred[768]{0:T(1024)(128)(4,1)S(1)} %broadcast_bitcast_fusion.2, bf16[768,2,128]{2,0,1:T(8,128)(2,1)S(1)} %get-tuple-element.345, bf16[64,2,16,128]{3,2,1,0:T(8,128)(2,1)S(1)} %bitcast.175), kind=kOutput, calls=%fused_computation.2.clone.1 | convolution fusion | flops 407369728 | bytes 7217920 | tf_op jit(solution)/shard_map/while/body/eval_jaxpr/tkgd,nkd->tkgn/dot_general | solution.py:92
  175.5 2.1 fusion.89
  177.7 4.3 %fusion.88 = f32[64,2,16]{2,0,1:T(8,128)S(1)} fusion(f32[2,64,16,768]{3,2,1,0:T(8,128)} %get-tuple-element.308, f32[64,2,16]{2,0,1:T(8,128)S(1)} %copy.202, pred[768]{0:T(1024)(128)(4,1)} %copy-done.3), kind=kLoop, calls=%fused_computation.7.clone.1 | loop fusion | flops 7862272 | bytes 6308608 | tf_op jit(solution)/shard_map/while/body/eval_jaxpr/reduce_sum | solution.py:106
  182.3 2.6 fusion.90
  190.3 15.1 %all_to_all.10 = f32[32,1,1024]{2,1,0:T(1,128)S(1)} all-to-all(f32[32,1,1024]{2,1,0:T(1,128)S(1)} %reshape.181), channel_id=1, replica_groups=mesh['heads'=4,'seq'=32] {'seq'}, dimensions={0} | all-to-all | bytes 262144 | tf_op jit(solution)/shard_map/all_to_all | solution.py:136
  205.4 5.0 %all-to-all-start = ((bf16[32,16,32,128]{3,2,1,0:T(8,128)(2,1)}), bf16[32,16,32,128]{3,2,1,0:T(8,128)(2,1)}, u32[]{:S(2)}, u32[]{:S(2)}) async-start(bf16[32,16,32,128]{3,2,1,0:T(8,128)(2,1)} %bitcast.179), calls=%async_computation | async-start | bytes 8388608 | tf_op jit(solution)/shard_map/all_to_all | solution.py:135
  217.6 45.4 %all-to-all-done = bf16[32,16,32,128]{3,2,1,0:T(8,128)(2,1)} async-done(((bf16[32,16,32,128]{3,2,1,0:T(8,128)(2,1)}), bf16[32,16,32,128]{3,2,1,0:T(8,128)(2,1)}, u32[]{:S(2)}, u32[]{:S(2)}) %all-to-all-start) | async-done | bytes 4194336 | tf_op jit(solution)/shard_map/all_to_all | solution.py:135
  262.9 4.4 %multiply_reduce_fusion = f32[16,32,128]{2,1,0:T(8,128)S(1)} fusion(bf16[32,16,32,128]{3,2,1,0:T(8,128)(2,1)} %all-to-all-done, f32[32,16,32]{2,1,0:T(8,128)S(1)} %get-tuple-element.211), kind=kLoop, calls=%fused_computation.43 | loop fusion | flops 6225920 | bytes 4521984 | tf_op jit(solution)/shard_map/reduce_sum | solution.py:142
  268.6 47.4 %all-gather.2.cloned.1.call-done = bf16[512,32,128]{2,1,0:T(8,128)(2,1)} async-done(((bf16[16,32,128]{2,1,0:T(8,128)(2,1)}), bf16[512,32,128]{2,1,0:T(8,128)(2,1)}) %all-gather.2.cloned.1.call-update) | async-done | bytes 4194320 | tf_op jit(solution)/shard_map/all_gather | solution.py:160
  315.9 6.8 %fusion.31 = f32[8,64,512]{2,1,0:T(8,128)} fusion(bf16[32,128,512]{2,1,0:T(8,128)(2,1)} %param.23, bf16[8,64,32,128]{3,2,1,0:T(8,128)(2,1)} %bitcast.187), kind=kOutput, calls=%fused_computation.47 | convolution fusion | flops 2147483648 | bytes 9437184 | tf_op jit(solution)/shard_map/rthd,hde->rte/dot_general | solution.py:163
  322.8 23.5 %reduce-scatter.2.cloned.1.call-done = f32[2,64,512]{2,1,0:T(8,128)} async-done(((f32[8,64,512]{2,1,0:T(8,128)}), f32[2,64,512]{2,1,0:T(8,128)}) %reduce-scatter.2.cloned.1.call-update) | async-done | bytes 262160 | tf_op jit(solution)/shard_map/reduce_scatter | solution.py:162
  (249 shorter events, 55.5 us)
Async XLA Ops:
  11.2 8.1 %copy-start.5 = (pred[256]{0:T(512)(128)(4,1)}, pred[256]{0:T(512)(128)(4,1)S(1)}, u32[]{:S(2)}) copy-start(pred[256]{0:T(512)(128)(4,1)S(1)} %add_compare_fusion.2) | copy-start | bytes 772 | tf_op jit(solution)/shard_map/while
  12.0 7.3 %copy-start.3 = (pred[768]{0:T(1024)(128)(4,1)}, pred[768]{0:T(1024)(128)(4,1)S(1)}, u32[]{:S(2)}) copy-start(pred[768]{0:T(1024)(128)(4,1)S(1)} %broadcast_bitcast_fusion.2) | copy-start | bytes 2308 | tf_op jit(solution)/shard_map/while
  21.4 4.4 %copy-start.4 = (pred[768]{0:T(1024)(128)(4,1)S(1)}, pred[768]{0:T(1024)(128)(4,1)}, u32[]{:S(2)}) copy-start(pred[768]{0:T(1024)(128)(4,1)} %copy-done.3) | copy-start | bytes 2308 | tf_op jit(solution)/shard_map/while
  21.5 4.6 %copy-start = (f32[2,64,16,768]{3,2,1,0:T(8,128)S(1)}, f32[2,64,16,768]{3,2,1,0:T(8,128)}, u32[]{:S(2)}) copy-start(f32[2,64,16,768]{3,2,1,0:T(8,128)} %get-tuple-element.308) | copy-start | bytes 18874372 | tf_op jit(solution)/shard_map/while
  26.2 2.6 copy-start.1
  28.8 0.8 copy-start.2
  33.5 8.0 %copy-start.5 = (pred[256]{0:T(512)(128)(4,1)}, pred[256]{0:T(512)(128)(4,1)S(1)}, u32[]{:S(2)}) copy-start(pred[256]{0:T(512)(128)(4,1)S(1)} %add_compare_fusion.2) | copy-start | bytes 772 | tf_op jit(solution)/shard_map/while
  34.3 7.2 %copy-start.3 = (pred[768]{0:T(1024)(128)(4,1)}, pred[768]{0:T(1024)(128)(4,1)S(1)}, u32[]{:S(2)}) copy-start(pred[768]{0:T(1024)(128)(4,1)S(1)} %broadcast_bitcast_fusion.2) | copy-start | bytes 2308 | tf_op jit(solution)/shard_map/while
  43.7 4.4 %copy-start.4 = (pred[768]{0:T(1024)(128)(4,1)S(1)}, pred[768]{0:T(1024)(128)(4,1)}, u32[]{:S(2)}) copy-start(pred[768]{0:T(1024)(128)(4,1)} %copy-done.3) | copy-start | bytes 2308 | tf_op jit(solution)/shard_map/while
  43.8 4.6 %copy-start = (f32[2,64,16,768]{3,2,1,0:T(8,128)S(1)}, f32[2,64,16,768]{3,2,1,0:T(8,128)}, u32[]{:S(2)}) copy-start(f32[2,64,16,768]{3,2,1,0:T(8,128)} %get-tuple-element.308) | copy-start | bytes 18874372 | tf_op jit(solution)/shard_map/while
  48.5 2.7 copy-start.1
  51.1 0.8 copy-start.2
  55.8 8.1 %copy-start.5 = (pred[256]{0:T(512)(128)(4,1)}, pred[256]{0:T(512)(128)(4,1)S(1)}, u32[]{:S(2)}) copy-start(pred[256]{0:T(512)(128)(4,1)S(1)} %add_compare_fusion.2) | copy-start | bytes 772 | tf_op jit(solution)/shard_map/while
  56.6 7.3 %copy-start.3 = (pred[768]{0:T(1024)(128)(4,1)}, pred[768]{0:T(1024)(128)(4,1)S(1)}, u32[]{:S(2)}) copy-start(pred[768]{0:T(1024)(128)(4,1)S(1)} %broadcast_bitcast_fusion.2) | copy-start | bytes 2308 | tf_op jit(solution)/shard_map/while
  66.0 4.4 %copy-start.4 = (pred[768]{0:T(1024)(128)(4,1)S(1)}, pred[768]{0:T(1024)(128)(4,1)}, u32[]{:S(2)}) copy-start(pred[768]{0:T(1024)(128)(4,1)} %copy-done.3) | copy-start | bytes 2308 | tf_op jit(solution)/shard_map/while
  66.1 4.6 %copy-start = (f32[2,64,16,768]{3,2,1,0:T(8,128)S(1)}, f32[2,64,16,768]{3,2,1,0:T(8,128)}, u32[]{:S(2)}) copy-start(f32[2,64,16,768]{3,2,1,0:T(8,128)} %get-tuple-element.308) | copy-start | bytes 18874372 | tf_op jit(solution)/shard_map/while
  70.8 2.6 copy-start.1
  73.4 0.8 copy-start.2
  78.1 8.0 %copy-start.5 = (pred[256]{0:T(512)(128)(4,1)}, pred[256]{0:T(512)(128)(4,1)S(1)}, u32[]{:S(2)}) copy-start(pred[256]{0:T(512)(128)(4,1)S(1)} %add_compare_fusion.2) | copy-start | bytes 772 | tf_op jit(solution)/shard_map/while
  78.9 7.3 %copy-start.3 = (pred[768]{0:T(1024)(128)(4,1)}, pred[768]{0:T(1024)(128)(4,1)S(1)}, u32[]{:S(2)}) copy-start(pred[768]{0:T(1024)(128)(4,1)S(1)} %broadcast_bitcast_fusion.2) | copy-start | bytes 2308 | tf_op jit(solution)/shard_map/while
  88.3 4.4 %copy-start.4 = (pred[768]{0:T(1024)(128)(4,1)S(1)}, pred[768]{0:T(1024)(128)(4,1)}, u32[]{:S(2)}) copy-start(pred[768]{0:T(1024)(128)(4,1)} %copy-done.3) | copy-start | bytes 2308 | tf_op jit(solution)/shard_map/while
  88.4 4.6 %copy-start = (f32[2,64,16,768]{3,2,1,0:T(8,128)S(1)}, f32[2,64,16,768]{3,2,1,0:T(8,128)}, u32[]{:S(2)}) copy-start(f32[2,64,16,768]{3,2,1,0:T(8,128)} %get-tuple-element.308) | copy-start | bytes 18874372 | tf_op jit(solution)/shard_map/while
  93.0 2.6 copy-start.1
  95.7 0.8 copy-start.2
  100.4 8.0 %copy-start.5 = (pred[256]{0:T(512)(128)(4,1)}, pred[256]{0:T(512)(128)(4,1)S(1)}, u32[]{:S(2)}) copy-start(pred[256]{0:T(512)(128)(4,1)S(1)} %add_compare_fusion.2) | copy-start | bytes 772 | tf_op jit(solution)/shard_map/while
  101.2 7.3 %copy-start.3 = (pred[768]{0:T(1024)(128)(4,1)}, pred[768]{0:T(1024)(128)(4,1)S(1)}, u32[]{:S(2)}) copy-start(pred[768]{0:T(1024)(128)(4,1)S(1)} %broadcast_bitcast_fusion.2) | copy-start | bytes 2308 | tf_op jit(solution)/shard_map/while
  110.6 4.4 %copy-start.4 = (pred[768]{0:T(1024)(128)(4,1)S(1)}, pred[768]{0:T(1024)(128)(4,1)}, u32[]{:S(2)}) copy-start(pred[768]{0:T(1024)(128)(4,1)} %copy-done.3) | copy-start | bytes 2308 | tf_op jit(solution)/shard_map/while
  110.7 4.6 %copy-start = (f32[2,64,16,768]{3,2,1,0:T(8,128)S(1)}, f32[2,64,16,768]{3,2,1,0:T(8,128)}, u32[]{:S(2)}) copy-start(f32[2,64,16,768]{3,2,1,0:T(8,128)} %get-tuple-element.308) | copy-start | bytes 18874372 | tf_op jit(solution)/shard_map/while
  115.3 2.6 copy-start.1
  118.0 0.8 copy-start.2
  122.7 8.0 %copy-start.5 = (pred[256]{0:T(512)(128)(4,1)}, pred[256]{0:T(512)(128)(4,1)S(1)}, u32[]{:S(2)}) copy-start(pred[256]{0:T(512)(128)(4,1)S(1)} %add_compare_fusion.2) | copy-start | bytes 772 | tf_op jit(solution)/shard_map/while
  123.5 7.3 %copy-start.3 = (pred[768]{0:T(1024)(128)(4,1)}, pred[768]{0:T(1024)(128)(4,1)S(1)}, u32[]{:S(2)}) copy-start(pred[768]{0:T(1024)(128)(4,1)S(1)} %broadcast_bitcast_fusion.2) | copy-start | bytes 2308 | tf_op jit(solution)/shard_map/while
  132.9 4.4 %copy-start.4 = (pred[768]{0:T(1024)(128)(4,1)S(1)}, pred[768]{0:T(1024)(128)(4,1)}, u32[]{:S(2)}) copy-start(pred[768]{0:T(1024)(128)(4,1)} %copy-done.3) | copy-start | bytes 2308 | tf_op jit(solution)/shard_map/while
  133.0 4.6 %copy-start = (f32[2,64,16,768]{3,2,1,0:T(8,128)S(1)}, f32[2,64,16,768]{3,2,1,0:T(8,128)}, u32[]{:S(2)}) copy-start(f32[2,64,16,768]{3,2,1,0:T(8,128)} %get-tuple-element.308) | copy-start | bytes 18874372 | tf_op jit(solution)/shard_map/while
  137.7 2.7 copy-start.1
  140.3 0.8 copy-start.2
  145.1 8.0 %copy-start.5 = (pred[256]{0:T(512)(128)(4,1)}, pred[256]{0:T(512)(128)(4,1)S(1)}, u32[]{:S(2)}) copy-start(pred[256]{0:T(512)(128)(4,1)S(1)} %add_compare_fusion.2) | copy-start | bytes 772 | tf_op jit(solution)/shard_map/while
  145.9 7.2 %copy-start.3 = (pred[768]{0:T(1024)(128)(4,1)}, pred[768]{0:T(1024)(128)(4,1)S(1)}, u32[]{:S(2)}) copy-start(pred[768]{0:T(1024)(128)(4,1)S(1)} %broadcast_bitcast_fusion.2) | copy-start | bytes 2308 | tf_op jit(solution)/shard_map/while
  155.3 4.4 %copy-start.4 = (pred[768]{0:T(1024)(128)(4,1)S(1)}, pred[768]{0:T(1024)(128)(4,1)}, u32[]{:S(2)}) copy-start(pred[768]{0:T(1024)(128)(4,1)} %copy-done.3) | copy-start | bytes 2308 | tf_op jit(solution)/shard_map/while
  155.4 4.6 %copy-start = (f32[2,64,16,768]{3,2,1,0:T(8,128)S(1)}, f32[2,64,16,768]{3,2,1,0:T(8,128)}, u32[]{:S(2)}) copy-start(f32[2,64,16,768]{3,2,1,0:T(8,128)} %get-tuple-element.308) | copy-start | bytes 18874372 | tf_op jit(solution)/shard_map/while
  160.0 2.6 copy-start.1
  162.7 0.8 copy-start.2
  167.4 8.0 %copy-start.5 = (pred[256]{0:T(512)(128)(4,1)}, pred[256]{0:T(512)(128)(4,1)S(1)}, u32[]{:S(2)}) copy-start(pred[256]{0:T(512)(128)(4,1)S(1)} %add_compare_fusion.2) | copy-start | bytes 772 | tf_op jit(solution)/shard_map/while
  168.2 7.2 %copy-start.3 = (pred[768]{0:T(1024)(128)(4,1)}, pred[768]{0:T(1024)(128)(4,1)S(1)}, u32[]{:S(2)}) copy-start(pred[768]{0:T(1024)(128)(4,1)S(1)} %broadcast_bitcast_fusion.2) | copy-start | bytes 2308 | tf_op jit(solution)/shard_map/while
  177.6 4.4 %copy-start.4 = (pred[768]{0:T(1024)(128)(4,1)S(1)}, pred[768]{0:T(1024)(128)(4,1)}, u32[]{:S(2)}) copy-start(pred[768]{0:T(1024)(128)(4,1)} %copy-done.3) | copy-start | bytes 2308 | tf_op jit(solution)/shard_map/while
  177.7 4.6 %copy-start = (f32[2,64,16,768]{3,2,1,0:T(8,128)S(1)}, f32[2,64,16,768]{3,2,1,0:T(8,128)}, u32[]{:S(2)}) copy-start(f32[2,64,16,768]{3,2,1,0:T(8,128)} %get-tuple-element.308) | copy-start | bytes 18874372 | tf_op jit(solution)/shard_map/while
  182.3 2.6 copy-start.1
  185.0 0.8 copy-start.2
  205.4 5.1 %copy-start.6 = (s32[8,64]{1,0:T(8,128)S(1)}, s32[8,64]{1,0:T(8,128)}, u32[]{:S(2)}) copy-start(s32[8,64]{1,0:T(8,128)} %param.22) | copy-start | bytes 6148
  205.4 57.5 %all-to-all-start = ((bf16[32,16,32,128]{3,2,1,0:T(8,128)(2,1)}), bf16[32,16,32,128]{3,2,1,0:T(8,128)(2,1)}, u32[]{:S(2)}, u32[]{:S(2)}) async-start(bf16[32,16,32,128]{3,2,1,0:T(8,128)(2,1)} %bitcast.179), calls=%async_computation | async-start | bytes 8388608 | tf_op jit(solution)/shard_map/all_to_all | solution.py:135
  210.4 105.6 %all-gather.2.cloned.1.call-start = ((), (), s32[]{:S(2)}) async-start(), calls=%async_computation.3 | async-start | bytes 4325376 | tf_op jit(solution)/shard_map/all_gather | solution.py:160
  268.3 77.9 %reduce-scatter.2.cloned.1.call-start = ((), (), s32[]{:S(2)}) async-start(), calls=%async_computation.4 | async-start | bytes 1310720 | tf_op jit(solution)/shard_map/reduce_scatter | solution.py:162
Sparse Core Ops, SparseCore 0:
  268.4 47.4 all-gather.1
  322.9 23.3 reduce-scatter.1

commit v2 on v1

--- a/solution.py
+++ b/solution.py
@@ -3,6 +3,8 @@
 import jax
 import jax.numpy as jnp
 from jax import lax
+from jax.experimental import pallas as pl
+from jax.experimental.pallas import tpu as pltpu
 from jax.sharding import PartitionSpec as P
 
 
@@ -53,6 +55,82 @@
         totals.reshape(requests, rows, heads_dev),
         weighted.reshape(requests, rows, heads_dev, head_dim),
     )
+
+
+def context_kernel(use_ref, len_ref, q_ref, kp_ref, vp_ref, ko_ref, vo_ref, acc_ref, st_ref):
+    r = pl.program_id(1)
+    scaling = 1.0 / math.sqrt(q_ref.shape[-1])
+    q = q_ref[0].reshape(-1, q_ref.shape[-1])
+    kp = kp_ref[0]
+    ko = ko_ref[0, 0]
+    dims = (((1,), (1,)), ((), ()))
+    s_pre = lax.dot_general(kp, q, dims, preferred_element_type=jnp.float32) * scaling
+    s_own = lax.dot_general(ko, q, dims, preferred_element_type=jnp.float32) * scaling
+    n_pre = kp.shape[0]
+    n_own = ko.shape[0]
+    block_len = n_pre // use_ref.shape[1]
+    block_id = lax.broadcasted_iota(jnp.int32, (n_pre, 1), 0) // block_len
+    pre_live = jnp.zeros((n_pre, 1), jnp.bool_)
+    for b in range(use_ref.shape[1]):
+        pre_live = jnp.logical_or(pre_live, jnp.logical_and(block_id == b, use_ref[r, b] == 1))
+    own_live = lax.broadcasted_iota(jnp.int32, (n_own, 1), 0) < len_ref[r]
+    s_pre = jnp.where(pre_live, s_pre, -1e30)
+    s_own = jnp.where(own_live, s_own, -1e30)
+    top = jnp.maximum(
+        jnp.max(s_pre, axis=0, keepdims=True), jnp.max(s_own, axis=0, keepdims=True)
+    )
+    w_pre = jnp.where(pre_live, jnp.exp(s_pre - top), 0.0)
+    w_own = jnp.where(own_live, jnp.exp(s_own - top), 0.0)
+    totals = jnp.sum(w_pre, axis=0, keepdims=True) + jnp.sum(w_own, axis=0, keepdims=True)
+    acc = jnp.dot(vp_ref[0], w_pre.astype(jnp.bfloat16), preferred_element_type=jnp.float32)
+    acc = acc + jnp.dot(
+        vo_ref[0, 0], w_own.astype(jnp.bfloat16), preferred_element_type=jnp.float32
+    )
+    pieces = acc_ref.shape[1]
+    width = acc_ref.shape[-1]
+    for c in range(pieces):
+        acc_ref[0, c, 0] = acc[:, c * width : (c + 1) * width].astype(acc_ref.dtype)
+    st_ref[0, 0] = jnp.zeros(st_ref.shape[2:], jnp.float32)
+    st_ref[0, 0, 0:1, :] = top
+    st_ref[0, 0, 1:2, :] = totals
+
+
+def context_part(queries, prefix_keys, prefix_values, use_rows, own_lengths, own_keys, own_values, pieces):
+    requests, tree_size, heads_dev, head_dim = queries.shape
+    block_count, block_len, kv_dev, _ = prefix_keys.shape
+    group_size = heads_dev // kv_dev
+    private_dev = own_keys.shape[1]
+    n_pre = block_count * block_len
+    rows = tree_size * group_size
+    width = rows // pieces
+    kp = jnp.transpose(prefix_keys.reshape(n_pre, kv_dev, head_dim), (1, 0, 2))
+    vp = jnp.transpose(prefix_values.reshape(n_pre, kv_dev, head_dim), (1, 2, 0))
+    ko = jnp.transpose(own_keys, (0, 2, 1, 3))
+    vo = jnp.transpose(own_values, (0, 2, 3, 1))
+    grid_spec = pltpu.PrefetchScalarGridSpec(
+        num_scalar_prefetch=2,
+        grid=(kv_dev, requests),
+        in_specs=[
+            pl.BlockSpec((1, tree_size, group_size, head_dim), lambda k, r, u, n: (r, 0, k, 0)),
+            pl.BlockSpec((1, n_pre, head_dim), lambda k, r, u, n: (k, 0, 0)),
+            pl.BlockSpec((1, head_dim, n_pre), lambda k, r, u, n: (k, 0, 0)),
+            pl.BlockSpec((1, 1, private_dev, head_dim), lambda k, r, u, n: (r, k, 0, 0)),
+            pl.BlockSpec((1, 1, head_dim, private_dev), lambda k, r, u, n: (r, k, 0, 0)),
+        ],
+        out_specs=[
+            pl.BlockSpec((1, pieces, 1, head_dim, width), lambda k, r, u, n: (r, 0, k, 0, 0)),
+            pl.BlockSpec((1, 1, 8, rows), lambda k, r, u, n: (r, k, 0, 0)),
+        ],
+    )
+    acc, st = pl.pallas_call(
+        context_kernel,
+        grid_spec=grid_spec,
+        out_shape=[
+            jax.ShapeDtypeStruct((requests, pieces, kv_dev, head_dim, width), jnp.bfloat16),
+            jax.ShapeDtypeStruct((requests, kv_dev, 8, rows), jnp.float32),
+        ],
+    )(use_rows, own_lengths, queries, kp, vp, ko, vo)
+    return acc, st
 
 
 def local(
@@ -68,70 +146,25 @@
     parents,
     out_weight,
 ):
-    tree_size = queries.shape[1]
-    heads_dev = queries.shape[2]
-    head_dim = queries.shape[3]
+    requests, tree_size, heads_dev, head_dim = queries.shape
     kv_dev = prefix_keys.shape[2]
     group_size = heads_dev // kv_dev
-    block_count = prefix_keys.shape[0]
-    block_len = prefix_keys.shape[1]
     private_dev = private_keys.shape[1]
     scaling = 1.0 / math.sqrt(head_dim)
     shard_index = lax.axis_index("seq")
-    prefix_flat_keys = prefix_keys.reshape(block_count * block_len, kv_dev, head_dim)
-    prefix_flat_values = prefix_values.reshape(block_count * block_len, kv_dev, head_dim)
-    positions = shard_index * private_dev + jnp.arange(private_dev, dtype=jnp.int32)
+    seq_size = lax.axis_size("seq")
     reach = ancestry(parents)
-
-    def one_request(item):
-        query_rows, use_row, length, own_keys, own_values = item
-        grouped = query_rows.reshape(tree_size, kv_dev, group_size, head_dim)
-        prefix_live = jnp.repeat(use_row == 1, block_len)
-        own_live = positions < length
-        prefix_scores = (
-            jnp.einsum(
-                "tkgd,nkd->tkgn", grouped, prefix_flat_keys, preferred_element_type=jnp.float32
-            )
-            * scaling
-        )
-        own_scores = (
-            jnp.einsum("tkgd,nkd->tkgn", grouped, own_keys, preferred_element_type=jnp.float32)
-            * scaling
-        )
-        prefix_scores = jnp.where(prefix_live, prefix_scores, -1e30)
-        own_scores = jnp.where(own_live, own_scores, -1e30)
-        highest = jnp.maximum(jnp.max(prefix_scores, axis=-1), jnp.max(own_scores, axis=-1))
-        prefix_weights = jnp.where(prefix_live, jnp.exp(prefix_scores - highest[..., None]), 0.0)
-        own_weights = jnp.where(own_live, jnp.exp(own_scores - highest[..., None]), 0.0)
-        totals = jnp.sum(prefix_weights, axis=-1) + jnp.sum(own_weights, axis=-1)
-        weighted = jnp.einsum(
-            "tkgn,nkd->tkgd",
-            prefix_weights.astype(jnp.bfloat16),
-            prefix_flat_values,
-            preferred_element_type=jnp.float32,
-        )
-        weighted = weighted + jnp.einsum(
-            "tkgn,nkd->tkgd",
-            own_weights.astype(jnp.bfloat16),
-            own_values,
-            preferred_element_type=jnp.float32,
-        )
-        return (
-            highest.reshape(tree_size, heads_dev),
-            totals.reshape(tree_size, heads_dev),
-            weighted.reshape(tree_size, heads_dev, head_dim),
-        )
-
-    highest, totals, weighted = lax.map(
-        one_request, (queries, block_use, private_lengths, private_keys, private_values)
-    )
-    requests = queries.shape[0]
-    seq_size = lax.axis_size("seq")
     row_count = requests * tree_size
     chunk = row_count // seq_size
-    sent = weighted.astype(jnp.bfloat16).reshape(seq_size, chunk, heads_dev, head_dim)
-    stats = jnp.stack([highest, totals], 0).reshape(2, seq_size, chunk, heads_dev)
-    stats = jnp.transpose(stats, (1, 0, 2, 3))
+    pieces = tree_size // chunk
+    own_lengths = jnp.clip(private_lengths - shard_index * private_dev, 0, private_dev)
+    acc, st = context_part(
+        queries, prefix_keys, prefix_values, block_use, own_lengths, private_keys, private_values, pieces
+    )
+    width = chunk * group_size
+    sent = acc.reshape(seq_size, kv_dev, head_dim, width)
+    stats = st[:, :, :2, :].reshape(requests, kv_dev, 2, pieces, width)
+    stats = jnp.transpose(stats, (0, 3, 2, 1, 4)).reshape(seq_size, 2, kv_dev, width)
     got = lax.all_to_all(sent, "seq", 0, 0, tiled=True)
     got_stats = lax.all_to_all(stats, "seq", 0, 0, tiled=True)
     part_top = got_stats[:, 0]
@@ -139,7 +172,14 @@
     top_all = jnp.max(part_top, axis=0)
     factor = jnp.exp(part_top - top_all[None])
     summed_totals = jnp.sum(part_totals * factor, axis=0)
-    summed_weighted = jnp.sum(got.astype(jnp.float32) * factor[..., None], axis=0)
+    summed_weighted = jnp.sum(got.astype(jnp.float32) * factor[:, :, None, :], axis=0)
+    top_all = jnp.transpose(top_all.reshape(kv_dev, chunk, group_size), (1, 0, 2)).reshape(chunk, heads_dev)
+    summed_totals = jnp.transpose(
+        summed_totals.reshape(kv_dev, chunk, group_size), (1, 0, 2)
+    ).reshape(chunk, heads_dev)
+    summed_weighted = jnp.transpose(
+        summed_weighted.reshape(kv_dev, head_dim, chunk, group_size), (2, 0, 3, 1)
+    ).reshape(chunk, heads_dev, head_dim)
     row0 = shard_index * chunk
     request = row0 // tree_size
     token0 = row0 % tree_size

time: 355 us -> 216 us (0.61)
  other arithmetic: 68 us -> 5 us
  matrix products: 71.7 us -> 9.75 us
  local copies, waits for them, and re-layouts: 62.4 us -> 11.7 us
  Pallas kernels: 0 us -> 37 us
    dot_general x32 -> x0, matrix products: 62 us -> none  [the longest x8 30 us: one_request(): jnp.einsum('tkgd,nkd->tkgn', grouped, prefix_flat_keys, preferred_element...]
    pallas_call x0 -> x1, Pallas kernels: none -> 37 us  [context_part(): pl.pallas_call(context_kernel, grid_spec=grid_spec, out_shape=[jax.ShapeD...]
    reduce_sum x9 -> x1, other arithmetic: 38.9 us -> 3.15 us  [local(): jnp.sum(got.astype(jnp.float32) * factor[:, :, None, :], axis=0)]
    dynamic_slice x24 -> x0, local copies, waits for them, and re-layouts: 32.7 us -> none  [local(): lax.map(one_request, (queries, block_use, private_lengths, private_keys,...]
    convert_element_type x8 -> x0, other arithmetic: 16.7 us -> none  [one_request(): own_weights.astype(jnp.bfloat16)]
    dynamic_update_slice x24 -> x0, local copies, waits for them, and re-layouts: 16.5 us -> none  [local(): lax.map(one_request, (queries, block_use, private_lengths, private_keys,...]
    eq x8 -> x0, other arithmetic: 5.61 us -> none  [one_request(): prefix_live = jnp.repeat(use_row == 1, block_len)]
    while x98 -> x0, local copies, waits for them, and re-layouts: 4.77 us -> none
  transfers between devices with their start and end apart: 3 -> 3, of which waited for: 3 -> 3; matrix products, arithmetic and copies ran while one was open for 2% -> 3% of each run, Pallas kernels for 0% -> 0%
where the time goes in v2:
time: 216 us; the launch traced here: 215 us
  waiting for transfers between devices  118 us (55%)
  Pallas kernels  37 us (17%)
  blocking collectives  15.1 us (7%)
  between operations  13.6 us (6%)
  local copies, waits for them, and re-layouts  11.7 us (5%)
  matrix products  9.75 us (5%)
  starting transfers between devices  5.07 us (2%)
  other arithmetic  5 us (2%)
    all_gather x1, waiting for transfers between devices, local(): attention = lax.all_gather(attention, 'seq', axis=0, tiled=True)  47.6 us
    all_to_all x1, waiting for transfers between devices, local(): got = lax.all_to_all(sent, 'seq', 0, 0, tiled=True)  46.6 us
    pallas_call x1, Pallas kernels, context_part(): pl.pallas_call(context_kernel, grid_spec=grid_spec, out_shape=[jax.ShapeD...  37 us
    reduce_scatter x1, waiting for transfers between devices, local(): lax.psum_scatter(jnp.einsum('rthd,hde->rte', attention, out_weight, prefe...  23.5 us
    all_to_all x1, blocking collectives, local(): got_stats = lax.all_to_all(stats, 'seq', 0, 0, tiled=True)  15.1 us
    unnamed x11, local copies, waits for them, and re-layouts  6.95 us
    dot_general x1, matrix products, local(): jnp.einsum('rthd,hde->rte', attention, out_weight, preferred_element_type...  6.78 us
    all_to_all x1, starting transfers between devices, local(): got = lax.all_to_all(sent, 'seq', 0, 0, tiled=True)  4.99 us
  transfers between devices with their start and end apart: 3, of which 3 were waited for; matrix products, arithmetic and copies ran while one was open for 3% of the time, Pallas kernels for 0%

profile of v2, /device:TPU:0, one launch (start us, length us, event | category | flops | bytes accessed | tf_op | source)
XLA Modules:
  0.0 215.0 jit_solution(11619102915474281192)
XLA Ops:
  6.5 0.0 copy-start
  6.5 0.0 copy-start.1
  6.5 0.0 copy-start.3
  6.5 3.7 %copy.70 = bf16[8,256,2,128]{1,3,2,0:T(8,128)(2,1)} copy(bf16[8,256,2,128]{3,2,1,0:T(2,128)(2,1)} %param.16) | data formatting | bytes 2097152 | tf_op args[5]
  10.2 2.4 %copy.109 = bf16[8,256,2,128]{3,1,2,0:T(8,128)(2,1)} copy(bf16[8,256,2,128]{3,2,1,0:T(2,128)(2,1)} %param.15) | data formatting | bytes 2097152 | tf_op args[4]
  12.6 0.0 copy-done
  12.7 0.8 copy.66
  13.5 0.0 copy-done.1
  13.5 1.0 copy.68
  14.5 0.0 copy-done.3
  14.5 0.5 subtract_clamp_fusion.len_ref
  15.0 37.0 %shard_map.109 = (bf16[8,4,2,128,256]{4,3,2,1,0:T(8,128)(2,1)}, f32[8,2,8,1024]{3,2,1,0:T(8,128)}) custom-call(s32[8,6]{1,0:T(8,128)} %use_ref.1, s32[8]{0:T(128)} %subtract_clamp_fusion.len_ref, bf16[8,64,32,128]{3,2,1,0:T(8,128)(2,1)} %q_ref.1, bf16[2,768,128]{2,1,0:T(8,128)(2,1)} %bitcast.95, bf16[2,128,768]{2,1,0:T(8,128)(2,1)} %bitcast.96, ...), custom_call_target="tpu_custom_call" | custom-call | tf_op jit(solution)/shard_map/pallas_call | solution.py:125
  52.1 1.1 slice.9
  53.1 0.1 reshape.139
  53.3 0.1 copy.71
  53.4 15.1 %all_to_all.10 = f32[32,2,2,256]{3,2,1,0:T(2,128)S(1)} all-to-all(f32[32,2,2,256]{3,2,1,0:T(2,128)S(1)} %bitcast.100), channel_id=1, replica_groups=mesh['heads'=4,'seq'=32] {'seq'}, dimensions={0} | all-to-all | bytes 262144 | tf_op jit(solution)/shard_map/all_to_all | solution.py:169
  68.4 0.0 copy-start.2
  68.4 5.0 %all-to-all-start = ((bf16[32,2,128,256]{3,2,1,0:T(8,128)(2,1)}), bf16[32,2,128,256]{3,2,1,0:T(8,128)(2,1)}, u32[]{:S(2)}, u32[]{:S(2)}) async-start(bf16[32,2,128,256]{3,2,1,0:T(8,128)(2,1)} %bitcast.94), calls=%async_computation | async-start | bytes 8388608 | tf_op jit(solution)/shard_map/all_to_all | solution.py:168
  73.4 0.0 all-gather.2.cloned.1.call-start
  73.5 0.0 copy-done.2
  73.5 0.5 convolution_minimum_fusion.4
  74.0 0.4 convolution_minimum_fusion.3
  74.4 0.4 convolution_minimum_fusion.2
  74.8 0.4 convolution_minimum_fusion.1
  75.2 0.4 convolution_minimum_fusion
  75.6 0.4 fusion.42
  76.0 0.8 constant_dynamic-slice_fusion
  76.9 0.9 constant_dynamic-slice_fusion.1
  77.8 0.3 fusion.41
  78.1 0.2 fusion.15
  78.4 0.1 squeeze_reshape.11
  78.5 0.1 squeeze_reshape.9
  78.5 0.3 convolution_bitcast_fusion
  78.9 0.1 reshape.143
  79.0 0.1 fusion.26
  79.0 0.1 reshape.150
  79.1 0.1 reshape.151
  79.2 0.1 reshape.144
  79.3 46.6 %all-to-all-done = bf16[32,2,128,256]{3,2,1,0:T(8,128)(2,1)} async-done(((bf16[32,2,128,256]{3,2,1,0:T(8,128)(2,1)}), bf16[32,2,128,256]{3,2,1,0:T(8,128)(2,1)}, u32[]{:S(2)}, u32[]{:S(2)}) %all-to-all-start) | async-done | bytes 4194336 | tf_op jit(solution)/shard_map/all_to_all | solution.py:168
  126.0 3.1 %multiply_reduce_fusion = f32[2,128,256]{2,1,0:T(8,128)S(1)} fusion(bf16[32,2,128,256]{3,2,1,0:T(8,128)(2,1)} %all-to-all-done, f32[32,2,256]{2,1,0:T(2,128)S(1)} %get-tuple-element.13), kind=kLoop, calls=%fused_computation | loop fusion | flops 6225920 | bytes 4521984 | tf_op jit(solution)/shard_map/reduce_sum | solution.py:175
  129.1 0.1 copy.73
  129.3 0.9 fusion.12
  130.2 0.0 all-gather.2.cloned.1.call-update
  130.2 0.0 reduce-scatter.2.cloned.1.call-start
  130.3 47.6 %all-gather.2.cloned.1.call-done = bf16[512,32,128]{2,1,0:T(8,128)(2,1)} async-done(((bf16[16,32,128]{2,1,0:T(8,128)(2,1)}), bf16[512,32,128]{2,1,0:T(8,128)(2,1)}) %all-gather.2.cloned.1.call-update) | async-done | bytes 4194320 | tf_op jit(solution)/shard_map/all_gather | solution.py:200
  177.9 6.8 %fusion.3 = f32[8,64,512]{2,1,0:T(8,128)} fusion(bf16[32,128,512]{2,1,0:T(8,128)(2,1)} %param.21, bf16[8,64,32,128]{3,2,1,0:T(8,128)(2,1)} %bitcast.104), kind=kOutput, calls=%fused_computation.4 | convolution fusion | flops 2147483648 | bytes 9437184 | tf_op jit(solution)/shard_map/rthd,hde->rte/dot_general | solution.py:203
  184.6 0.0 reduce-scatter.2.cloned.1.call-update
  184.7 23.5 %reduce-scatter.2.cloned.1.call-done = f32[2,64,512]{2,1,0:T(8,128)} async-done(((f32[8,64,512]{2,1,0:T(8,128)}), f32[2,64,512]{2,1,0:T(8,128)}) %reduce-scatter.2.cloned.1.call-update) | async-done | bytes 262160 | tf_op jit(solution)/shard_map/reduce_scatter | solution.py:202
  (10 shorter events, 0.2 us)
Async XLA Ops:
  6.5 6.1 %copy-start = (bf16[6,128,2,128]{3,2,1,0:T(2,128)(2,1)S(1)}, bf16[6,128,2,128]{3,2,1,0:T(2,128)(2,1)}, u32[]{:S(2)}) copy-start(bf16[6,128,2,128]{3,2,1,0:T(2,128)(2,1)} %param.12) | copy-start | bytes 1179652
  6.5 6.9 %copy-start.1 = (bf16[6,128,2,128]{3,2,1,0:T(2,128)(2,1)S(1)}, bf16[6,128,2,128]{3,2,1,0:T(2,128)(2,1)}, u32[]{:S(2)}) copy-start(bf16[6,128,2,128]{3,2,1,0:T(2,128)(2,1)} %param.13) | copy-start | bytes 1179652
  6.5 8.0 %copy-start.3 = (s32[8]{0:T(128)S(1)}, s32[8]{0:T(128)}, u32[]{:S(2)}) copy-start(s32[8]{0:T(128)} %param.17) | copy-start | bytes 100
  68.4 5.1 %copy-start.2 = (s32[8,64]{1,0:T(8,128)S(1)}, s32[8,64]{1,0:T(8,128)}, u32[]{:S(2)}) copy-start(s32[8,64]{1,0:T(8,128)} %param.20) | copy-start | bytes 6148
  68.4 57.5 %all-to-all-start = ((bf16[32,2,128,256]{3,2,1,0:T(8,128)(2,1)}), bf16[32,2,128,256]{3,2,1,0:T(8,128)(2,1)}, u32[]{:S(2)}, u32[]{:S(2)}) async-start(bf16[32,2,128,256]{3,2,1,0:T(8,128)(2,1)} %bitcast.94), calls=%async_computation | async-start | bytes 8388608 | tf_op jit(solution)/shard_map/all_to_all | solution.py:168
  73.4 104.4 %all-gather.2.cloned.1.call-start = ((), (), s32[]{:S(2)}) async-start(), calls=%async_computation.3 | async-start | bytes 4325376 | tf_op jit(solution)/shard_map/all_gather | solution.py:200
  130.2 77.9 %reduce-scatter.2.cloned.1.call-start = ((), (), s32[]{:S(2)}) async-start(), calls=%async_computation.4 | async-start | bytes 1310720 | tf_op jit(solution)/shard_map/reduce_scatter | solution.py:202
Sparse Core Ops, SparseCore 0:
  130.4 47.4 all-gather.1
  184.8 23.3 reduce-scatter.1

commit v3 on v2

--- a/solution.py
+++ b/solution.py
@@ -57,7 +57,7 @@
     )
 
 
-def context_kernel(use_ref, len_ref, q_ref, kp_ref, vp_ref, ko_ref, vo_ref, acc_ref, st_ref):
+def context_kernel(use_ref, len_ref, q_ref, kp_ref, vp_ref, ko_ref, vo_ref, acc_ref):
     r = pl.program_id(1)
     scaling = 1.0 / math.sqrt(q_ref.shape[-1])
     q = q_ref[0].reshape(-1, q_ref.shape[-1])
@@ -79,20 +79,25 @@
     top = jnp.maximum(
         jnp.max(s_pre, axis=0, keepdims=True), jnp.max(s_own, axis=0, keepdims=True)
     )
-    w_pre = jnp.where(pre_live, jnp.exp(s_pre - top), 0.0)
-    w_own = jnp.where(own_live, jnp.exp(s_own - top), 0.0)
+    top = jnp.maximum(top, -1e29).astype(jnp.bfloat16).astype(jnp.float32)
+    w_pre = jnp.exp(s_pre - top)
+    w_own = jnp.exp(s_own - top)
     totals = jnp.sum(w_pre, axis=0, keepdims=True) + jnp.sum(w_own, axis=0, keepdims=True)
     acc = jnp.dot(vp_ref[0], w_pre.astype(jnp.bfloat16), preferred_element_type=jnp.float32)
     acc = acc + jnp.dot(
         vo_ref[0, 0], w_own.astype(jnp.bfloat16), preferred_element_type=jnp.float32
     )
+    head_dim = acc.shape[0]
     pieces = acc_ref.shape[1]
     width = acc_ref.shape[-1]
+    extra = acc_ref.shape[3] - head_dim
+    high = totals.astype(jnp.bfloat16).astype(jnp.float32)
+    low = totals - high
+    row_id = lax.broadcasted_iota(jnp.int32, (extra, totals.shape[1]), 0)
+    stats = jnp.where(row_id == 0, top, jnp.where(row_id == 1, high, jnp.where(row_id == 2, low, 0.0)))
     for c in range(pieces):
-        acc_ref[0, c, 0] = acc[:, c * width : (c + 1) * width].astype(acc_ref.dtype)
-    st_ref[0, 0] = jnp.zeros(st_ref.shape[2:], jnp.float32)
-    st_ref[0, 0, 0:1, :] = top
-    st_ref[0, 0, 1:2, :] = totals
+        acc_ref[0, c, 0, 0:head_dim, :] = acc[:, c * width : (c + 1) * width].astype(acc_ref.dtype)
+        acc_ref[0, c, 0, head_dim:, :] = stats[:, c * width : (c + 1) * width].astype(acc_ref.dtype)
 
 
 def context_part(queries, prefix_keys, prefix_values, use_rows, own_lengths, own_keys, own_values, pieces):
@@ -117,20 +122,17 @@
             pl.BlockSpec((1, 1, private_dev, head_dim), lambda k, r, u, n: (r, k, 0, 0)),
             pl.BlockSpec((1, 1, head_dim, private_dev), lambda k, r, u, n: (r, k, 0, 0)),
         ],
-        out_specs=[
-            pl.BlockSpec((1, pieces, 1, head_dim, width), lambda k, r, u, n: (r, 0, k, 0, 0)),
-            pl.BlockSpec((1, 1, 8, rows), lambda k, r, u, n: (r, k, 0, 0)),
-        ],
-    )
-    acc, st = pl.pallas_call(
+        out_specs=pl.BlockSpec(
+            (1, pieces, 1, head_dim + 16, width), lambda k, r, u, n: (r, 0, k, 0, 0)
+        ),
+    )
+    return pl.pallas_call(
         context_kernel,
         grid_spec=grid_spec,
-        out_shape=[
-            jax.ShapeDtypeStruct((requests, pieces, kv_dev, head_dim, width), jnp.bfloat16),
-            jax.ShapeDtypeStruct((requests, kv_dev, 8, rows), jnp.float32),
-        ],
+        out_shape=jax.ShapeDtypeStruct(
+            (requests, pieces, kv_dev, head_dim + 16, width), jnp.bfloat16
+        ),
     )(use_rows, own_lengths, queries, kp, vp, ko, vo)
-    return acc, st
 
 
 def local(
@@ -158,21 +160,22 @@
     chunk = row_count // seq_size
     pieces = tree_size // chunk
     own_lengths = jnp.clip(private_lengths - shard_index * private_dev, 0, private_dev)
-    acc, st = context_part(
+    acc = context_part(
         queries, prefix_keys, prefix_values, block_use, own_lengths, private_keys, private_values, pieces
     )
     width = chunk * group_size
-    sent = acc.reshape(seq_size, kv_dev, head_dim, width)
-    stats = st[:, :, :2, :].reshape(requests, kv_dev, 2, pieces, width)
-    stats = jnp.transpose(stats, (0, 3, 2, 1, 4)).reshape(seq_size, 2, kv_dev, width)
+    sent = acc.reshape(seq_size, kv_dev, head_dim + 16, width)
     got = lax.all_to_all(sent, "seq", 0, 0, tiled=True)
-    got_stats = lax.all_to_all(stats, "seq", 0, 0, tiled=True)
-    part_top = got_stats[:, 0]
-    part_totals = got_stats[:, 1]
+    part_top = got[:, :, head_dim].astype(jnp.float32)
+    part_totals = got[:, :, head_dim + 1].astype(jnp.float32) + got[:, :, head_dim + 2].astype(
+        jnp.float32
+    )
     top_all = jnp.max(part_top, axis=0)
     factor = jnp.exp(part_top - top_all[None])
     summed_totals = jnp.sum(part_totals * factor, axis=0)
-    summed_weighted = jnp.sum(got.astype(jnp.float32) * factor[:, :, None, :], axis=0)
+    summed_weighted = jnp.sum(
+        got[:, :, :head_dim].astype(jnp.float32) * factor[:, :, None, :], axis=0
+    )
     top_all = jnp.transpose(top_all.reshape(kv_dev, chunk, group_size), (1, 0, 2)).reshape(chunk, heads_dev)
     summed_totals = jnp.transpose(
         summed_totals.reshape(kv_dev, chunk, group_size), (1, 0, 2)
@@ -199,12 +202,10 @@
     attention = (final_weighted / final_totals[..., None]).astype(jnp.bfloat16)
     attention = lax.all_gather(attention, "seq", axis=0, tiled=True)
     attention = attention.reshape(requests, tree_size, heads_dev, head_dim)
-    return lax.psum_scatter(
-        jnp.einsum("rthd,hde->rte", attention, out_weight, preferred_element_type=jnp.float32),
-        "heads",
-        scatter_dimension=0,
-        tiled=True,
-    )
+    heads_size = lax.axis_size("heads")
+    partial = jnp.einsum("rthd,hde->rte", attention, out_weight, preferred_element_type=jnp.float32)
+    partial = partial.reshape(heads_size, requests // heads_size, tree_size, partial.shape[-1])
+    return jnp.sum(lax.all_to_all(partial, "heads", 0, 0, tiled=True), axis=0)
 
 
 def solution(mesh):

time: 216 us -> 204 us (0.944)
  waiting for transfers between devices: 118 us -> 101 us
  blocking collectives: 15.1 us -> 19.7 us
  matrix products: 9.75 us -> 5.3 us
  Pallas kernels: 37 us -> 33.5 us
  other arithmetic: 5 us -> 8.16 us
  local copies, waits for them, and re-layouts: 11.7 us -> 14.6 us
  starting transfers between devices: 5.07 us -> 7.72 us
    reduce_scatter x1 -> x0, waiting for transfers between devices: 23.5 us -> none  [local(): lax.psum_scatter(jnp.einsum('rthd,hde->rte', attention, out_weight, prefe...]
    all_to_all x1, waiting for transfers between devices: 46.6 us -> 53.4 us  [local(): got = lax.all_to_all(sent, 'seq', 0, 0, tiled=True)]
    all_to_all x1, blocking collectives: 15.1 us -> 19.7 us  [local(): return jnp.sum(lax.all_to_all(partial, 'heads', 0, 0, tiled=True), axis=0)]
    dot_general x1, matrix products: 6.78 us -> 2.32 us  [local(): jnp.einsum('rthd,hde->rte', attention, out_weight, preferred_element_type...]
    dot_general x0 -> x1, local copies, waits for them, and re-layouts: none -> 3.96 us  [local(): jnp.einsum('rthd,hde->rte', attention, out_weight, preferred_element_type...]
    pallas_call x1, Pallas kernels: 37 us -> 33.5 us  [context_part(): pl.pallas_call(context_kernel, grid_spec=grid_spec, out_shape=jax.ShapeDt...]
    all_to_all x1, starting transfers between devices: 4.99 us -> 7.67 us  [local(): got = lax.all_to_all(sent, 'seq', 0, 0, tiled=True)]
  transfers between devices with their start and end apart: 3 -> 2, of which waited for: 3 -> 2; matrix products, arithmetic and copies ran while one was open for 3% -> 3% of each run, Pallas kernels for 0% -> 0%
where the time goes in v3:
time: 204 us
  waiting for transfers between devices  101 us (50%)
  Pallas kernels  33.5 us (16%)
  blocking collectives  19.7 us (10%)
  local copies, waits for them, and re-layouts  14.6 us (7%)
  between operations  13.6 us (7%)
  other arithmetic  8.16 us (4%)
  starting transfers between devices  7.72 us (4%)
  matrix products  5.3 us (3%)
    all_to_all x1, waiting for transfers between devices, local(): got = lax.all_to_all(sent, 'seq', 0, 0, tiled=True)  53.4 us
    all_gather x1, waiting for transfers between devices, local(): attention = lax.all_gather(attention, 'seq', axis=0, tiled=True)  47.9 us
    pallas_call x1, Pallas kernels, context_part(): pl.pallas_call(context_kernel, grid_spec=grid_spec, out_shape=jax.ShapeDt...  33.5 us
    all_to_all x1, blocking collectives, local(): return jnp.sum(lax.all_to_all(partial, 'heads', 0, 0, tiled=True), axis=0)  19.7 us
    all_to_all x1, starting transfers between devices, local(): got = lax.all_to_all(sent, 'seq', 0, 0, tiled=True)  7.67 us
    unnamed x11, local copies, waits for them, and re-layouts  6.3 us
  transfers between devices with their start and end apart: 2, of which 2 were waited for; matrix products, arithmetic and copies ran while one was open for 3% of the time, Pallas kernels for 0%

profile of v3, /device:TPU:0, one launch (start us, length us, event | category | flops | bytes accessed | tf_op | source)
XLA Modules:
  0.0 203.9 jit_solution(11188204428376476443)
XLA Ops:
  6.5 0.0 copy-start
  6.5 0.0 copy-start.3
  6.5 1.9 copy.64
  8.4 1.9 copy.66
  10.4 2.5 %copy.110 = bf16[8,256,2,128]{3,1,2,0:T(8,128)(2,1)} copy(bf16[8,256,2,128]{3,2,1,0:T(2,128)(2,1)} %param.15) | data formatting | bytes 2097152 | tf_op args[4]
  12.8 0.0 copy-done
  12.8 1.9 copy.68
  14.8 0.0 copy-done.3
  14.8 0.5 subtract_clamp_fusion.len_ref
  15.3 33.5 %shard_map.109 = bf16[8,4,2,144,256]{4,3,2,1,0:T(8,128)(2,1)} custom-call(s32[8,6]{1,0:T(8,128)} %use_ref.1, s32[8]{0:T(128)} %subtract_clamp_fusion.len_ref, bf16[8,64,32,128]{3,2,1,0:T(8,128)(2,1)} %q_ref.1, bf16[2,768,128]{2,1,0:T(8,128)(2,1)} %bitcast.102, bf16[2,128,768]{2,1,0:T(8,128)(2,1)} %bitcast.103, bf16[8,2,256,128]{3,2,1,0:T(8,128)(2,1)} %bitcast.100, ...), custom_call_target="tpu_custom_call" | custom-call | tf_op jit(solution)/shard_map/pallas_call | solution.py:129
  48.8 0.0 copy-start.1
  48.8 7.7 %all-to-all-start = ((bf16[32,2,144,256]{3,2,1,0:T(8,128)(2,1)}), bf16[32,2,144,256]{3,2,1,0:T(8,128)(2,1)}, u32[]{:S(2)}, u32[]{:S(2)}) async-start(bf16[32,2,144,256]{3,2,1,0:T(8,128)(2,1)} %bitcast.96), calls=%async_computation | async-start | bytes 9437184 | tf_op jit(solution)/shard_map/all_to_all | solution.py:168
  56.5 0.0 all-gather.2.cloned.1.call-start
  56.5 0.0 copy-done.1
  56.6 0.5 convolution_minimum_fusion.4
  57.1 0.4 convolution_minimum_fusion.3
  57.5 0.4 convolution_minimum_fusion.2
  57.9 0.4 convolution_minimum_fusion.1
  58.3 0.4 convolution_minimum_fusion
  58.6 0.4 fusion.43
  59.1 0.8 constant_dynamic-slice_fusion
  59.9 0.9 constant_dynamic-slice_fusion.1
  60.8 0.3 fusion.42
  61.1 0.3 convolution_bitcast_fusion
  61.4 0.2 fusion.12
  61.7 0.1 squeeze_reshape.11
  61.8 0.1 squeeze_reshape.9
  61.9 53.4 %all-to-all-done = bf16[32,2,144,256]{3,2,1,0:T(8,128)(2,1)} async-done(((bf16[32,2,144,256]{3,2,1,0:T(8,128)(2,1)}), bf16[32,2,144,256]{3,2,1,0:T(8,128)(2,1)}, u32[]{:S(2)}, u32[]{:S(2)}) %all-to-all-start) | async-done | bytes 4718624 | tf_op jit(solution)/shard_map/all_to_all | solution.py:168
  115.2 1.0 fusion.41
  116.3 0.1 reshape.157
  116.4 0.1 fusion.23
  116.4 3.2 %multiply_reduce_fusion = f32[2,128,256]{2,1,0:T(8,128)S(1)} fusion(bf16[32,2,144,256]{3,2,1,0:T(8,128)(2,1)} %all-to-all-done, f32[32,2,256]{2,1,0:T(2,128)S(1)} %fusion.23), kind=kLoop, calls=%fused_computation | loop fusion | flops 6225920 | bytes 4521984 | tf_op jit(solution)/shard_map/reduce_sum | solution.py:176
  119.6 0.1 copy.70
  119.8 1.3 fusion.27
  121.0 0.1 fusion.28
  121.1 0.1 reshape.149
  121.2 0.1 reshape.150
  121.3 0.1 reshape.153
  121.4 0.9 fusion.9
  122.3 0.0 all-gather.2.cloned.1.call-update
  122.4 47.9 %all-gather.2.cloned.1.call-done = bf16[512,32,128]{2,1,0:T(8,128)(2,1)} async-done(((bf16[16,32,128]{2,1,0:T(8,128)(2,1)}), bf16[512,32,128]{2,1,0:T(8,128)(2,1)}) %all-gather.2.cloned.1.call-update) | async-done | bytes 4194320 | tf_op jit(solution)/shard_map/all_gather | solution.py:203
  170.3 0.0 copy-start.2
  170.3 4.0 %copy.80 = bf16[8,64,128,32]{2,1,3,0:T(8,128)(2,1)S(1)} copy(bf16[8,64,128,32]{2,3,1,0:T(8,128)(2,1)} %bitcast.98) | data formatting | bytes 8388608 | tf_op jit(solution)/shard_map/rthd,hde->rte/dot_general | solution.py:206
  174.3 0.0 copy-done.2
  174.3 2.3 %fusion.2 = f32[4,2,64,512]{3,2,1,0:T(8,128)S(1)} fusion(bf16[4,2,64,128,32]{3,2,4,1,0:T(8,128)(2,1)S(1)} %bitcast.99, bf16[32,128,512]{2,1,0:T(8,128)(2,1)S(1)} %copy-done.2), kind=kOutput, calls=%fused_computation.3 | convolution fusion | flops 2147483648 | bytes 9437184 | tf_op jit(solution)/shard_map/rthd,hde->rte/dot_general | solution.py:206
  176.6 19.7 %all_to_all.10 = f32[4,2,64,512]{3,2,1,0:T(8,128)S(1)} all-to-all(f32[4,2,64,512]{3,2,1,0:T(8,128)S(1)} %fusion.2), channel_id=1, replica_groups=mesh['heads'=4,'seq'=32] {'heads'}, dimensions={0} | all-to-all | bytes 2097152 | tf_op jit(solution)/shard_map/all_to_all | solution.py:208
  196.3 0.8 reduce_sum.39
  (10 shorter events, 0.1 us)
Async XLA Ops:
  6.5 6.3 %copy-start = (bf16[8,256,2,128]{3,2,1,0:T(2,128)(2,1)S(1)}, bf16[8,256,2,128]{3,2,1,0:T(2,128)(2,1)}, u32[]{:S(2)}) copy-start(bf16[8,256,2,128]{3,2,1,0:T(2,128)(2,1)} %param.16) | copy-start | bytes 3145732
  6.5 8.2 %copy-start.3 = (s32[8]{0:T(128)S(1)}, s32[8]{0:T(128)}, u32[]{:S(2)}) copy-start(s32[8]{0:T(128)} %param.17) | copy-start | bytes 100
  48.8 7.8 %copy-start.1 = (s32[8,64]{1,0:T(8,128)S(1)}, s32[8,64]{1,0:T(8,128)}, u32[]{:S(2)}) copy-start(s32[8,64]{1,0:T(8,128)} %param.20) | copy-start | bytes 6148
  48.8 66.5 %all-to-all-start = ((bf16[32,2,144,256]{3,2,1,0:T(8,128)(2,1)}), bf16[32,2,144,256]{3,2,1,0:T(8,128)(2,1)}, u32[]{:S(2)}, u32[]{:S(2)}) async-start(bf16[32,2,144,256]{3,2,1,0:T(8,128)(2,1)} %bitcast.96), calls=%async_computation | async-start | bytes 9437184 | tf_op jit(solution)/shard_map/all_to_all | solution.py:168
  56.5 113.8 %all-gather.2.cloned.1.call-start = ((), (), s32[]{:S(2)}) async-start(), calls=%async_computation.2 | async-start | bytes 4325376 | tf_op jit(solution)/shard_map/all_gather | solution.py:203
  170.3 4.0 %copy-start.2 = (bf16[32,128,512]{2,1,0:T(8,128)(2,1)S(1)}, bf16[32,128,512]{2,1,0:T(8,128)(2,1)}, u32[]{:S(2)}) copy-start(bf16[32,128,512]{2,1,0:T(8,128)(2,1)} %param.21) | copy-start | bytes 12582916
Sparse Core Ops, SparseCore 0:
  122.5 47.7 all-gather.1

commit v4 on v3

--- a/solution.py
+++ b/solution.py
@@ -5,7 +5,8 @@
 from jax import lax
 from jax.experimental import pallas as pl
 from jax.experimental.pallas import tpu as pltpu
-from jax.sharding import PartitionSpec as P
+from jax.sharding import Mesh, PartitionSpec as P
+import numpy as np
 
 
 def ancestry(parents):
@@ -135,6 +136,18 @@
     )(use_rows, own_lengths, queries, kp, vp, ko, vo)
 
 
+SEQ = ("sx", "sy", "sc")
+
+
+def unpack(parts, head_dim, axis):
+    top = parts[:, :, :, head_dim] if axis == 1 else parts[:, :, head_dim]
+    high = parts[:, :, :, head_dim + 1] if axis == 1 else parts[:, :, head_dim + 1]
+    low = parts[:, :, :, head_dim + 2] if axis == 1 else parts[:, :, head_dim + 2]
+    weighted = parts[:, :, :, :head_dim] if axis == 1 else parts[:, :, :head_dim]
+    totals = high.astype(jnp.float32) + low.astype(jnp.float32)
+    return top.astype(jnp.float32), totals, weighted.astype(jnp.float32)
+
+
 def local(
     queries,
     prefix_keys,
@@ -153,8 +166,8 @@
     group_size = heads_dev // kv_dev
     private_dev = private_keys.shape[1]
     scaling = 1.0 / math.sqrt(head_dim)
-    shard_index = lax.axis_index("seq")
-    seq_size = lax.axis_size("seq")
+    shard_index = lax.axis_index(SEQ)
+    seq_size = lax.axis_size(SEQ)
     reach = ancestry(parents)
     row_count = requests * tree_size
     chunk = row_count // seq_size
@@ -164,18 +177,34 @@
         queries, prefix_keys, prefix_values, block_use, own_lengths, private_keys, private_values, pieces
     )
     width = chunk * group_size
-    sent = acc.reshape(seq_size, kv_dev, head_dim + 16, width)
-    got = lax.all_to_all(sent, "seq", 0, 0, tiled=True)
-    part_top = got[:, :, head_dim].astype(jnp.float32)
-    part_totals = got[:, :, head_dim + 1].astype(jnp.float32) + got[:, :, head_dim + 2].astype(
-        jnp.float32
-    )
+    pair = lax.axis_size("sc")
+    core = lax.axis_index("sc")
+    parts = acc.reshape(seq_size // pair, pair, kv_dev, head_dim + 16, width)
+    parts = lax.all_to_all(parts, "sc", 1, 1, tiled=True)
+    part_top, part_totals, part_weighted = unpack(parts, head_dim, 1)
+    pair_top = jnp.max(part_top, axis=1)
+    factor = jnp.exp(part_top - pair_top[:, None])
+    pair_totals = jnp.sum(part_totals * factor, axis=1)
+    pair_weighted = jnp.sum(part_weighted * factor[:, :, :, None, :], axis=1)
+    high = pair_totals.astype(jnp.bfloat16)
+    low = (pair_totals - high.astype(jnp.float32)).astype(jnp.bfloat16)
+    zeros = jnp.zeros(pair_top.shape[:2] + (13,) + pair_top.shape[2:], jnp.bfloat16)
+    sent = jnp.concatenate(
+        [
+            pair_weighted.astype(jnp.bfloat16),
+            pair_top.astype(jnp.bfloat16)[:, :, None],
+            high[:, :, None],
+            low[:, :, None],
+            zeros,
+        ],
+        axis=2,
+    )
+    got = lax.all_to_all(sent, ("sx", "sy"), 0, 0, tiled=True)
+    part_top, part_totals, part_weighted = unpack(got, head_dim, 0)
     top_all = jnp.max(part_top, axis=0)
     factor = jnp.exp(part_top - top_all[None])
     summed_totals = jnp.sum(part_totals * factor, axis=0)
-    summed_weighted = jnp.sum(
-        got[:, :, :head_dim].astype(jnp.float32) * factor[:, :, None, :], axis=0
-    )
+    summed_weighted = jnp.sum(part_weighted * factor[:, :, None, :], axis=0)
     top_all = jnp.transpose(top_all.reshape(kv_dev, chunk, group_size), (1, 0, 2)).reshape(chunk, heads_dev)
     summed_totals = jnp.transpose(
         summed_totals.reshape(kv_dev, chunk, group_size), (1, 0, 2)
@@ -200,7 +229,11 @@
         (top_all, summed_totals, summed_weighted), draft
     )
     attention = (final_weighted / final_totals[..., None]).astype(jnp.bfloat16)
-    attention = lax.all_gather(attention, "seq", axis=0, tiled=True)
+    attention = lax.all_gather(attention, ("sx", "sy"), axis=0, tiled=False)
+    other = lax.ppermute(attention, "sc", [(i, (i + 1) % pair) for i in range(pair)])
+    first = jnp.where(core == 0, attention, other)
+    second = jnp.where(core == 0, other, attention)
+    attention = jnp.stack([first, second], 1)
     attention = attention.reshape(requests, tree_size, heads_dev, head_dim)
     heads_size = lax.axis_size("heads")
     partial = jnp.einsum("rthd,hde->rte", attention, out_weight, preferred_element_type=jnp.float32)
@@ -209,22 +242,25 @@
 
 
 def solution(mesh):
+    heads_size = mesh.shape["heads"]
+    sizes = [mesh.shape["seq"] // 8, 4, 2]
+    fine = Mesh(np.asarray(mesh.devices).reshape([heads_size] + sizes), ("heads",) + SEQ)
     return jax.shard_map(
         local,
-        mesh=mesh,
+        mesh=fine,
         in_specs=(
             P(None, None, "heads", None),
-            P("seq", None, "heads", None),
-            P("seq", None, "heads", None),
-            P(None, "seq"),
-            P(None, "seq", "heads", None),
-            P(None, "seq", "heads", None),
+            P(SEQ, None, "heads", None),
+            P(SEQ, None, "heads", None),
+            P(None, SEQ),
+            P(None, SEQ, "heads", None),
+            P(None, SEQ, "heads", None),
             P(),
             P(None, None, "heads", None),
             P(None, None, "heads", None),
             P(),
-            P("heads", None, "seq"),
+            P("heads", None, SEQ),
         ),
-        out_specs=P("heads", None, "seq"),
+        out_specs=P("heads", None, SEQ),
         check_vma=False,
     )

time: 204 us -> 203 us (level)
  waiting for transfers between devices: 101 us -> 77.9 us
  local copies, waits for them, and re-layouts: 14.6 us -> 28.7 us
  blocking collectives: 19.7 us -> 27.1 us
    all_to_all x1, waiting for transfers between devices: 53.4 us -> 28.1 us  [local(): got = lax.all_to_all(sent, ('sx', 'sy'), 0, 0, tiled=True)]
    concatenate x0 -> x2, local copies, waits for them, and re-layouts: none -> 11.8 us  [local(): jnp.concatenate([pair_weighted.astype(jnp.bfloat16), pair_top.astype(jnp....]
    all_to_all x0 -> x1, blocking collectives: none -> 7.52 us  [local(): parts = lax.all_to_all(parts, 'sc', 1, 1, tiled=True)]
    ppermute x0 -> x1, waiting for transfers between devices: none -> 4.37 us  [local(): lax.ppermute(attention, 'sc', [(i, (i + 1) % pair) for i in range(pair)])]
    reshape x0 -> x1, local copies, waits for them, and re-layouts: none -> 2.64 us  [local(): parts = acc.reshape(seq_size // pair, pair, kv_dev, head_dim + 16, width)]
    all_gather x1, waiting for transfers between devices: 47.9 us -> 45.4 us  [local(): attention = lax.all_gather(attention, ('sx', 'sy'), axis=0, tiled=False)]
    dot_general x1, local copies, waits for them, and re-layouts: 3.96 us -> 1.63 us  [local(): jnp.einsum('rthd,hde->rte', attention, out_weight, preferred_element_type...]
    another operation x0 -> x2, other arithmetic: none -> 2.26 us  [local(): attention = jnp.stack([first, second], 1)]
  transfers between devices with their start and end apart: 2 -> 3, of which waited for: 2 -> 3; matrix products, arithmetic and copies ran while one was open for 3% -> 3% of each run, Pallas kernels for 0% -> 0%
where the time goes in v4:
time: 203 us; the launch traced here: 202 us
  waiting for transfers between devices  77.9 us (38%)
  Pallas kernels  33.5 us (17%)
  local copies, waits for them, and re-layouts  28.7 us (14%)
  blocking collectives  27.1 us (13%)
  between operations  13.7 us (7%)
  other arithmetic  8.59 us (4%)
  starting transfers between devices  7.37 us (4%)
  matrix products  5.29 us (3%)
    all_gather x1, waiting for transfers between devices, local(): attention = lax.all_gather(attention, ('sx', 'sy'), axis=0, tiled=False)  45.4 us
    pallas_call x1, Pallas kernels, context_part(): pl.pallas_call(context_kernel, grid_spec=grid_spec, out_shape=jax.ShapeDt...  33.5 us
    all_to_all x1, waiting for transfers between devices, local(): got = lax.all_to_all(sent, ('sx', 'sy'), 0, 0, tiled=True)  28.1 us
    all_to_all x1, blocking collectives, local(): return jnp.sum(lax.all_to_all(partial, 'heads', 0, 0, tiled=True), axis=0)  19.6 us
    concatenate x2, local copies, waits for them, and re-layouts, local(): jnp.concatenate([pair_weighted.astype(jnp.bfloat16), pair_top.astype(jnp....  11.8 us
    unnamed x13, local copies, waits for them, and re-layouts  7.54 us
    all_to_all x1, blocking collectives, local(): parts = lax.all_to_all(parts, 'sc', 1, 1, tiled=True)  7.52 us
    all_to_all x1, starting transfers between devices, local(): got = lax.all_to_all(sent, ('sx', 'sy'), 0, 0, tiled=True)  7.14 us
  transfers between devices with their start and end apart: 3, of which 3 were waited for; matrix products, arithmetic and copies ran while one was open for 3% of the time, Pallas kernels for 0%

profile of v4, /device:TPU:0, one launch (start us, length us, event | category | flops | bytes accessed | tf_op | source)
XLA Modules:
  0.0 202.2 jit_solution(1485896831297310540)
XLA Ops:
  6.5 0.0 copy-start
  6.5 0.0 copy-start.1
  6.5 0.0 copy-start.4
  6.5 2.5 %copy.199 = bf16[8,256,2,128]{3,1,2,0:T(8,128)(2,1)} copy(bf16[8,256,2,128]{3,2,1,0:T(2,128)(2,1)} %param.15) | data formatting | bytes 2097152 | tf_op args[4]
  9.1 3.6 %copy.146 = bf16[8,256,2,128]{1,3,2,0:T(8,128)(2,1)} copy(bf16[8,256,2,128]{3,2,1,0:T(2,128)(2,1)} %param.16) | data formatting | bytes 2097152 | tf_op args[5]
  12.7 0.0 copy-done
  12.7 0.8 copy.142
  13.5 0.0 copy-done.1
  13.5 1.0 copy.144
  14.6 0.0 copy-done.4
  14.6 0.5 subtract_clamp_fusion.len_ref
  15.1 33.5 %shard_map.109 = bf16[8,4,2,144,256]{4,3,2,1,0:T(8,128)(2,1)} custom-call(s32[8,6]{1,0:T(8,128)} %use_ref.1, s32[8]{0:T(128)} %subtract_clamp_fusion.len_ref, bf16[8,64,32,128]{3,2,1,0:T(8,128)(2,1)} %q_ref.1, bf16[2,768,128]{2,1,0:T(8,128)(2,1)} %bitcast.131, bf16[2,128,768]{2,1,0:T(8,128)(2,1)} %bitcast.132, bf16[8,2,256,128]{3,2,1,0:T(8,128)(2,1)} %bitcast.129, ...), custom_call_target="tpu_custom_call" | custom-call | tf_op jit(solution)/shard_map/pallas_call | solution.py:130
  48.6 2.6 %copy.147 = bf16[16,2,2,144,256]{4,3,2,0,1:T(8,128)(2,1)S(1)} copy(bf16[16,2,2,144,256]{4,3,2,1,0:T(8,128)(2,1)} %bitcast.125) | data formatting | bytes 9437184 | tf_op jit(solution)/shard_map/reshape | solution.py:182
  51.2 7.5 %all_to_all.15 = bf16[16,2,2,144,256]{4,3,2,0,1:T(8,128)(2,1)S(1)} all-to-all(bf16[16,2,2,144,256]{4,3,2,0,1:T(8,128)(2,1)S(1)} %copy.147), channel_id=1, replica_groups=mesh['heads'=4,'sx'=4,'sy'=4,'sc'=2] {'sc'}, dimensions={1} | all-to-all | bytes 9437184 | tf_op jit(solution)/shard_map/all_to_all | solution.py:183
  58.7 0.1 fusion.48
  58.9 0.1 fusion.28
  59.0 0.1 fusion.27
  59.2 0.1 fusion.23
  59.3 2.8 %multiply_reduce_fusion = bf16[16,2,128,256]{3,2,1,0:T(8,128)(2,1)} fusion(bf16[16,2,2,144,256]{4,3,2,0,1:T(8,128)(2,1)S(1)} %all_to_all.15, f32[16,2,2,256]{3,2,0,1:T(2,128)S(1)} %fusion.23), kind=kLoop, calls=%fused_computation | loop fusion | flops 5242880 | bytes 6356992 | tf_op jit(solution)/shard_map/reduce_sum | solution.py:188
  62.1 8.3 %concatenate.3 = bf16[16,2,144,256]{3,2,1,0:T(8,128)(2,1)S(1)} concatenate(bf16[16,2,128,256]{3,2,1,0:T(8,128)(2,1)} %multiply_reduce_fusion, bf16[16,2,1,256]{3,2,1,0:T(2,128)(2,1)S(1)} %copy.149, bf16[16,2,1,256]{3,2,1,0:T(2,128)(2,1)S(1)} %reduce_sum.72, bf16[16,2,1,256]{3,2,1,0:T(2,128)(2,1)S(1)} %subtract_convert_fusion, bf16[16,2,13,256]{3,2,1,0:T(8,128)(2,1)S(1)} %broadcast_in_dim.22), dimensions={2} | concatenate | bytes 4718592 | tf_op jit(solution)/shard_map/concatenate | solution.py:192
  70.5 0.0 copy-start.2
  70.5 3.5 %copy.150 = bf16[16,2,144,256]{3,1,2,0:T(2,128)(2,1)} copy(bf16[16,2,144,256]{3,2,1,0:T(8,128)(2,1)S(1)} %concatenate.3) | data formatting | bytes 4718592 | tf_op jit(solution)/shard_map/concatenate | solution.py:192
  74.0 7.1 %all-to-all-start.1 = ((bf16[16,2,144,256]{3,1,2,0:T(2,128)(2,1)}), bf16[16,2,144,256]{3,1,2,0:T(2,128)(2,1)S(1)}, u32[]{:S(2)}, u32[]{:S(2)}) async-start(bf16[16,2,144,256]{3,1,2,0:T(2,128)(2,1)} %copy.150), calls=%async_computation.1 | async-start | bytes 4718592 | tf_op jit(solution)/shard_map/all_to_all | solution.py:202
  81.2 0.2 all-gather.2.cloned.1.call-start
  81.4 0.0 copy-done.2
  81.5 0.5 convolution_minimum_fusion.4
  82.0 0.4 convolution_minimum_fusion.3
  82.4 0.4 convolution_minimum_fusion.2
  82.8 0.4 convolution_minimum_fusion.1
  83.1 0.4 convolution_minimum_fusion
  83.5 0.4 fusion.50
  84.0 0.8 constant_dynamic-slice_fusion
  84.8 0.9 constant_dynamic-slice_fusion.1
  85.7 0.3 fusion.49
  86.0 0.2 fusion.12
  86.3 0.1 squeeze_reshape.11
  86.4 0.1 squeeze_reshape.9
  86.5 0.3 convolution_bitcast_fusion
  86.7 28.1 %all-to-all-done.1 = bf16[16,2,144,256]{3,1,2,0:T(2,128)(2,1)S(1)} async-done(((bf16[16,2,144,256]{3,1,2,0:T(2,128)(2,1)}), bf16[16,2,144,256]{3,1,2,0:T(2,128)(2,1)S(1)}, u32[]{:S(2)}, u32[]{:S(2)}) %all-to-all-start.1) | async-done | bytes 2359328 | tf_op jit(solution)/shard_map/all_to_all | solution.py:202
  114.9 0.1 reshape.216
  115.0 0.1 fusion.38
  115.1 0.1 reshape.207
  115.2 0.1 reshape.208
  115.3 0.1 reshape.212
  115.4 1.5 slice.36
  116.9 0.4 multiply_reduce_fusion.1
  117.3 0.1 copy.154
  117.5 0.9 fusion.9
  118.5 0.0 all-gather.2.cloned.1.call-update
  118.5 45.4 %all-gather.2.cloned.1.call-done = bf16[16,16,32,128]{3,2,1,0:T(8,128)(2,1)} async-done(((bf16[1,16,32,128]{3,2,1,0:T(8,128)(2,1)}), bf16[16,16,32,128]{3,2,1,0:T(8,128)(2,1)}) %all-gather.2.cloned.1.call-update) | async-done | bytes 2097168 | tf_op jit(solution)/shard_map/all_gather | solution.py:232
  163.8 0.0 collective-permute-start
  163.8 4.4 %collective-permute-done = bf16[16,16,32,128]{3,2,1,0:T(8,128)(2,1)S(1)} collective-permute-done((bf16[16,16,32,128]{3,2,1,0:T(8,128)(2,1)}, bf16[16,16,32,128]{3,2,1,0:T(8,128)(2,1)S(1)}, u32[]{:S(2)}, u32[]{:S(2)}) %collective-permute-start) | collective-permute-done | bytes 2097184 | tf_op jit(solution)/shard_map/ppermute | solution.py:233
  168.2 1.9 select_bitcast_fusion.1
  170.1 0.4 pad_maximum_fusion
  170.5 0.0 copy-start.3
  170.5 1.6 copy.166
  172.1 0.5 copy-done.3
  172.7 2.3 %fusion.2 = f32[4,2,64,512]{3,2,1,0:T(8,128)S(1)} fusion(bf16[4,2,64,128,32]{3,2,4,1,0:T(8,128)(2,1)S(1)} %bitcast.128, bf16[32,128,512]{2,1,0:T(8,128)(2,1)S(1)} %copy-done.3), kind=kOutput, calls=%fused_computation.7 | convolution fusion | flops 2147483648 | bytes 9437184 | tf_op jit(solution)/shard_map/rthd,hde->rte/dot_general | solution.py:239
  175.0 19.6 %all_to_all.16 = f32[4,2,64,512]{3,2,1,0:T(8,128)S(1)} all-to-all(f32[4,2,64,512]{3,2,1,0:T(8,128)S(1)} %fusion.2), channel_id=1, replica_groups=mesh['heads'=4,'sx'=4,'sy'=4,'sc'=2] {'heads'}, dimensions={0} | all-to-all | bytes 2097152 | tf_op jit(solution)/shard_map/all_to_all | solution.py:241
  194.6 0.8 reduce_sum.62
  (17 shorter events, 0.3 us)
Async XLA Ops:
  6.5 6.2 %copy-start = (bf16[6,128,2,128]{3,2,1,0:T(2,128)(2,1)S(1)}, bf16[6,128,2,128]{3,2,1,0:T(2,128)(2,1)}, u32[]{:S(2)}) copy-start(bf16[6,128,2,128]{3,2,1,0:T(2,128)(2,1)} %param.12) | copy-start | bytes 1179652
  6.5 7.0 %copy-start.1 = (bf16[6,128,2,128]{3,2,1,0:T(2,128)(2,1)S(1)}, bf16[6,128,2,128]{3,2,1,0:T(2,128)(2,1)}, u32[]{:S(2)}) copy-start(bf16[6,128,2,128]{3,2,1,0:T(2,128)(2,1)} %param.13) | copy-start | bytes 1179652
  6.5 8.0 %copy-start.4 = (s32[8]{0:T(128)S(1)}, s32[8]{0:T(128)}, u32[]{:S(2)}) copy-start(s32[8]{0:T(128)} %param.17) | copy-start | bytes 100
  70.5 11.0 %copy-start.2 = (s32[8,64]{1,0:T(8,128)S(1)}, s32[8,64]{1,0:T(8,128)}, u32[]{:S(2)}) copy-start(s32[8,64]{1,0:T(8,128)} %param.20) | copy-start | bytes 6148
  74.0 40.9 %all-to-all-start.1 = ((bf16[16,2,144,256]{3,1,2,0:T(2,128)(2,1)}), bf16[16,2,144,256]{3,1,2,0:T(2,128)(2,1)S(1)}, u32[]{:S(2)}, u32[]{:S(2)}) async-start(bf16[16,2,144,256]{3,1,2,0:T(2,128)(2,1)} %copy.150), calls=%async_computation.1 | async-start | bytes 4718592 | tf_op jit(solution)/shard_map/all_to_all | solution.py:202
  81.2 82.7 %all-gather.2.cloned.1.call-start = ((), (), s32[]{:S(2)}) async-start(), calls=%async_computation.3 | async-start | bytes 2228224 | tf_op jit(solution)/shard_map/all_gather | solution.py:232
  163.8 4.4 %collective-permute-start = (bf16[16,16,32,128]{3,2,1,0:T(8,128)(2,1)}, bf16[16,16,32,128]{3,2,1,0:T(8,128)(2,1)S(1)}, u32[]{:S(2)}, u32[]{:S(2)}) collective-permute-start(bf16[16,16,32,128]{3,2,1,0:T(8,128)(2,1)} %all-gather.2.cloned.1.call-done), channel_id=1, source_target_pairs={{0,1},{1,0},{2,3},{3,2},{4,5},{5,4},{6,7},{7,6},{8,9},{9,8},{10,11... | collective-permute-start | bytes 6291464 | tf_op jit(solution)/shard_map/ppermute | solution.py:233
  170.5 2.2 %copy-start.3 = (bf16[32,128,512]{2,1,0:T(8,128)(2,1)S(1)}, bf16[32,128,512]{2,1,0:T(8,128)(2,1)}, u32[]{:S(2)}) copy-start(bf16[32,128,512]{2,1,0:T(8,128)(2,1)} %param.21) | copy-start | bytes 12582916
Sparse Core Ops, SparseCore 0:
  118.6 45.1 all-gather.1

commit v5 on v4

--- a/solution.py
+++ b/solution.py
@@ -229,7 +229,9 @@
         (top_all, summed_totals, summed_weighted), draft
     )
     attention = (final_weighted / final_totals[..., None]).astype(jnp.bfloat16)
-    attention = lax.all_gather(attention, ("sx", "sy"), axis=0, tiled=False)
+    peers = seq_size // pair
+    attention = jnp.broadcast_to(attention[None], (peers,) + attention.shape)
+    attention = lax.all_to_all(attention, ("sx", "sy"), 0, 0, tiled=True)
     other = lax.ppermute(attention, "sc", [(i, (i + 1) % pair) for i in range(pair)])
     first = jnp.where(core == 0, attention, other)
     second = jnp.where(core == 0, other, attention)

time: 203 us -> 177 us (0.87)
  waiting for transfers between devices: 77.9 us -> 32.6 us
  blocking collectives: 27.1 us -> 60.4 us
  between operations: 13.7 us -> 0.35 us
    all_gather x1 -> x0, waiting for transfers between devices: 45.4 us -> none  [local(): attention = lax.all_gather(attention, ('sx', 'sy'), axis=0, tiled=False)]
    all_to_all x0 -> x1, blocking collectives: none -> 32.4 us  [local(): attention = lax.all_to_all(attention, ('sx', 'sy'), 0, 0, tiled=True)]
  transfers between devices with their start and end apart: 3 -> 2, of which waited for: 3 -> 2; matrix products, arithmetic and copies ran while one was open for 3% -> 3% of each run, Pallas kernels for 0% -> 0%
where the time goes in v5:
time: 177 us; the launch traced here: 176 us
  blocking collectives  60.4 us (34%)
  Pallas kernels  33.5 us (19%)
  waiting for transfers between devices  32.6 us (18%)
  local copies, waits for them, and re-layouts  29.1 us (16%)
  other arithmetic  7.93 us (4%)
  starting transfers between devices  7.17 us (4%)
  matrix products  5.29 us (3%)
    pallas_call x1, Pallas kernels, context_part(): pl.pallas_call(context_kernel, grid_spec=grid_spec, out_shape=jax.ShapeDt...  33.5 us
    all_to_all x1, blocking collectives, local(): attention = lax.all_to_all(attention, ('sx', 'sy'), 0, 0, tiled=True)  32.4 us
    all_to_all x1, waiting for transfers between devices, local(): got = lax.all_to_all(sent, ('sx', 'sy'), 0, 0, tiled=True)  28.4 us
    all_to_all x1, blocking collectives, local(): return jnp.sum(lax.all_to_all(partial, 'heads', 0, 0, tiled=True), axis=0)  20.5 us
    concatenate x2, local copies, waits for them, and re-layouts, local(): jnp.concatenate([pair_weighted.astype(jnp.bfloat16), pair_top.astype(jnp....  11.8 us
    unnamed x13, local copies, waits for them, and re-layouts  7.54 us
    all_to_all x1, blocking collectives, local(): parts = lax.all_to_all(parts, 'sc', 1, 1, tiled=True)  7.52 us
    all_to_all x1, starting transfers between devices, local(): got = lax.all_to_all(sent, ('sx', 'sy'), 0, 0, tiled=True)  7.16 us
  transfers between devices with their start and end apart: 2, of which 2 were waited for; matrix products, arithmetic and copies ran while one was open for 3% of the time, Pallas kernels for 0%

profile of v5, /device:TPU:0, one launch (start us, length us, event | category | flops | bytes accessed | tf_op | source)
XLA Modules:
  0.0 176.5 jit_solution(5224543562097162091)
XLA Ops:
  0.0 0.0 copy-start
  0.0 0.0 copy-start.1
  0.0 0.0 copy-start.4
  0.0 2.5 %copy.199 = bf16[8,256,2,128]{3,1,2,0:T(8,128)(2,1)} copy(bf16[8,256,2,128]{3,2,1,0:T(2,128)(2,1)} %param.15) | data formatting | bytes 2097152 | tf_op args[4]
  2.5 3.6 %copy.146 = bf16[8,256,2,128]{1,3,2,0:T(8,128)(2,1)} copy(bf16[8,256,2,128]{3,2,1,0:T(2,128)(2,1)} %param.16) | data formatting | bytes 2097152 | tf_op args[5]
  6.2 0.0 copy-done
  6.2 0.8 copy.142
  7.0 0.0 copy-done.1
  7.0 1.0 copy.144
  8.0 0.0 copy-done.4
  8.0 0.5 subtract_clamp_fusion.len_ref
  8.5 33.5 %shard_map.109 = bf16[8,4,2,144,256]{4,3,2,1,0:T(8,128)(2,1)} custom-call(s32[8,6]{1,0:T(8,128)} %use_ref.1, s32[8]{0:T(128)} %subtract_clamp_fusion.len_ref, bf16[8,64,32,128]{3,2,1,0:T(8,128)(2,1)} %q_ref.1, bf16[2,768,128]{2,1,0:T(8,128)(2,1)} %bitcast.131, bf16[2,128,768]{2,1,0:T(8,128)(2,1)} %bitcast.132, bf16[8,2,256,128]{3,2,1,0:T(8,128)(2,1)} %bitcast.129, ...), custom_call_target="tpu_custom_call" | custom-call | tf_op jit(solution)/shard_map/pallas_call | solution.py:130
  42.0 2.6 %copy.147 = bf16[16,2,2,144,256]{4,3,2,0,1:T(8,128)(2,1)S(1)} copy(bf16[16,2,2,144,256]{4,3,2,1,0:T(8,128)(2,1)} %bitcast.125) | data formatting | bytes 9437184 | tf_op jit(solution)/shard_map/reshape | solution.py:182
  44.7 7.5 %all_to_all.20 = bf16[16,2,2,144,256]{4,3,2,0,1:T(8,128)(2,1)S(1)} all-to-all(bf16[16,2,2,144,256]{4,3,2,0,1:T(8,128)(2,1)S(1)} %copy.147), channel_id=1, replica_groups=mesh['heads'=4,'sx'=4,'sy'=4,'sc'=2] {'sc'}, dimensions={1} | all-to-all | bytes 9437184 | tf_op jit(solution)/shard_map/all_to_all | solution.py:183
  52.2 0.1 fusion.48
  52.4 0.1 fusion.28
  52.5 0.1 fusion.27
  52.6 0.1 fusion.23
  52.7 2.8 %multiply_reduce_fusion = bf16[16,2,128,256]{3,2,1,0:T(8,128)(2,1)} fusion(bf16[16,2,2,144,256]{4,3,2,0,1:T(8,128)(2,1)S(1)} %all_to_all.20, f32[16,2,2,256]{3,2,0,1:T(2,128)S(1)} %fusion.23), kind=kLoop, calls=%fused_computation | loop fusion | flops 5242880 | bytes 6356992 | tf_op jit(solution)/shard_map/reduce_sum | solution.py:188
  55.6 8.3 %concatenate.3 = bf16[16,2,144,256]{3,2,1,0:T(8,128)(2,1)S(1)} concatenate(bf16[16,2,128,256]{3,2,1,0:T(8,128)(2,1)} %multiply_reduce_fusion, bf16[16,2,1,256]{3,2,1,0:T(2,128)(2,1)S(1)} %copy.149, bf16[16,2,1,256]{3,2,1,0:T(2,128)(2,1)S(1)} %reduce_sum.72, bf16[16,2,1,256]{3,2,1,0:T(2,128)(2,1)S(1)} %subtract_convert_fusion, bf16[16,2,13,256]{3,2,1,0:T(8,128)(2,1)S(1)} %broadcast_in_dim.24), dimensions={2} | concatenate | bytes 4718592 | tf_op jit(solution)/shard_map/concatenate | solution.py:192
  63.9 0.0 copy-start.2
  63.9 3.5 %copy.150 = bf16[16,2,144,256]{3,1,2,0:T(2,128)(2,1)} copy(bf16[16,2,144,256]{3,2,1,0:T(8,128)(2,1)S(1)} %concatenate.3) | data formatting | bytes 4718592 | tf_op jit(solution)/shard_map/concatenate | solution.py:192
  67.5 7.2 %all-to-all-start.1 = ((bf16[16,2,144,256]{3,1,2,0:T(2,128)(2,1)}), bf16[16,2,144,256]{3,1,2,0:T(2,128)(2,1)S(1)}, u32[]{:S(2)}, u32[]{:S(2)}) async-start(bf16[16,2,144,256]{3,1,2,0:T(2,128)(2,1)} %copy.150), calls=%async_computation.1 | async-start | bytes 4718592 | tf_op jit(solution)/shard_map/all_to_all | solution.py:202
  74.7 0.0 copy-done.2
  74.7 0.5 convolution_minimum_fusion.4
  75.2 0.4 convolution_minimum_fusion.3
  75.6 0.4 convolution_minimum_fusion.2
  76.0 0.4 convolution_minimum_fusion.1
  76.4 0.4 convolution_minimum_fusion
  76.8 0.4 fusion.50
  77.2 0.8 constant_dynamic-slice_fusion
  78.0 0.9 constant_dynamic-slice_fusion.1
  79.0 0.3 fusion.49
  79.3 0.2 fusion.12
  79.6 0.1 squeeze_reshape.11
  79.6 0.1 squeeze_reshape.9
  79.7 0.3 convolution_bitcast_fusion
  80.0 28.4 %all-to-all-done.1 = bf16[16,2,144,256]{3,1,2,0:T(2,128)(2,1)S(1)} async-done(((bf16[16,2,144,256]{3,1,2,0:T(2,128)(2,1)}), bf16[16,2,144,256]{3,1,2,0:T(2,128)(2,1)S(1)}, u32[]{:S(2)}, u32[]{:S(2)}) %all-to-all-start.1) | async-done | bytes 2359328 | tf_op jit(solution)/shard_map/all_to_all | solution.py:202
  108.4 0.1 reshape.200
  108.5 0.1 fusion.38
  108.5 0.1 reshape.191
  108.6 0.1 reshape.192
  108.7 0.1 reshape.196
  108.8 1.5 slice.36
  110.4 0.4 multiply_reduce_fusion.1
  110.8 0.1 copy.154
  111.0 0.3 fusion.9
  111.3 0.4 broadcast_in_dim.29
  111.7 32.4 %all_to_all.21 = bf16[16,16,32,128]{3,2,1,0:T(8,128)(2,1)S(1)} all-to-all(bf16[16,16,32,128]{3,2,1,0:T(8,128)(2,1)S(1)} %broadcast_in_dim.29), channel_id=1, replica_groups=mesh['heads'=4,'sx'=4,'sy'=4,'sc'=2] {'sx','sy'}, dimensions={0} | all-to-all | bytes 4194304 | tf_op jit(solution)/shard_map/all_to_all | solution.py:234
  144.1 0.0 collective-permute-start
  144.1 4.3 %collective-permute-done = bf16[16,16,32,128]{3,2,1,0:T(8,128)(2,1)} collective-permute-done((bf16[16,16,32,128]{3,2,1,0:T(8,128)(2,1)S(1)}, bf16[16,16,32,128]{3,2,1,0:T(8,128)(2,1)}, u32[]{:S(2)}, u32[]{:S(2)}) %collective-permute-start) | collective-permute-done | bytes 2097184 | tf_op jit(solution)/shard_map/ppermute | solution.py:235
  148.4 1.9 %select_bitcast_fusion.1 = (bf16[16,1,16,32,128]{4,3,2,1,0:T(8,128)(2,1)S(1)}, bf16[16,1,16,32,128]{4,3,2,1,0:T(8,128)(2,1)S(1)}) fusion(bf16[16,16,32,128]{3,2,1,0:T(8,128)(2,1)S(1)} %all_to_all.21, bf16[16,16,32,128]{3,2,1,0:T(8,128)(2,1)} %collective-permute-done, pred[]{:T(512)S(6)} %eq.36), kind=kLoop, calls=%fused_computation.6 | loop fusion | flops 2097152 | bytes 8388609 | tf_op jit(solution)/shard_map/stack | solution.py:238
  150.3 0.4 pad_maximum_fusion
  150.7 0.0 copy-start.3
  150.7 1.6 copy.166
  152.3 0.5 copy-done.3
  152.8 2.3 %fusion.2 = f32[4,2,64,512]{3,2,1,0:T(8,128)S(1)} fusion(bf16[4,2,64,128,32]{3,2,4,1,0:T(8,128)(2,1)S(1)} %bitcast.128, bf16[32,128,512]{2,1,0:T(8,128)(2,1)S(1)} %copy-done.3), kind=kOutput, calls=%fused_computation.7 | convolution fusion | flops 2147483648 | bytes 9437184 | tf_op jit(solution)/shard_map/rthd,hde->rte/dot_general | solution.py:241
  155.2 20.5 %all_to_all.22 = f32[4,2,64,512]{3,2,1,0:T(8,128)S(1)} all-to-all(f32[4,2,64,512]{3,2,1,0:T(8,128)S(1)} %fusion.2), channel_id=1, replica_groups=mesh['heads'=4,'sx'=4,'sy'=4,'sc'=2] {'heads'}, dimensions={0} | all-to-all | bytes 2097152 | tf_op jit(solution)/shard_map/all_to_all | solution.py:243
  175.7 0.8 reduce_sum.62
  (17 shorter events, 0.3 us)
Async XLA Ops:
  0.0 6.2 %copy-start = (bf16[6,128,2,128]{3,2,1,0:T(2,128)(2,1)S(1)}, bf16[6,128,2,128]{3,2,1,0:T(2,128)(2,1)}, u32[]{:S(2)}) copy-start(bf16[6,128,2,128]{3,2,1,0:T(2,128)(2,1)} %param.12) | copy-start | bytes 1179652
  0.0 7.0 %copy-start.1 = (bf16[6,128,2,128]{3,2,1,0:T(2,128)(2,1)S(1)}, bf16[6,128,2,128]{3,2,1,0:T(2,128)(2,1)}, u32[]{:S(2)}) copy-start(bf16[6,128,2,128]{3,2,1,0:T(2,128)(2,1)} %param.13) | copy-start | bytes 1179652
  0.0 8.0 %copy-start.4 = (s32[8]{0:T(128)S(1)}, s32[8]{0:T(128)}, u32[]{:S(2)}) copy-start(s32[8]{0:T(128)} %param.17) | copy-start | bytes 100
  63.9 10.8 %copy-start.2 = (s32[8,64]{1,0:T(8,128)S(1)}, s32[8,64]{1,0:T(8,128)}, u32[]{:S(2)}) copy-start(s32[8,64]{1,0:T(8,128)} %param.20) | copy-start | bytes 6148
  67.5 40.9 %all-to-all-start.1 = ((bf16[16,2,144,256]{3,1,2,0:T(2,128)(2,1)}), bf16[16,2,144,256]{3,1,2,0:T(2,128)(2,1)S(1)}, u32[]{:S(2)}, u32[]{:S(2)}) async-start(bf16[16,2,144,256]{3,1,2,0:T(2,128)(2,1)} %copy.150), calls=%async_computation.1 | async-start | bytes 4718592 | tf_op jit(solution)/shard_map/all_to_all | solution.py:202
  144.1 4.3 %collective-permute-start = (bf16[16,16,32,128]{3,2,1,0:T(8,128)(2,1)S(1)}, bf16[16,16,32,128]{3,2,1,0:T(8,128)(2,1)}, u32[]{:S(2)}, u32[]{:S(2)}) collective-permute-start(bf16[16,16,32,128]{3,2,1,0:T(8,128)(2,1)S(1)} %all_to_all.21), channel_id=1, source_target_pairs={{0,1},{1,0},{2,3},{3,2},{4,5},{5,4},{6,7},{7,6},{8,9},{9,8},{10,11... | collective-permute-start | bytes 6291464 | tf_op jit(solution)/shard_map/ppermute | solution.py:235
  150.7 2.2 %copy-start.3 = (bf16[32,128,512]{2,1,0:T(8,128)(2,1)S(1)}, bf16[32,128,512]{2,1,0:T(8,128)(2,1)}, u32[]{:S(2)}) copy-start(bf16[32,128,512]{2,1,0:T(8,128)(2,1)} %param.21) | copy-start | bytes 12582916

commit v6 on v5

--- a/solution.py
+++ b/solution.py
@@ -89,19 +89,25 @@
         vo_ref[0, 0], w_own.astype(jnp.bfloat16), preferred_element_type=jnp.float32
     )
     head_dim = acc.shape[0]
-    pieces = acc_ref.shape[1]
+    pieces = acc_ref.shape[0] * acc_ref.shape[2]
     width = acc_ref.shape[-1]
-    extra = acc_ref.shape[3] - head_dim
+    extra = acc_ref.shape[-2] - head_dim
     high = totals.astype(jnp.bfloat16).astype(jnp.float32)
     low = totals - high
     row_id = lax.broadcasted_iota(jnp.int32, (extra, totals.shape[1]), 0)
     stats = jnp.where(row_id == 0, top, jnp.where(row_id == 1, high, jnp.where(row_id == 2, low, 0.0)))
+    pair = acc_ref.shape[0]
     for c in range(pieces):
-        acc_ref[0, c, 0, 0:head_dim, :] = acc[:, c * width : (c + 1) * width].astype(acc_ref.dtype)
-        acc_ref[0, c, 0, head_dim:, :] = stats[:, c * width : (c + 1) * width].astype(acc_ref.dtype)
-
-
-def context_part(queries, prefix_keys, prefix_values, use_rows, own_lengths, own_keys, own_values, pieces):
+        spot = (c % pair, 0, c // pair, 0)
+        acc_ref[spot + (slice(0, head_dim),)] = acc[:, c * width : (c + 1) * width].astype(
+            acc_ref.dtype
+        )
+        acc_ref[spot + (slice(head_dim, None),)] = stats[:, c * width : (c + 1) * width].astype(
+            acc_ref.dtype
+        )
+
+
+def context_part(queries, prefix_keys, prefix_values, use_rows, own_lengths, own_keys, own_values, pieces, pair):
     requests, tree_size, heads_dev, head_dim = queries.shape
     block_count, block_len, kv_dev, _ = prefix_keys.shape
     group_size = heads_dev // kv_dev
@@ -124,14 +130,15 @@
             pl.BlockSpec((1, 1, head_dim, private_dev), lambda k, r, u, n: (r, k, 0, 0)),
         ],
         out_specs=pl.BlockSpec(
-            (1, pieces, 1, head_dim + 16, width), lambda k, r, u, n: (r, 0, k, 0, 0)
+            (pair, 1, pieces // pair, 1, head_dim + 16, width),
+            lambda k, r, u, n: (0, r, 0, k, 0, 0),
         ),
     )
     return pl.pallas_call(
         context_kernel,
         grid_spec=grid_spec,
         out_shape=jax.ShapeDtypeStruct(
-            (requests, pieces, kv_dev, head_dim + 16, width), jnp.bfloat16
+            (pair, requests, pieces // pair, kv_dev, head_dim + 16, width), jnp.bfloat16
         ),
     )(use_rows, own_lengths, queries, kp, vp, ko, vo)
 
@@ -172,33 +179,32 @@
     row_count = requests * tree_size
     chunk = row_count // seq_size
     pieces = tree_size // chunk
+    pair = lax.axis_size("sc")
+    core = lax.axis_index("sc")
     own_lengths = jnp.clip(private_lengths - shard_index * private_dev, 0, private_dev)
     acc = context_part(
-        queries, prefix_keys, prefix_values, block_use, own_lengths, private_keys, private_values, pieces
+        queries, prefix_keys, prefix_values, block_use, own_lengths, private_keys, private_values, pieces, pair
     )
     width = chunk * group_size
-    pair = lax.axis_size("sc")
-    core = lax.axis_index("sc")
-    parts = acc.reshape(seq_size // pair, pair, kv_dev, head_dim + 16, width)
-    parts = lax.all_to_all(parts, "sc", 1, 1, tiled=True)
-    part_top, part_totals, part_weighted = unpack(parts, head_dim, 1)
-    pair_top = jnp.max(part_top, axis=1)
-    factor = jnp.exp(part_top - pair_top[:, None])
-    pair_totals = jnp.sum(part_totals * factor, axis=1)
-    pair_weighted = jnp.sum(part_weighted * factor[:, :, :, None, :], axis=1)
-    high = pair_totals.astype(jnp.bfloat16)
-    low = (pair_totals - high.astype(jnp.float32)).astype(jnp.bfloat16)
-    zeros = jnp.zeros(pair_top.shape[:2] + (13,) + pair_top.shape[2:], jnp.bfloat16)
-    sent = jnp.concatenate(
-        [
-            pair_weighted.astype(jnp.bfloat16),
-            pair_top.astype(jnp.bfloat16)[:, :, None],
-            high[:, :, None],
-            low[:, :, None],
-            zeros,
-        ],
-        axis=2,
-    )
+    parts = acc.reshape(pair, seq_size // pair, kv_dev, head_dim + 16, width)
+    parts = lax.all_to_all(parts, "sc", 0, 0, tiled=True).astype(jnp.float32)
+    part_top = parts[:, :, :, head_dim : head_dim + 1]
+    pair_top = jnp.max(part_top, axis=0)
+    factor = jnp.exp(part_top - pair_top[None])
+    scaled = jnp.sum(parts * factor, axis=0)
+    pair_totals = scaled[:, :, head_dim + 1 : head_dim + 2] + scaled[:, :, head_dim + 2 : head_dim + 3]
+    high = pair_totals.astype(jnp.bfloat16).astype(jnp.float32)
+    low = pair_totals - high
+    row = lax.broadcasted_iota(jnp.int32, scaled.shape, 2)
+    sent = jnp.where(
+        row < head_dim,
+        scaled,
+        jnp.where(
+            row == head_dim,
+            pair_top,
+            jnp.where(row == head_dim + 1, high, jnp.where(row == head_dim + 2, low, 0.0)),
+        ),
+    ).astype(jnp.bfloat16)
     got = lax.all_to_all(sent, ("sx", "sy"), 0, 0, tiled=True)
     part_top, part_totals, part_weighted = unpack(got, head_dim, 0)
     top_all = jnp.max(part_top, axis=0)

time: 177 us -> 169 us (0.955)
  local copies, waits for them, and re-layouts: 29.1 us -> 18.2 us
    concatenate x2 -> x0, local copies, waits for them, and re-layouts: 11.8 us -> none  [local(): jnp.concatenate([pair_weighted.astype(jnp.bfloat16), pair_top.astype(jnp....]
    convert_element_type x0 -> x1, local copies, waits for them, and re-layouts: none -> 3.54 us  [local(): sent = jnp.where(row < head_dim, scaled, jnp.where(row == head_dim, pair_...]
    convert_element_type x1 -> x3, other arithmetic: 0.03 us -> 2.72 us  [the longest x1 1.41 us: local(): sent = jnp.where(row < head_dim, scaled, jnp.where(row == head_dim, pair_...]
    reshape x1 -> x0, local copies, waits for them, and re-layouts: 2.64 us -> none  [local(): parts = acc.reshape(seq_size // pair, pair, kv_dev, head_dim + 16, width)]
    unnamed x13 -> x15, local copies, waits for them, and re-layouts: 7.54 us -> 7.61 us
where the time goes in v6:
time: 169 us; the launch traced here: 168 us
  blocking collectives  61.9 us (37%)
  Pallas kernels  33.5 us (20%)
  waiting for transfers between devices  32.7 us (19%)
  local copies, waits for them, and re-layouts  18.2 us (11%)
  other arithmetic  9.05 us (5%)
  starting transfers between devices  7.16 us (4%)
  matrix products  5.29 us (3%)
    pallas_call x1, Pallas kernels, context_part(): pl.pallas_call(context_kernel, grid_spec=grid_spec, out_shape=jax.ShapeDt...  33.5 us
    all_to_all x1, blocking collectives, local(): attention = lax.all_to_all(attention, ('sx', 'sy'), 0, 0, tiled=True)  32.4 us
    all_to_all x1, waiting for transfers between devices, local(): got = lax.all_to_all(sent, ('sx', 'sy'), 0, 0, tiled=True)  28.4 us
    all_to_all x1, blocking collectives, local(): return jnp.sum(lax.all_to_all(partial, 'heads', 0, 0, tiled=True), axis=0)  20.5 us
    all_to_all x1, blocking collectives, local(): parts = lax.all_to_all(parts, 'sc', 0, 0, tiled=True).astype(jnp.float32)  8.93 us
    unnamed x15, local copies, waits for them, and re-layouts  7.61 us
    all_to_all x1, starting transfers between devices, local(): got = lax.all_to_all(sent, ('sx', 'sy'), 0, 0, tiled=True)  7.16 us
    ppermute x1, waiting for transfers between devices, local(): lax.ppermute(attention, 'sc', [(i, (i + 1) % pair) for i in range(pair)])  4.29 us
  transfers between devices with their start and end apart: 2, of which 2 were waited for; matrix products, arithmetic and copies ran while one was open for 3% of the time, Pallas kernels for 0%

profile of v6, /device:TPU:0, one launch (start us, length us, event | category | flops | bytes accessed | tf_op | source)
XLA Modules:
  0.0 168.1 jit_solution(7444059450707036658)
XLA Ops:
  0.0 0.0 copy-start
  0.0 0.0 copy-start.1
  0.0 0.0 copy-start.4
  0.0 2.5 %copy.178 = bf16[8,256,2,128]{3,1,2,0:T(8,128)(2,1)} copy(bf16[8,256,2,128]{3,2,1,0:T(2,128)(2,1)} %param.15) | data formatting | bytes 2097152 | tf_op args[4]
  2.5 3.6 %copy.128 = bf16[8,256,2,128]{1,3,2,0:T(8,128)(2,1)} copy(bf16[8,256,2,128]{3,2,1,0:T(2,128)(2,1)} %param.16) | data formatting | bytes 2097152 | tf_op args[5]
  6.2 0.0 copy-done
  6.2 0.8 copy.124
  7.0 0.0 copy-done.1
  7.0 1.0 copy.126
  8.0 0.0 copy-done.4
  8.0 0.5 subtract_clamp_fusion.len_ref
  8.5 33.5 %shard_map.109 = bf16[2,8,2,2,144,256]{5,4,3,2,1,0:T(8,128)(2,1)} custom-call(s32[8,6]{1,0:T(8,128)} %use_ref.1, s32[8]{0:T(128)} %subtract_clamp_fusion.len_ref, bf16[8,64,32,128]{3,2,1,0:T(8,128)(2,1)} %q_ref.1, bf16[2,768,128]{2,1,0:T(8,128)(2,1)} %bitcast.123, bf16[2,128,768]{2,1,0:T(8,128)(2,1)} %bitcast.124, bf16[8,2,256,128]{3,2,1,0:T(8,128)(2,1)} %bitcast.121, ...), custom_call_target="tpu_custom_call" | custom-call | tf_op jit(solution)/shard_map/pallas_call | solution.py:137
  42.1 8.9 %all_to_all.20 = bf16[2,16,2,144,256]{4,3,2,1,0:T(8,128)(2,1)S(1)} all-to-all(bf16[2,16,2,144,256]{4,3,2,1,0:T(8,128)(2,1)} %bitcast.117), channel_id=1, replica_groups=mesh['heads'=4,'sx'=4,'sy'=4,'sc'=2] {'sc'}, dimensions={0} | all-to-all | bytes 9437184 | tf_op jit(solution)/shard_map/all_to_all | solution.py:190
  51.0 1.3 convert_element_type.52
  52.3 0.1 slice_reduce_fusion
  52.4 0.1 subtract_exponential_fusion
  52.6 1.4 multiply_reduce_fusion
  53.9 0.1 convert_convert_fusion
  54.0 0.1 fusion.33
  54.1 1.4 select_convert_fusion
  55.6 0.0 copy-start.2
  55.6 3.5 %copy.129 = bf16[16,2,144,256]{3,1,2,0:T(2,128)(2,1)} copy(bf16[16,2,144,256]{3,2,1,0:T(8,128)(2,1)S(1)} %select_convert_fusion) | data formatting | bytes 4718592 | tf_op jit(solution)/shard_map/convert_element_type | solution.py:207
  59.1 7.2 %all-to-all-start.1 = ((bf16[16,2,144,256]{3,1,2,0:T(2,128)(2,1)}), bf16[16,2,144,256]{3,1,2,0:T(2,128)(2,1)S(1)}, u32[]{:S(2)}, u32[]{:S(2)}) async-start(bf16[16,2,144,256]{3,1,2,0:T(2,128)(2,1)} %copy.129), calls=%async_computation.1 | async-start | bytes 4718592 | tf_op jit(solution)/shard_map/all_to_all | solution.py:208
  66.3 0.0 copy-done.2
  66.3 0.5 convolution_minimum_fusion.4
  66.9 0.4 convolution_minimum_fusion.3
  67.3 0.4 convolution_minimum_fusion.2
  67.6 0.4 convolution_minimum_fusion.1
  68.0 0.4 convolution_minimum_fusion
  68.4 0.4 fusion.43
  68.8 0.8 constant_dynamic-slice_fusion
  69.7 0.9 constant_dynamic-slice_fusion.1
  70.6 0.3 fusion.42
  70.9 0.2 fusion.12
  71.2 0.1 squeeze_reshape.11
  71.3 0.1 squeeze_reshape.9
  71.3 0.3 convolution_bitcast_fusion
  71.6 28.4 %all-to-all-done.1 = bf16[16,2,144,256]{3,1,2,0:T(2,128)(2,1)S(1)} async-done(((bf16[16,2,144,256]{3,1,2,0:T(2,128)(2,1)}), bf16[16,2,144,256]{3,1,2,0:T(2,128)(2,1)S(1)}, u32[]{:S(2)}, u32[]{:S(2)}) %all-to-all-start.1) | async-done | bytes 2359328 | tf_op jit(solution)/shard_map/all_to_all | solution.py:208
  100.0 0.1 reshape.176
  100.1 0.1 fusion.31
  100.2 0.1 reshape.168
  100.3 0.1 reshape.169
  100.4 0.1 reshape.172
  100.5 1.5 slice.31
  102.0 0.4 multiply_reduce_fusion.1
  102.5 0.1 copy.133
  102.6 0.3 fusion.9
  102.9 0.4 broadcast_in_dim.78
  103.3 32.4 %all_to_all.21 = bf16[16,16,32,128]{3,2,1,0:T(8,128)(2,1)S(1)} all-to-all(bf16[16,16,32,128]{3,2,1,0:T(8,128)(2,1)S(1)} %broadcast_in_dim.78), channel_id=1, replica_groups=mesh['heads'=4,'sx'=4,'sy'=4,'sc'=2] {'sx','sy'}, dimensions={0} | all-to-all | bytes 4194304 | tf_op jit(solution)/shard_map/all_to_all | solution.py:240
  135.7 0.0 collective-permute-start
  135.7 4.3 %collective-permute-done = bf16[16,16,32,128]{3,2,1,0:T(8,128)(2,1)} collective-permute-done((bf16[16,16,32,128]{3,2,1,0:T(8,128)(2,1)S(1)}, bf16[16,16,32,128]{3,2,1,0:T(8,128)(2,1)}, u32[]{:S(2)}, u32[]{:S(2)}) %collective-permute-start) | collective-permute-done | bytes 2097184 | tf_op jit(solution)/shard_map/ppermute | solution.py:241
  140.0 1.9 %select_bitcast_fusion.1 = (bf16[16,1,16,32,128]{4,3,2,1,0:T(8,128)(2,1)S(1)}, bf16[16,1,16,32,128]{4,3,2,1,0:T(8,128)(2,1)S(1)}) fusion(bf16[16,16,32,128]{3,2,1,0:T(8,128)(2,1)S(1)} %all_to_all.21, bf16[16,16,32,128]{3,2,1,0:T(8,128)(2,1)} %collective-permute-done, pred[]{:T(512)S(6)} %eq.54), kind=kLoop, calls=%fused_computation.7 | loop fusion | flops 2097152 | bytes 8388609 | tf_op jit(solution)/shard_map/stack | solution.py:244
  141.9 0.4 pad_maximum_fusion
  142.3 0.0 copy-start.3
  142.3 1.6 copy.145
  143.9 0.5 copy-done.3
  144.5 2.3 %fusion.2 = f32[4,2,64,512]{3,2,1,0:T(8,128)S(1)} fusion(bf16[4,2,64,128,32]{3,2,4,1,0:T(8,128)(2,1)S(1)} %bitcast.120, bf16[32,128,512]{2,1,0:T(8,128)(2,1)S(1)} %copy-done.3), kind=kOutput, calls=%fused_computation.8 | convolution fusion | flops 2147483648 | bytes 9437184 | tf_op jit(solution)/shard_map/rthd,hde->rte/dot_general | solution.py:247
  146.8 20.5 %all_to_all.22 = f32[4,2,64,512]{3,2,1,0:T(8,128)S(1)} all-to-all(f32[4,2,64,512]{3,2,1,0:T(8,128)S(1)} %fusion.2), channel_id=1, replica_groups=mesh['heads'=4,'sx'=4,'sy'=4,'sc'=2] {'heads'}, dimensions={0} | all-to-all | bytes 2097152 | tf_op jit(solution)/shard_map/all_to_all | solution.py:249
  167.3 0.8 reduce_sum.49
  (16 shorter events, 0.3 us)
Async XLA Ops:
  0.0 6.2 %copy-start = (bf16[6,128,2,128]{3,2,1,0:T(2,128)(2,1)S(1)}, bf16[6,128,2,128]{3,2,1,0:T(2,128)(2,1)}, u32[]{:S(2)}) copy-start(bf16[6,128,2,128]{3,2,1,0:T(2,128)(2,1)} %param.12) | copy-start | bytes 1179652
  0.0 7.0 %copy-start.1 = (bf16[6,128,2,128]{3,2,1,0:T(2,128)(2,1)S(1)}, bf16[6,128,2,128]{3,2,1,0:T(2,128)(2,1)}, u32[]{:S(2)}) copy-start(bf16[6,128,2,128]{3,2,1,0:T(2,128)(2,1)} %param.13) | copy-start | bytes 1179652
  0.0 8.0 %copy-start.4 = (s32[8]{0:T(128)S(1)}, s32[8]{0:T(128)}, u32[]{:S(2)}) copy-start(s32[8]{0:T(128)} %param.17) | copy-start | bytes 100
  55.6 10.8 %copy-start.2 = (s32[8,64]{1,0:T(8,128)S(1)}, s32[8,64]{1,0:T(8,128)}, u32[]{:S(2)}) copy-start(s32[8,64]{1,0:T(8,128)} %param.20) | copy-start | bytes 6148
  59.1 40.9 %all-to-all-start.1 = ((bf16[16,2,144,256]{3,1,2,0:T(2,128)(2,1)}), bf16[16,2,144,256]{3,1,2,0:T(2,128)(2,1)S(1)}, u32[]{:S(2)}, u32[]{:S(2)}) async-start(bf16[16,2,144,256]{3,1,2,0:T(2,128)(2,1)} %copy.129), calls=%async_computation.1 | async-start | bytes 4718592 | tf_op jit(solution)/shard_map/all_to_all | solution.py:208
  135.7 4.3 %collective-permute-start = (bf16[16,16,32,128]{3,2,1,0:T(8,128)(2,1)S(1)}, bf16[16,16,32,128]{3,2,1,0:T(8,128)(2,1)}, u32[]{:S(2)}, u32[]{:S(2)}) collective-permute-start(bf16[16,16,32,128]{3,2,1,0:T(8,128)(2,1)S(1)} %all_to_all.21), channel_id=1, source_target_pairs={{0,1},{1,0},{2,3},{3,2},{4,5},{5,4},{6,7},{7,6},{8,9},{9,8},{10,11... | collective-permute-start | bytes 6291464 | tf_op jit(solution)/shard_map/ppermute | solution.py:241
  142.3 2.2 %copy-start.3 = (bf16[32,128,512]{2,1,0:T(8,128)(2,1)S(1)}, bf16[32,128,512]{2,1,0:T(8,128)(2,1)}, u32[]{:S(2)}) copy-start(bf16[32,128,512]{2,1,0:T(8,128)(2,1)} %param.21) | copy-start | bytes 12582916

commit v7 on v6

--- a/solution.py
+++ b/solution.py
@@ -239,12 +239,12 @@
     attention = jnp.broadcast_to(attention[None], (peers,) + attention.shape)
     attention = lax.all_to_all(attention, ("sx", "sy"), 0, 0, tiled=True)
     other = lax.ppermute(attention, "sc", [(i, (i + 1) % pair) for i in range(pair)])
-    first = jnp.where(core == 0, attention, other)
-    second = jnp.where(core == 0, other, attention)
-    attention = jnp.stack([first, second], 1)
-    attention = attention.reshape(requests, tree_size, heads_dev, head_dim)
+    mine = jnp.einsum("xshd,hde->xse", attention, out_weight, preferred_element_type=jnp.float32)
+    theirs = jnp.einsum("xshd,hde->xse", other, out_weight, preferred_element_type=jnp.float32)
+    first = jnp.where(core == 0, mine, theirs)
+    second = jnp.where(core == 0, theirs, mine)
+    partial = jnp.stack([first, second], 1)
     heads_size = lax.axis_size("heads")
-    partial = jnp.einsum("rthd,hde->rte", attention, out_weight, preferred_element_type=jnp.float32)
     partial = partial.reshape(heads_size, requests // heads_size, tree_size, partial.shape[-1])
     return jnp.sum(lax.all_to_all(partial, "heads", 0, 0, tiled=True), axis=0)
 

time: 169 us -> 163 us (0.964)
  matrix products: 5.29 us -> 9.4 us
  local copies, waits for them, and re-layouts: 18.2 us -> 14.5 us
  waiting for transfers between devices: 32.7 us -> 29.1 us
  other arithmetic: 9.05 us -> 6.88 us
    dot_general x1 -> x2, matrix products: 2.32 us -> 6.43 us  [the longest x1 3.57 us: local(): jnp.einsum('xshd,hde->xse', attention, out_weight, preferred_element_type...]
    ppermute x1, waiting for transfers between devices: 4.29 us -> 0.71 us  [local(): lax.ppermute(attention, 'sc', [(i, (i + 1) % pair) for i in range(pair)])]
    another operation x2 -> x1, other arithmetic: 2.26 us -> 0.08 us  [local(): partial = jnp.stack([first, second], 1)]
    unnamed x15 -> x17, local copies, waits for them, and re-layouts: 7.61 us -> 5.43 us
  transfers between devices with their start and end apart: 2 -> 2, of which waited for: 2 -> 2; matrix products, arithmetic and copies ran while one was open for 3% -> 5% of each run, Pallas kernels for 0% -> 0%
where the time goes in v7:
time: 163 us
  blocking collectives  61.8 us (38%)
  Pallas kernels  33.5 us (21%)
  waiting for transfers between devices  29.1 us (18%)
  local copies, waits for them, and re-layouts  14.5 us (9%)
  matrix products  9.4 us (6%)
  starting transfers between devices  7.29 us (4%)
  other arithmetic  6.88 us (4%)
    pallas_call x1, Pallas kernels, context_part(): pl.pallas_call(context_kernel, grid_spec=grid_spec, out_shape=jax.ShapeDt...  33.5 us
    all_to_all x1, blocking collectives, local(): attention = lax.all_to_all(attention, ('sx', 'sy'), 0, 0, tiled=True)  32.4 us
    all_to_all x1, waiting for transfers between devices, local(): got = lax.all_to_all(sent, ('sx', 'sy'), 0, 0, tiled=True)  28.4 us
    all_to_all x1, blocking collectives, local(): return jnp.sum(lax.all_to_all(partial, 'heads', 0, 0, tiled=True), axis=0)  20.5 us
    all_to_all x1, blocking collectives, local(): parts = lax.all_to_all(parts, 'sc', 0, 0, tiled=True).astype(jnp.float32)  8.93 us
    all_to_all x1, starting transfers between devices, local(): got = lax.all_to_all(sent, ('sx', 'sy'), 0, 0, tiled=True)  7.29 us
    unnamed x17, local copies, waits for them, and re-layouts  5.43 us
    dot_general x1, matrix products, local(): jnp.einsum('xshd,hde->xse', attention, out_weight, preferred_element_type...  3.57 us
  transfers between devices with their start and end apart: 2, of which 2 were waited for; matrix products, arithmetic and copies ran while one was open for 5% of the time, Pallas kernels for 0%

profile of v7, /device:TPU:0, one launch (start us, length us, event | category | flops | bytes accessed | tf_op | source)
XLA Modules:
  0.0 162.9 jit_solution(9630737391576496577)
XLA Ops:
  0.0 0.0 copy-start
  0.0 0.0 copy-start.1
  0.0 0.0 copy-start.2
  0.0 2.6 %copy.178 = bf16[8,256,2,128]{3,1,2,0:T(8,128)(2,1)} copy(bf16[8,256,2,128]{3,2,1,0:T(2,128)(2,1)} %param.15) | data formatting | bytes 2097152 | tf_op args[4]
  2.6 0.0 copy-done
  2.6 0.0 copy-start.5
  2.6 1.9 %copy.128 = bf16[8,256,2,128]{1,3,2,0:T(8,128)(2,1)} copy(bf16[8,256,2,128]{3,2,1,0:T(2,128)(2,1)S(1)} %copy-done) | data formatting | bytes 2097152 | tf_op args[5]
  4.5 0.0 copy-done.1
  4.5 0.8 copy.124
  5.4 0.0 copy-done.2
  5.4 1.0 copy.126
  6.4 0.0 copy-done.5
  6.4 0.5 subtract_clamp_fusion.len_ref
  6.9 33.5 %shard_map.109 = bf16[2,8,2,2,144,256]{5,4,3,2,1,0:T(8,128)(2,1)} custom-call(s32[8,6]{1,0:T(8,128)} %use_ref.1, s32[8]{0:T(128)} %subtract_clamp_fusion.len_ref, bf16[8,64,32,128]{3,2,1,0:T(8,128)(2,1)} %q_ref.1, bf16[2,768,128]{2,1,0:T(8,128)(2,1)} %bitcast.127, bf16[2,128,768]{2,1,0:T(8,128)(2,1)} %bitcast.128, bf16[8,2,256,128]{3,2,1,0:T(8,128)(2,1)} %bitcast.125, ...), custom_call_target="tpu_custom_call" | custom-call | tf_op jit(solution)/shard_map/pallas_call | solution.py:137
  40.5 8.9 %all_to_all.20 = bf16[2,16,2,144,256]{4,3,2,1,0:T(8,128)(2,1)S(1)} all-to-all(bf16[2,16,2,144,256]{4,3,2,1,0:T(8,128)(2,1)} %bitcast.122), channel_id=1, replica_groups=mesh['heads'=4,'sx'=4,'sy'=4,'sc'=2] {'sc'}, dimensions={0} | all-to-all | bytes 9437184 | tf_op jit(solution)/shard_map/all_to_all | solution.py:190
  49.4 1.3 convert_element_type.52
  50.7 0.1 slice_reduce_fusion
  50.8 0.1 subtract_exponential_fusion
  50.9 1.4 multiply_reduce_fusion
  52.3 0.1 convert_convert_fusion
  52.4 0.1 fusion.38
  52.5 1.4 select_convert_fusion
  53.9 3.5 %copy.129 = bf16[16,2,144,256]{3,1,2,0:T(2,128)(2,1)} copy(bf16[16,2,144,256]{3,2,1,0:T(8,128)(2,1)S(1)} %select_convert_fusion) | data formatting | bytes 4718592 | tf_op jit(solution)/shard_map/convert_element_type | solution.py:207
  57.5 0.0 copy-start.3
  57.5 7.3 %all-to-all-start.1 = ((bf16[16,2,144,256]{3,1,2,0:T(2,128)(2,1)}), bf16[16,2,144,256]{3,1,2,0:T(2,128)(2,1)S(1)}, u32[]{:S(2)}, u32[]{:S(2)}) async-start(bf16[16,2,144,256]{3,1,2,0:T(2,128)(2,1)} %copy.129), calls=%async_computation.1 | async-start | bytes 4718592 | tf_op jit(solution)/shard_map/all_to_all | solution.py:208
  64.8 0.0 copy-done.3
  64.8 0.5 convolution_minimum_fusion.4
  65.4 0.4 convolution_minimum_fusion.3
  65.7 0.4 convolution_minimum_fusion.2
  66.1 0.4 convolution_minimum_fusion.1
  66.5 0.4 convolution_minimum_fusion
  66.9 0.4 fusion.50
  67.3 0.8 constant_dynamic-slice_fusion
  68.2 0.9 constant_dynamic-slice_fusion.1
  69.1 0.3 fusion.47
  69.4 0.2 fusion.17
  69.7 0.1 squeeze_reshape.11
  69.8 0.1 squeeze_reshape.9
  69.8 0.3 convolution_bitcast_fusion
  70.1 28.4 %all-to-all-done.1 = bf16[16,2,144,256]{3,1,2,0:T(2,128)(2,1)S(1)} async-done(((bf16[16,2,144,256]{3,1,2,0:T(2,128)(2,1)}), bf16[16,2,144,256]{3,1,2,0:T(2,128)(2,1)S(1)}, u32[]{:S(2)}, u32[]{:S(2)}) %all-to-all-start.1) | async-done | bytes 2359328 | tf_op jit(solution)/shard_map/all_to_all | solution.py:208
  98.5 0.1 reshape.174
  98.6 0.1 fusion.36
  98.7 0.1 reshape.166
  98.8 0.1 reshape.167
  98.9 0.1 reshape.170
  99.0 1.5 slice.31
  100.5 0.4 multiply_reduce_fusion.1
  100.9 0.1 copy.133
  101.1 0.3 fusion.14
  101.4 0.1 copy.144
  101.5 0.4 broadcast_in_dim.78
  101.9 32.4 %all_to_all.21 = bf16[16,16,32,128]{3,1,2,0:T(8,128)(2,1)S(1)} all-to-all(bf16[16,16,32,128]{3,1,2,0:T(8,128)(2,1)S(1)} %broadcast_in_dim.78), channel_id=1, replica_groups=mesh['heads'=4,'sx'=4,'sy'=4,'sc'=2] {'sx','sy'}, dimensions={0} | all-to-all | bytes 4194304 | tf_op jit(solution)/shard_map/all_to_all | solution.py:240
  134.3 0.0 collective-permute-start
  134.3 0.0 copy-start.4
  134.3 3.6 %fusion.4 = f32[16,16,512]{2,1,0:T(8,128)S(1)} fusion(bf16[16,16,32,128]{3,1,2,0:T(8,128)(2,1)S(1)} %all_to_all.21, bf16[32,128,512]{2,1,0:T(8,128)(2,1)} %param.21), kind=kOutput, calls=%fused_computation.7 | convolution fusion | flops 1073741824 | bytes 6815744 | tf_op jit(solution)/shard_map/xshd,hde->xse/dot_general | solution.py:242
  137.9 0.7 collective-permute-done
  138.6 0.0 copy-done.4
  138.6 2.9 %select_bitcast_fusion.1 = (f32[16,1,16,512]{3,2,0,1:T(8,128)S(1)}, f32[16,1,16,512]{3,2,0,1:T(8,128)S(1)}) fusion(f32[16,16,512]{2,1,0:T(8,128)S(1)} %fusion.4, pred[]{:T(512)S(6)} %eq.54, bf16[16,16,32,128]{3,1,2,0:T(8,128)(2,1)} %collective-permute-done, bf16[32,128,512]{2,1,0:T(8,128)(2,1)S(1)} %copy-done.4), kind=kOutput, calls=%fused_computation.21 | convolution fusion | flops 1074003968 | bytes 7864321 | tf_op jit(solution)/shard_map/xshd,hde->xse/dot_general | solution.py:243
  141.5 0.1 pad_maximum_fusion
  141.5 0.1 copy.145
  141.6 20.5 %all_to_all.22 = f32[4,2,64,512]{3,2,1,0:T(8,128)S(1)} all-to-all(f32[4,2,64,512]{3,2,1,0:T(8,128)S(1)} %bitcast.124), channel_id=1, replica_groups=mesh['heads'=4,'sx'=4,'sy'=4,'sc'=2] {'heads'}, dimensions={0} | all-to-all | bytes 2097152 | tf_op jit(solution)/shard_map/all_to_all | solution.py:249
  162.1 0.8 reduce_sum.49
  (16 shorter events, 0.3 us)
Async XLA Ops:
  0.0 2.6 %copy-start = (bf16[8,256,2,128]{3,2,1,0:T(2,128)(2,1)S(1)}, bf16[8,256,2,128]{3,2,1,0:T(2,128)(2,1)}, u32[]{:S(2)}) copy-start(bf16[8,256,2,128]{3,2,1,0:T(2,128)(2,1)} %param.16) | copy-start | bytes 3145732
  0.0 4.5 %copy-start.1 = (bf16[6,128,2,128]{3,2,1,0:T(2,128)(2,1)S(1)}, bf16[6,128,2,128]{3,2,1,0:T(2,128)(2,1)}, u32[]{:S(2)}) copy-start(bf16[6,128,2,128]{3,2,1,0:T(2,128)(2,1)} %param.12) | copy-start | bytes 1179652
  0.0 5.4 %copy-start.2 = (bf16[6,128,2,128]{3,2,1,0:T(2,128)(2,1)S(1)}, bf16[6,128,2,128]{3,2,1,0:T(2,128)(2,1)}, u32[]{:S(2)}) copy-start(bf16[6,128,2,128]{3,2,1,0:T(2,128)(2,1)} %param.13) | copy-start | bytes 1179652
  2.6 3.8 %copy-start.5 = (s32[8]{0:T(128)S(1)}, s32[8]{0:T(128)}, u32[]{:S(2)}) copy-start(s32[8]{0:T(128)} %param.17) | copy-start | bytes 100
  57.5 7.4 %copy-start.3 = (s32[8,64]{1,0:T(8,128)S(1)}, s32[8,64]{1,0:T(8,128)}, u32[]{:S(2)}) copy-start(s32[8,64]{1,0:T(8,128)} %param.20) | copy-start | bytes 6148
  57.5 41.0 %all-to-all-start.1 = ((bf16[16,2,144,256]{3,1,2,0:T(2,128)(2,1)}), bf16[16,2,144,256]{3,1,2,0:T(2,128)(2,1)S(1)}, u32[]{:S(2)}, u32[]{:S(2)}) async-start(bf16[16,2,144,256]{3,1,2,0:T(2,128)(2,1)} %copy.129), calls=%async_computation.1 | async-start | bytes 4718592 | tf_op jit(solution)/shard_map/all_to_all | solution.py:208
  134.3 4.3 %collective-permute-start = (bf16[16,16,32,128]{3,1,2,0:T(8,128)(2,1)S(1)}, bf16[16,16,32,128]{3,1,2,0:T(8,128)(2,1)}, u32[]{:S(2)}, u32[]{:S(2)}) collective-permute-start(bf16[16,16,32,128]{3,1,2,0:T(8,128)(2,1)S(1)} %all_to_all.21), channel_id=1, source_target_pairs={{0,1},{1,0},{2,3},{3,2},{4,5},{5,4},{6,7},{7,6},{8,9},{9,8},{10,11... | collective-permute-start | bytes 6291464 | tf_op jit(solution)/shard_map/ppermute | solution.py:241
  134.3 4.3 %copy-start.4 = (bf16[32,128,512]{2,1,0:T(8,128)(2,1)S(1)}, bf16[32,128,512]{2,1,0:T(8,128)(2,1)}, u32[]{:S(2)}) copy-start(bf16[32,128,512]{2,1,0:T(8,128)(2,1)} %param.21) | copy-start | bytes 12582916

commit v8 on v7

--- a/solution.py
+++ b/solution.py
@@ -144,6 +144,11 @@
 
 
 SEQ = ("sx", "sy", "sc")
+
+
+def exchange(x, axis_name):
+    flat = lax.all_to_all(x.reshape(x.shape[0], -1), axis_name, 0, 0, tiled=True)
+    return flat.reshape(x.shape)
 
 
 def unpack(parts, head_dim, axis):
@@ -205,7 +210,7 @@
             jnp.where(row == head_dim + 1, high, jnp.where(row == head_dim + 2, low, 0.0)),
         ),
     ).astype(jnp.bfloat16)
-    got = lax.all_to_all(sent, ("sx", "sy"), 0, 0, tiled=True)
+    got = exchange(sent, ("sx", "sy"))
     part_top, part_totals, part_weighted = unpack(got, head_dim, 0)
     top_all = jnp.max(part_top, axis=0)
     factor = jnp.exp(part_top - top_all[None])

time: 163 us -> 258 us (1.58)
  other arithmetic: 6.88 us -> 59.1 us
  local copies, waits for them, and re-layouts: 14.5 us -> 56.3 us
    convert_element_type x1 -> x2, other arithmetic: 1.41 us -> 37.1 us  [local(): sent = jnp.where(row < head_dim, scaled, jnp.where(row == head_dim, pair_...]
    broadcast_in_dim x0 -> x6, local copies, waits for them, and re-layouts: none -> 19.6 us  [the longest x2 6.57 us: local(): jnp.where(row == head_dim, pair_top, jnp.where(row == head_dim + 1, high,...]
    unnamed x17 -> x23, local copies, waits for them, and re-layouts: 5.43 us -> 21 us
    all_to_all x0 -> x1, other arithmetic: none -> 14.8 us  [exchange(): lax.all_to_all(x.reshape(x.shape[0], -1), axis_name, 0, 0, tiled=True)]
    reduce_sum x0 -> x1, local copies, waits for them, and re-layouts: none -> 10.5 us  [local(): scaled = jnp.sum(parts * factor, axis=0)]
    convert_element_type x1, local copies, waits for them, and re-layouts: 3.54 us -> 0.51 us  [local(): sent = jnp.where(row < head_dim, scaled, jnp.where(row == head_dim, pair_...]
  transfers between devices with their start and end apart: 2 -> 2, of which waited for: 2 -> 2; matrix products, arithmetic and copies ran while one was open for 5% -> 3% of each run, Pallas kernels for 0% -> 0%
where the time goes in v8:
time: 258 us; the launch traced here: 257 us
  blocking collectives  61.9 us (24%)
  other arithmetic  59.1 us (23%)
  local copies, waits for them, and re-layouts  56.3 us (22%)
  Pallas kernels  33.5 us (13%)
  waiting for transfers between devices  29.1 us (11%)
  matrix products  9.4 us (4%)
  starting transfers between devices  7.16 us (3%)
    convert_element_type x2, other arithmetic, local(): sent = jnp.where(row < head_dim, scaled, jnp.where(row == head_dim, pair_...  37.1 us
    pallas_call x1, Pallas kernels, context_part(): pl.pallas_call(context_kernel, grid_spec=grid_spec, out_shape=jax.ShapeDt...  33.5 us
    all_to_all x1, blocking collectives, local(): attention = lax.all_to_all(attention, ('sx', 'sy'), 0, 0, tiled=True)  32.4 us
    all_to_all x1, waiting for transfers between devices, exchange(): lax.all_to_all(x.reshape(x.shape[0], -1), axis_name, 0, 0, tiled=True)  28.4 us
    unnamed x23, local copies, waits for them, and re-layouts  21 us
    all_to_all x1, blocking collectives, local(): return jnp.sum(lax.all_to_all(partial, 'heads', 0, 0, tiled=True), axis=0)  20.5 us
    all_to_all x1, other arithmetic, exchange(): lax.all_to_all(x.reshape(x.shape[0], -1), axis_name, 0, 0, tiled=True)  14.8 us
    reduce_sum x1, local copies, waits for them, and re-layouts, local(): scaled = jnp.sum(parts * factor, axis=0)  10.5 us
  transfers between devices with their start and end apart: 2, of which 2 were waited for; matrix products, arithmetic and copies ran while one was open for 3% of the time, Pallas kernels for 0%

profile of v8, /device:TPU:0, one launch (start us, length us, event | category | flops | bytes accessed | tf_op | source)
XLA Modules:
  0.0 256.9 jit_solution(15544870618208457585)
XLA Ops:
  0.0 2.5 copy.120
  2.5 3.6 %copy.70 = bf16[8,256,2,128]{1,3,2,0:T(8,128)(2,1)} copy(bf16[8,256,2,128]{3,2,1,0:T(2,128)(2,1)} %param.16) | data formatting | bytes 2097152 | tf_op args[5]
  6.2 0.8 copy.66
  7.0 1.0 copy.68
  8.0 0.5 subtract_clamp_fusion.len_ref
  8.5 33.5 %shard_map.109 = bf16[2,8,2,2,144,256]{5,4,3,2,1,0:T(8,128)(2,1)} custom-call(s32[8,6]{1,0:T(8,128)} %use_ref.1, s32[8]{0:T(128)} %subtract_clamp_fusion.len_ref, bf16[8,64,32,128]{3,2,1,0:T(8,128)(2,1)} %q_ref.1, bf16[2,768,128]{2,1,0:T(8,128)(2,1)} %bitcast.136, bf16[2,128,768]{2,1,0:T(8,128)(2,1)} %bitcast.137, bf16[8,2,256,128]{3,2,1,0:T(8,128)(2,1)} %bitcast.134, ...), custom_call_target="tpu_custom_call" | custom-call | tf_op jit(solution)/shard_map/pallas_call | solution.py:137
  42.1 8.9 %all_to_all.21 = bf16[2,16,2,144,256]{4,3,2,1,0:T(8,128)(2,1)S(1)} all-to-all(bf16[2,16,2,144,256]{4,3,2,1,0:T(8,128)(2,1)} %bitcast.127), channel_id=1, replica_groups=mesh['heads'=4,'sx'=4,'sy'=4,'sc'=2] {'sc'}, dimensions={0} | all-to-all | bytes 9437184 | tf_op jit(solution)/shard_map/all_to_all | solution.py:195
  51.0 1.3 convert_element_type.60
  52.3 0.1 slice_reduce_fusion
  52.4 0.1 subtract_exponential_fusion
  52.6 1.4 multiply_reduce_fusion
  54.0 2.1 copy-done
  56.1 0.1 fusion.40
  56.2 10.5 %reduce_sum.48 = bf16[16,1,73728]{2,1,0:T(2,128)(2,1)} reshape(f32[16,2,144,256]{3,2,1,0:T(8,128)} %copy-done) | data formatting | bytes 7077888 | tf_op jit(solution)/shard_map/reduce_sum | solution.py:199
  66.8 0.2 broadcast_in_dim.77
  66.9 6.3 %broadcast_in_dim.78 = bf16[16,1,73728]{2,1,0:T(2,128)(2,1)} reshape(bf16[16,2,144,256]{3,2,1,0:T(8,128)(2,1)S(1)} %broadcast_in_dim.77) | data formatting | bytes 4718592 | tf_op jit(solution)/shard_map/jit(_where)/broadcast_in_dim | solution.py:210
  73.3 0.2 broadcast_in_dim.80
  73.5 6.4 %broadcast_in_dim.81 = bf16[16,1,73728]{2,1,0:T(2,128)(2,1)} reshape(bf16[16,2,144,256]{3,2,1,0:T(8,128)(2,1)S(1)} %broadcast_in_dim.80) | data formatting | bytes 4718592 | tf_op jit(solution)/shard_map/jit(_where)/broadcast_in_dim | solution.py:210
  79.8 0.2 broadcast_in_dim.74
  80.0 6.4 %broadcast_in_dim.75 = bf16[16,1,73728]{2,1,0:T(2,128)(2,1)} reshape(bf16[16,2,144,256]{3,2,1,0:T(8,128)(2,1)S(1)} %broadcast_in_dim.74) | data formatting | bytes 4718592 | tf_op jit(solution)/shard_map/jit(_where)/broadcast_in_dim | solution.py:207
  86.4 0.1 iota.52
  86.5 0.1 iota.53
  86.6 0.1 iota.56
  86.7 0.1 iota.60
  86.9 0.1 iota.64
  87.1 21.7 %fusion = bf16[16,1,73728]{2,1,0:T(2,128)(2,1)} fusion(bf16[16,1,73728]{2,1,0:T(2,128)(2,1)} %reduce_sum.48, pred[73728]{0:T(1024)(128)(4,1)S(1)} %iota.53, bf16[16,1,73728]{2,1,0:T(2,128)(2,1)} %broadcast_in_dim.75, pred[73728]{0:T(1024)(128)(4,1)S(1)} %iota.57, bf16[16,1,73728]{2,1,0:T(2,128)(2,1)} %broadcast_in_dim.78, pred[73728]{0:T(1024)(128)(4,1)S(1)} %iota.61, ...), kind=kLoop, calls=%fused_computation.5 | loop fusion | flops 4718592 | bytes 12091392 | tf_op jit(solution)/shard_map/convert_element_type | solution.py:212
  108.7 0.5 broadcast.136
  109.2 15.4 %reduce.6 = bf16[16,73728]{1,0:T(8,128)(2,1)S(1)} reduce(bf16[16,1,73728]{2,1,0:T(2,128)(2,1)} %fusion, bf16[]{:T(256)} %broadcast.136), dimensions={1}, to_apply=%fusion.reduce_sub_computation | reduce | bytes 4718594 | tf_op jit(solution)/shard_map/convert_element_type | solution.py:212
  124.7 3.0 %reshape.352 = bf16[16,2,36864]{2,1,0:T(2,128)(2,1)} reshape(bf16[16,73728]{1,0:T(8,128)(2,1)S(1)} %reduce.6) | data formatting | bytes 4718592
  127.8 7.2 %all-to-all-start.1 = ((bf16[16,2,36864]{2,1,0:T(2,128)(2,1)}), bf16[16,2,36864]{2,1,0:T(2,128)(2,1)S(1)}, u32[]{:S(2)}, u32[]{:S(2)}) async-start(bf16[16,2,36864]{2,1,0:T(2,128)(2,1)} %reshape.352), calls=%async_computation.1 | async-start | bytes 4718592 | tf_op jit(solution)/shard_map/all_to_all | solution.py:150
  135.0 0.5 convolution_minimum_fusion.4
  135.5 0.4 convolution_minimum_fusion.3
  135.9 0.4 convolution_minimum_fusion.2
  136.3 0.4 convolution_minimum_fusion.1
  136.7 0.4 convolution_minimum_fusion
  137.1 0.4 fusion.52
  137.5 0.8 constant_dynamic-slice_fusion
  138.3 0.9 constant_dynamic-slice_fusion.1
  139.2 0.3 fusion.49
  139.6 0.2 fusion.18
  139.8 0.1 squeeze_reshape.11
  139.9 0.1 squeeze_reshape.9
  140.0 0.3 convolution_bitcast_fusion
  140.3 28.4 %all-to-all-done.1 = bf16[16,2,36864]{2,1,0:T(2,128)(2,1)S(1)} async-done(((bf16[16,2,36864]{2,1,0:T(2,128)(2,1)}), bf16[16,2,36864]{2,1,0:T(2,128)(2,1)S(1)}, u32[]{:S(2)}, u32[]{:S(2)}) %all-to-all-start.1) | async-done | bytes 2359328 | tf_op jit(solution)/shard_map/all_to_all | solution.py:150
  168.6 6.9 %reshape.353 = bf16[16,1,73728]{2,1,0:T(2,128)(2,1)} reshape(bf16[16,2,36864]{2,1,0:T(2,128)(2,1)S(1)} %all-to-all-done.1) | data formatting | bytes 4718592
  175.6 14.8 %reduce.5 = bf16[16,73728]{1,0:T(8,128)(2,1)S(1)} reduce(bf16[16,1,73728]{2,1,0:T(2,128)(2,1)} %reshape.353, bf16[]{:T(256)} %constant.102), dimensions={1}, to_apply=%all_to_all.14.reduce_sub_computation | reduce | bytes 4718594 | tf_op jit(solution)/shard_map/all_to_all | solution.py:150
  190.4 0.5 copy.96
  191.0 1.3 copy-done.1
  192.4 0.1 reshape.345
  192.6 0.1 reshape.337
  192.7 0.1 reshape.338
  192.8 0.1 reshape.341
  192.8 2.0 multiply_reduce_fusion.1
  194.9 0.1 copy.72
  195.1 0.3 fusion.15
  195.4 0.4 broadcast_in_dim.87
  195.8 32.4 %all_to_all.22 = bf16[16,16,32,128]{3,1,2,0:T(8,128)(2,1)S(1)} all-to-all(bf16[16,16,32,128]{3,1,2,0:T(8,128)(2,1)S(1)} %broadcast_in_dim.87), channel_id=1, replica_groups=mesh['heads'=4,'sx'=4,'sy'=4,'sc'=2] {'sx','sy'}, dimensions={0} | all-to-all | bytes 4194304 | tf_op jit(solution)/shard_map/all_to_all | solution.py:245
  228.2 3.6 %fusion.5 = f32[16,16,512]{2,1,0:T(8,128)S(1)} fusion(bf16[16,16,32,128]{3,1,2,0:T(8,128)(2,1)S(1)} %all_to_all.22, bf16[32,128,512]{2,1,0:T(8,128)(2,1)} %param.21), kind=kOutput, calls=%fused_computation.11 | convolution fusion | flops 1073741824 | bytes 6815744 | tf_op jit(solution)/shard_map/xshd,hde->xse/dot_general | solution.py:247
  231.8 0.7 collective-permute-done
  232.5 2.9 %select_bitcast_fusion.1 = (f32[16,1,16,512]{3,2,0,1:T(8,128)S(1)}, f32[16,1,16,512]{3,2,0,1:T(8,128)S(1)}) fusion(f32[16,16,512]{2,1,0:T(8,128)S(1)} %fusion.5, pred[]{:T(512)S(6)} %eq.54, bf16[16,16,32,128]{3,1,2,0:T(8,128)(2,1)} %collective-permute-done, bf16[32,128,512]{2,1,0:T(8,128)(2,1)S(1)} %copy-done.5), kind=kOutput, calls=%fused_computation.25 | convolution fusion | flops 1074003968 | bytes 7864321 | tf_op jit(solution)/shard_map/xshd,hde->xse/dot_general | solution.py:248
  235.4 0.1 pad_maximum_fusion
  235.5 0.1 copy.83
  235.6 20.5 %all_to_all.23 = f32[4,2,64,512]{3,2,1,0:T(8,128)S(1)} all-to-all(f32[4,2,64,512]{3,2,1,0:T(8,128)S(1)} %bitcast.133), channel_id=1, replica_groups=mesh['heads'=4,'sx'=4,'sy'=4,'sc'=2] {'heads'}, dimensions={0} | all-to-all | bytes 2097152 | tf_op jit(solution)/shard_map/all_to_all | solution.py:254
  256.1 0.8 reduce_sum.52
  (39 shorter events, 0.7 us)
Async XLA Ops:
  0.0 6.2 %copy-start.2 = (bf16[6,128,2,128]{3,2,1,0:T(2,128)(2,1)S(1)}, bf16[6,128,2,128]{3,2,1,0:T(2,128)(2,1)}, u32[]{:S(2)}) copy-start(bf16[6,128,2,128]{3,2,1,0:T(2,128)(2,1)} %param.12) | copy-start | bytes 1179652
  0.0 7.0 %copy-start.3 = (bf16[6,128,2,128]{3,2,1,0:T(2,128)(2,1)S(1)}, bf16[6,128,2,128]{3,2,1,0:T(2,128)(2,1)}, u32[]{:S(2)}) copy-start(bf16[6,128,2,128]{3,2,1,0:T(2,128)(2,1)} %param.13) | copy-start | bytes 1179652
  0.0 8.0 %copy-start.6 = (s32[8]{0:T(128)S(1)}, s32[8]{0:T(128)}, u32[]{:S(2)}) copy-start(s32[8]{0:T(128)} %param.17) | copy-start | bytes 100
  53.9 2.2 copy-start
  124.7 10.3 %copy-start.4 = (s32[8,64]{1,0:T(8,128)S(1)}, s32[8,64]{1,0:T(8,128)}, u32[]{:S(2)}) copy-start(s32[8,64]{1,0:T(8,128)} %param.20) | copy-start | bytes 6148
  127.8 40.9 %all-to-all-start.1 = ((bf16[16,2,36864]{2,1,0:T(2,128)(2,1)}), bf16[16,2,36864]{2,1,0:T(2,128)(2,1)S(1)}, u32[]{:S(2)}, u32[]{:S(2)}) async-start(bf16[16,2,36864]{2,1,0:T(2,128)(2,1)} %reshape.352), calls=%async_computation.1 | async-start | bytes 4718592 | tf_op jit(solution)/shard_map/all_to_all | solution.py:150
  190.9 1.4 copy-start.1
  228.2 4.3 %collective-permute-start = (bf16[16,16,32,128]{3,1,2,0:T(8,128)(2,1)S(1)}, bf16[16,16,32,128]{3,1,2,0:T(8,128)(2,1)}, u32[]{:S(2)}, u32[]{:S(2)}) collective-permute-start(bf16[16,16,32,128]{3,1,2,0:T(8,128)(2,1)S(1)} %all_to_all.22), channel_id=1, source_target_pairs={{0,1},{1,0},{2,3},{3,2},{4,5},{5,4},{6,7},{7,6},{8,9},{9,8},{10,11... | collective-permute-start | bytes 6291464 | tf_op jit(solution)/shard_map/ppermute | solution.py:246
  228.2 4.3 %copy-start.5 = (bf16[32,128,512]{2,1,0:T(8,128)(2,1)S(1)}, bf16[32,128,512]{2,1,0:T(8,128)(2,1)}, u32[]{:S(2)}) copy-start(bf16[32,128,512]{2,1,0:T(8,128)(2,1)} %param.21) | copy-start | bytes 12582916

commit v9 on v7

--- a/solution.py
+++ b/solution.py
@@ -58,12 +58,24 @@
     )
 
 
+def pick(ref, k):
+    heads = ref.shape[-2]
+    rows = [ref[..., j, :].reshape(-1, ref.shape[-1]) for j in range(heads)]
+    picked = rows[0]
+    for j in range(1, heads):
+        picked = jnp.where(k == j, rows[j], picked)
+    return picked
+
+
 def context_kernel(use_ref, len_ref, q_ref, kp_ref, vp_ref, ko_ref, vo_ref, acc_ref):
-    r = pl.program_id(1)
+    r = pl.program_id(0)
+    k = pl.program_id(1)
     scaling = 1.0 / math.sqrt(q_ref.shape[-1])
     q = q_ref[0].reshape(-1, q_ref.shape[-1])
-    kp = kp_ref[0]
-    ko = ko_ref[0, 0]
+    kp = pick(kp_ref, k)
+    ko = pick(ko_ref, k)
+    vp = pick(vp_ref, k)
+    vo = pick(vo_ref, k)
     dims = (((1,), (1,)), ((), ()))
     s_pre = lax.dot_general(kp, q, dims, preferred_element_type=jnp.float32) * scaling
     s_own = lax.dot_general(ko, q, dims, preferred_element_type=jnp.float32) * scaling
@@ -84,9 +96,10 @@
     w_pre = jnp.exp(s_pre - top)
     w_own = jnp.exp(s_own - top)
     totals = jnp.sum(w_pre, axis=0, keepdims=True) + jnp.sum(w_own, axis=0, keepdims=True)
-    acc = jnp.dot(vp_ref[0], w_pre.astype(jnp.bfloat16), preferred_element_type=jnp.float32)
-    acc = acc + jnp.dot(
-        vo_ref[0, 0], w_own.astype(jnp.bfloat16), preferred_element_type=jnp.float32
+    lead = (((0,), (0,)), ((), ()))
+    acc = lax.dot_general(vp, w_pre.astype(jnp.bfloat16), lead, preferred_element_type=jnp.float32)
+    acc = acc + lax.dot_general(
+        vo, w_own.astype(jnp.bfloat16), lead, preferred_element_type=jnp.float32
     )
     head_dim = acc.shape[0]
     pieces = acc_ref.shape[0] * acc_ref.shape[2]
@@ -115,23 +128,19 @@
     n_pre = block_count * block_len
     rows = tree_size * group_size
     width = rows // pieces
-    kp = jnp.transpose(prefix_keys.reshape(n_pre, kv_dev, head_dim), (1, 0, 2))
-    vp = jnp.transpose(prefix_values.reshape(n_pre, kv_dev, head_dim), (1, 2, 0))
-    ko = jnp.transpose(own_keys, (0, 2, 1, 3))
-    vo = jnp.transpose(own_values, (0, 2, 3, 1))
     grid_spec = pltpu.PrefetchScalarGridSpec(
         num_scalar_prefetch=2,
-        grid=(kv_dev, requests),
+        grid=(requests, kv_dev),
         in_specs=[
-            pl.BlockSpec((1, tree_size, group_size, head_dim), lambda k, r, u, n: (r, 0, k, 0)),
-            pl.BlockSpec((1, n_pre, head_dim), lambda k, r, u, n: (k, 0, 0)),
-            pl.BlockSpec((1, head_dim, n_pre), lambda k, r, u, n: (k, 0, 0)),
-            pl.BlockSpec((1, 1, private_dev, head_dim), lambda k, r, u, n: (r, k, 0, 0)),
-            pl.BlockSpec((1, 1, head_dim, private_dev), lambda k, r, u, n: (r, k, 0, 0)),
+            pl.BlockSpec((1, tree_size, group_size, head_dim), lambda r, k, u, n: (r, 0, k, 0)),
+            pl.BlockSpec((block_count, block_len, kv_dev, head_dim), lambda r, k, u, n: (0, 0, 0, 0)),
+            pl.BlockSpec((block_count, block_len, kv_dev, head_dim), lambda r, k, u, n: (0, 0, 0, 0)),
+            pl.BlockSpec((1, private_dev, kv_dev, head_dim), lambda r, k, u, n: (r, 0, 0, 0)),
+            pl.BlockSpec((1, private_dev, kv_dev, head_dim), lambda r, k, u, n: (r, 0, 0, 0)),
         ],
         out_specs=pl.BlockSpec(
             (pair, 1, pieces // pair, 1, head_dim + 16, width),
-            lambda k, r, u, n: (0, r, 0, k, 0, 0),
+            lambda r, k, u, n: (0, r, 0, k, 0, 0),
         ),
     )
     return pl.pallas_call(
@@ -140,7 +149,7 @@
         out_shape=jax.ShapeDtypeStruct(
             (pair, requests, pieces // pair, kv_dev, head_dim + 16, width), jnp.bfloat16
         ),
-    )(use_rows, own_lengths, queries, kp, vp, ko, vo)
+    )(use_rows, own_lengths, queries, prefix_keys, prefix_values, own_keys, own_values)
 
 
 SEQ = ("sx", "sy", "sc")

time: 163 us -> 192 us (1.18)
  Pallas kernels: 33.5 us -> 68.3 us
  local copies, waits for them, and re-layouts: 14.5 us -> 8.14 us
    pallas_call x1, Pallas kernels: 33.5 us -> 68.3 us  [context_part(): pl.pallas_call(context_kernel, grid_spec=grid_spec, out_shape=jax.ShapeDt...]
    unnamed x17 -> x6, local copies, waits for them, and re-layouts: 5.43 us -> 0.08 us
where the time goes in v9:
time: 192 us
  Pallas kernels  68.3 us (36%)
  blocking collectives  61.8 us (32%)
  waiting for transfers between devices  29.1 us (15%)
  matrix products  9.41 us (5%)
  local copies, waits for them, and re-layouts  8.14 us (4%)
  other arithmetic  7.53 us (4%)
  starting transfers between devices  7.28 us (4%)
    pallas_call x1, Pallas kernels, context_part(): pl.pallas_call(context_kernel, grid_spec=grid_spec, out_shape=jax.ShapeDt...  68.3 us
    all_to_all x1, blocking collectives, local(): attention = lax.all_to_all(attention, ('sx', 'sy'), 0, 0, tiled=True)  32.4 us
    all_to_all x1, waiting for transfers between devices, local(): got = lax.all_to_all(sent, ('sx', 'sy'), 0, 0, tiled=True)  28.4 us
    all_to_all x1, blocking collectives, local(): return jnp.sum(lax.all_to_all(partial, 'heads', 0, 0, tiled=True), axis=0)  20.5 us
    all_to_all x1, blocking collectives, local(): parts = lax.all_to_all(parts, 'sc', 0, 0, tiled=True).astype(jnp.float32)  8.93 us
    all_to_all x1, starting transfers between devices, local(): got = lax.all_to_all(sent, ('sx', 'sy'), 0, 0, tiled=True)  7.27 us
  transfers between devices with their start and end apart: 2, of which 2 were waited for; matrix products, arithmetic and copies ran while one was open for 5% of the time, Pallas kernels for 0%

profile of v9, /device:TPU:0, one launch (start us, length us, event | category | flops | bytes accessed | tf_op | source)
XLA Modules:
  0.0 191.9 jit_solution(17870371280670650837)
XLA Ops:
  0.0 1.2 subtract_clamp_fusion.len_ref
  1.2 68.3 %shard_map.109 = bf16[2,8,2,2,144,256]{5,4,3,2,1,0:T(8,128)(2,1)} custom-call(s32[8,6]{1,0:T(8,128)} %use_ref.1, s32[8]{0:T(128)} %subtract_clamp_fusion.len_ref, bf16[8,64,32,128]{3,2,1,0:T(8,128)(2,1)} %q_ref.1, bf16[6,128,2,128]{3,2,1,0:T(2,128)(2,1)} %kp_ref.1, bf16[6,128,2,128]{3,2,1,0:T(2,128)(2,1)} %vp_ref.1, bf16[8,256,2,128]{3,2,1,0:T(2,128)(2,1)} %ko_ref.1, ...), custom_call_target="tpu_custom_call" | custom-call | tf_op jit(solution)/shard_map/pallas_call | solution.py:146
  69.4 8.9 %all_to_all.20 = bf16[2,16,2,144,256]{4,3,2,1,0:T(8,128)(2,1)S(1)} all-to-all(bf16[2,16,2,144,256]{4,3,2,1,0:T(8,128)(2,1)} %bitcast.113), channel_id=1, replica_groups=mesh['heads'=4,'sx'=4,'sy'=4,'sc'=2] {'sc'}, dimensions={0} | all-to-all | bytes 9437184 | tf_op jit(solution)/shard_map/all_to_all | solution.py:199
  78.4 1.3 convert_element_type.52
  79.6 0.1 slice_reduce_fusion
  79.8 0.1 subtract_exponential_fusion
  79.9 1.4 multiply_reduce_fusion
  81.3 0.1 convert_convert_fusion
  81.4 0.1 fusion.38
  81.5 1.4 select_convert_fusion
  82.9 3.5 %copy.90 = bf16[16,2,144,256]{3,1,2,0:T(2,128)(2,1)} copy(bf16[16,2,144,256]{3,2,1,0:T(8,128)(2,1)S(1)} %select_convert_fusion) | data formatting | bytes 4718592 | tf_op jit(solution)/shard_map/convert_element_type | solution.py:216
  86.4 0.0 copy-start
  86.4 7.3 %all-to-all-start.1 = ((bf16[16,2,144,256]{3,1,2,0:T(2,128)(2,1)}), bf16[16,2,144,256]{3,1,2,0:T(2,128)(2,1)S(1)}, u32[]{:S(2)}, u32[]{:S(2)}) async-start(bf16[16,2,144,256]{3,1,2,0:T(2,128)(2,1)} %copy.90), calls=%async_computation.1 | async-start | bytes 4718592 | tf_op jit(solution)/shard_map/all_to_all | solution.py:217
  93.8 0.0 copy-done
  93.8 0.5 convolution_minimum_fusion.4
  94.3 0.4 convolution_minimum_fusion.3
  94.7 0.4 convolution_minimum_fusion.2
  95.1 0.4 convolution_minimum_fusion.1
  95.5 0.4 convolution_minimum_fusion
  95.9 0.4 fusion.50
  96.3 0.8 constant_dynamic-slice_fusion
  97.1 0.9 constant_dynamic-slice_fusion.1
  98.1 0.3 fusion.47
  98.4 0.2 fusion.17
  98.6 0.1 squeeze_reshape.11
  98.7 0.1 squeeze_reshape.9
  98.8 0.3 convolution_bitcast_fusion
  99.1 28.4 %all-to-all-done.1 = bf16[16,2,144,256]{3,1,2,0:T(2,128)(2,1)S(1)} async-done(((bf16[16,2,144,256]{3,1,2,0:T(2,128)(2,1)}), bf16[16,2,144,256]{3,1,2,0:T(2,128)(2,1)S(1)}, u32[]{:S(2)}, u32[]{:S(2)}) %all-to-all-start.1) | async-done | bytes 2359328 | tf_op jit(solution)/shard_map/all_to_all | solution.py:217
  127.5 0.1 reshape.166
  127.6 0.1 fusion.36
  127.6 0.1 reshape.158
  127.7 0.1 reshape.159
  127.8 0.1 reshape.162
  127.9 1.5 slice.31
  129.5 0.4 multiply_reduce_fusion.1
  129.9 0.1 copy.94
  130.1 0.3 fusion.14
  130.4 0.1 copy.105
  130.4 0.4 broadcast_in_dim.78
  130.8 32.4 %all_to_all.21 = bf16[16,16,32,128]{3,1,2,0:T(8,128)(2,1)S(1)} all-to-all(bf16[16,16,32,128]{3,1,2,0:T(8,128)(2,1)S(1)} %broadcast_in_dim.78), channel_id=1, replica_groups=mesh['heads'=4,'sx'=4,'sy'=4,'sc'=2] {'sx','sy'}, dimensions={0} | all-to-all | bytes 4194304 | tf_op jit(solution)/shard_map/all_to_all | solution.py:249
  163.2 0.0 collective-permute-start
  163.2 0.0 copy-start.1
  163.2 3.6 %fusion.4 = f32[16,16,512]{2,1,0:T(8,128)S(1)} fusion(bf16[16,16,32,128]{3,1,2,0:T(8,128)(2,1)S(1)} %all_to_all.21, bf16[32,128,512]{2,1,0:T(8,128)(2,1)} %param.21), kind=kOutput, calls=%fused_computation.7 | convolution fusion | flops 1073741824 | bytes 6815744 | tf_op jit(solution)/shard_map/xshd,hde->xse/dot_general | solution.py:251
  166.8 0.7 collective-permute-done
  167.5 0.0 copy-done.1
  167.5 2.9 %select_bitcast_fusion.1 = (f32[16,1,16,512]{3,2,0,1:T(8,128)S(1)}, f32[16,1,16,512]{3,2,0,1:T(8,128)S(1)}) fusion(f32[16,16,512]{2,1,0:T(8,128)S(1)} %fusion.4, pred[]{:T(512)S(6)} %eq.54, bf16[16,16,32,128]{3,1,2,0:T(8,128)(2,1)} %collective-permute-done, bf16[32,128,512]{2,1,0:T(8,128)(2,1)S(1)} %copy-done.1), kind=kOutput, calls=%fused_computation.20 | convolution fusion | flops 1074003968 | bytes 7864321 | tf_op jit(solution)/shard_map/xshd,hde->xse/dot_general | solution.py:252
  170.4 0.1 pad_maximum_fusion
  170.5 0.1 copy.106
  170.6 20.5 %all_to_all.22 = f32[4,2,64,512]{3,2,1,0:T(8,128)S(1)} all-to-all(f32[4,2,64,512]{3,2,1,0:T(8,128)S(1)} %bitcast.115), channel_id=1, replica_groups=mesh['heads'=4,'sx'=4,'sy'=4,'sc'=2] {'heads'}, dimensions={0} | all-to-all | bytes 2097152 | tf_op jit(solution)/shard_map/all_to_all | solution.py:258
  191.1 0.8 reduce_sum.49
  (16 shorter events, 0.3 us)
Async XLA Ops:
  86.4 7.3 %copy-start = (s32[8,64]{1,0:T(8,128)S(1)}, s32[8,64]{1,0:T(8,128)}, u32[]{:S(2)}) copy-start(s32[8,64]{1,0:T(8,128)} %param.20) | copy-start | bytes 6148
  86.4 41.0 %all-to-all-start.1 = ((bf16[16,2,144,256]{3,1,2,0:T(2,128)(2,1)}), bf16[16,2,144,256]{3,1,2,0:T(2,128)(2,1)S(1)}, u32[]{:S(2)}, u32[]{:S(2)}) async-start(bf16[16,2,144,256]{3,1,2,0:T(2,128)(2,1)} %copy.90), calls=%async_computation.1 | async-start | bytes 4718592 | tf_op jit(solution)/shard_map/all_to_all | solution.py:217
  163.2 4.3 %collective-permute-start = (bf16[16,16,32,128]{3,1,2,0:T(8,128)(2,1)S(1)}, bf16[16,16,32,128]{3,1,2,0:T(8,128)(2,1)}, u32[]{:S(2)}, u32[]{:S(2)}) collective-permute-start(bf16[16,16,32,128]{3,1,2,0:T(8,128)(2,1)S(1)} %all_to_all.21), channel_id=1, source_target_pairs={{0,1},{1,0},{2,3},{3,2},{4,5},{5,4},{6,7},{7,6},{8,9},{9,8},{10,11... | collective-permute-start | bytes 6291464 | tf_op jit(solution)/shard_map/ppermute | solution.py:250
  163.2 4.3 %copy-start.1 = (bf16[32,128,512]{2,1,0:T(8,128)(2,1)S(1)}, bf16[32,128,512]{2,1,0:T(8,128)(2,1)}, u32[]{:S(2)}) copy-start(bf16[32,128,512]{2,1,0:T(8,128)(2,1)} %param.21) | copy-start | bytes 12582916

commit v10 on v7

--- a/solution.py
+++ b/solution.py
@@ -187,11 +187,15 @@
     )
     width = chunk * group_size
     parts = acc.reshape(pair, seq_size // pair, kv_dev, head_dim + 16, width)
-    parts = lax.all_to_all(parts, "sc", 0, 0, tiled=True).astype(jnp.float32)
-    part_top = parts[:, :, :, head_dim : head_dim + 1]
-    pair_top = jnp.max(part_top, axis=0)
-    factor = jnp.exp(part_top - pair_top[None])
-    scaled = jnp.sum(parts * factor, axis=0)
+    keep = lax.dynamic_index_in_dim(parts, core, 0, keepdims=False)
+    send = lax.dynamic_index_in_dim(parts, pair - 1 - core, 0, keepdims=False)
+    recv = lax.ppermute(send, "sc", [(i, (i + 1) % pair) for i in range(pair)])
+    keep = keep.astype(jnp.float32)
+    recv = recv.astype(jnp.float32)
+    keep_top = keep[:, :, head_dim : head_dim + 1]
+    recv_top = recv[:, :, head_dim : head_dim + 1]
+    pair_top = jnp.maximum(keep_top, recv_top)
+    scaled = keep * jnp.exp(keep_top - pair_top) + recv * jnp.exp(recv_top - pair_top)
     pair_totals = scaled[:, :, head_dim + 1 : head_dim + 2] + scaled[:, :, head_dim + 2 : head_dim + 3]
     high = pair_totals.astype(jnp.bfloat16).astype(jnp.float32)
     low = pair_totals - high

time: 163 us -> 163 us (level)
  blocking collectives: 61.8 us -> 52.9 us
  other arithmetic: 6.88 us -> 14.5 us
  waiting for transfers between devices: 29.1 us -> 33.8 us
  local copies, waits for them, and re-layouts: 14.5 us -> 11.1 us
    all_to_all x1 -> x0, blocking collectives: 8.93 us -> none  [local(): parts = lax.all_to_all(parts, 'sc', 0, 0, tiled=True).astype(jnp.float32)]
    squeeze x0 -> x1, other arithmetic: none -> 6.09 us  [local(): send = lax.dynamic_index_in_dim(parts, pair - 1 - core, 0, keepdims=False)]
    ppermute x0 -> x1, waiting for transfers between devices: none -> 4.71 us  [local(): recv = lax.ppermute(send, 'sc', [(i, (i + 1) % pair) for i in range(pair)])]
    convert_element_type x1 -> x0, local copies, waits for them, and re-layouts: 3.54 us -> none  [local(): sent = jnp.where(row < head_dim, scaled, jnp.where(row == head_dim, pair_...]
    unnamed x17 -> x19, local copies, waits for them, and re-layouts: 5.43 us -> 7.12 us
  transfers between devices with their start and end apart: 2 -> 3, of which waited for: 2 -> 3; matrix products, arithmetic and copies ran while one was open for 5% -> 5% of each run, Pallas kernels for 0% -> 0%
where the time goes in v10:
time: 163 us
  blocking collectives  52.9 us (32%)
  waiting for transfers between devices  33.8 us (21%)
  Pallas kernels  33.5 us (21%)
  other arithmetic  14.5 us (9%)
  local copies, waits for them, and re-layouts  11.1 us (7%)
  matrix products  9.4 us (6%)
  starting transfers between devices  7.16 us (4%)
    pallas_call x1, Pallas kernels, context_part(): pl.pallas_call(context_kernel, grid_spec=grid_spec, out_shape=jax.ShapeDt...  33.5 us
    all_to_all x1, blocking collectives, local(): attention = lax.all_to_all(attention, ('sx', 'sy'), 0, 0, tiled=True)  32.4 us
    all_to_all x1, waiting for transfers between devices, local(): got = lax.all_to_all(sent, ('sx', 'sy'), 0, 0, tiled=True)  28.4 us
    all_to_all x1, blocking collectives, local(): return jnp.sum(lax.all_to_all(partial, 'heads', 0, 0, tiled=True), axis=0)  20.5 us
    all_to_all x1, starting transfers between devices, local(): got = lax.all_to_all(sent, ('sx', 'sy'), 0, 0, tiled=True)  7.16 us
    unnamed x19, local copies, waits for them, and re-layouts  7.12 us
    squeeze x1, other arithmetic, local(): send = lax.dynamic_index_in_dim(parts, pair - 1 - core, 0, keepdims=False)  6.09 us
    ppermute x1, waiting for transfers between devices, local(): recv = lax.ppermute(send, 'sc', [(i, (i + 1) % pair) for i in range(pair)])  4.71 us
  transfers between devices with their start and end apart: 3, of which 3 were waited for; matrix products, arithmetic and copies ran while one was open for 5% of the time, Pallas kernels for 0%

profile of v10, /device:TPU:0, one launch (start us, length us, event | category | flops | bytes accessed | tf_op | source)
XLA Modules:
  0.0 162.9 jit_solution(11851618899997604570)
XLA Ops:
  0.0 0.0 copy-start.1
  0.0 0.0 copy-start.2
  0.0 0.0 copy-start.5
  0.0 2.5 %copy.139 = bf16[8,256,2,128]{3,1,2,0:T(8,128)(2,1)} copy(bf16[8,256,2,128]{3,2,1,0:T(2,128)(2,1)} %param.15) | data formatting | bytes 2097152 | tf_op args[4]
  2.6 3.6 %copy.86 = bf16[8,256,2,128]{1,3,2,0:T(8,128)(2,1)} copy(bf16[8,256,2,128]{3,2,1,0:T(2,128)(2,1)} %param.16) | data formatting | bytes 2097152 | tf_op args[5]
  6.2 0.0 copy-done.1
  6.2 0.8 copy.82
  7.0 0.0 copy-done.2
  7.0 1.0 copy.84
  8.1 0.0 copy-done.5
  8.1 0.5 subtract_clamp_fusion.len_ref
  8.6 33.5 %shard_map.109 = bf16[2,8,2,2,144,256]{5,4,3,2,1,0:T(8,128)(2,1)} custom-call(s32[8,6]{1,0:T(8,128)} %use_ref.1, s32[8]{0:T(128)} %subtract_clamp_fusion.len_ref, bf16[8,64,32,128]{3,2,1,0:T(8,128)(2,1)} %q_ref.1, bf16[2,768,128]{2,1,0:T(8,128)(2,1)} %bitcast.133, bf16[2,128,768]{2,1,0:T(8,128)(2,1)} %bitcast.134, bf16[8,2,256,128]{3,2,1,0:T(8,128)(2,1)} %bitcast.131, ...), custom_call_target="tpu_custom_call" | custom-call | tf_op jit(solution)/shard_map/pallas_call | solution.py:137
  42.1 6.1 %dynamic-slice_bitcast_fusion = (bf16[16,2,144,256]{3,2,1,0:T(8,128)(2,1)}, f32[16,2,144,256]{3,2,1,0:T(8,128)}) fusion(bf16[2,16,2,144,256]{4,3,2,1,0:T(8,128)(2,1)} %bitcast.127, s32[]{:T(128)S(6)} %select_n.71, s32[]{:T(128)S(6)} %select_n.70), kind=kLoop, calls=%fused_computation.8 | loop fusion | flops 1179648 | bytes 11796488 | tf_op jit(solution)/shard_map/jit(dynamic_index_in_dim)/squeeze | solution.py:191
  48.2 0.0 collective-permute-start
  48.2 0.0 copy-start
  48.2 4.7 %collective-permute-done = bf16[16,2,144,256]{3,2,1,0:T(8,128)(2,1)S(1)} collective-permute-done((bf16[16,2,144,256]{3,2,1,0:T(8,128)(2,1)}, bf16[16,2,144,256]{3,2,1,0:T(8,128)(2,1)S(1)}, u32[]{:S(2)}, u32[]{:S(2)}) %collective-permute-start) | collective-permute-done | bytes 2359328 | tf_op jit(solution)/shard_map/ppermute | solution.py:192
  53.0 0.6 convert_element_type.60
  53.5 1.0 subtract_exponential_fusion.1
  54.5 0.1 subtract_exponential_fusion
  54.7 0.0 copy-done
  54.7 1.2 multiply_add_fusion
  55.8 0.1 fusion.39
  55.9 0.1 convert_convert_fusion
  56.1 0.0 copy-start.3
  56.1 2.9 %select_convert_fusion = bf16[16,2,144,256]{3,2,1,0:T(8,128)(2,1)} fusion(f32[16,2,144,256]{3,2,1,0:T(8,128)S(1)} %multiply_add_fusion, bf16[16,2,256]{2,1,0:T(2,128)(2,1)S(1)} %bitcast.140, bf16[16,2,256]{2,1,0:T(2,128)(2,1)S(1)} %bitcast.141, bf16[16,2,256]{2,1,0:T(2,128)(2,1)S(1)} %bitcast.139, pred[144]{0:T(512)(128)(4,1)S(1)} %get-tuple-element.20, ...), kind=kLoop, calls=%fused_computation | loop fusion | flops 4718592 | bytes 7127616 | tf_op jit(solution)/shard_map/convert_element_type | solution.py:211
  59.0 7.2 %all-to-all-start = ((bf16[16,2,144,256]{3,2,1,0:T(8,128)(2,1)}), bf16[16,2,144,256]{3,2,1,0:T(8,128)(2,1)S(1)}, u32[]{:S(2)}, u32[]{:S(2)}) async-start(bf16[16,2,144,256]{3,2,1,0:T(8,128)(2,1)} %select_convert_fusion), calls=%async_computation | async-start | bytes 4718592 | tf_op jit(solution)/shard_map/all_to_all | solution.py:212
  66.2 0.0 copy-done.3
  66.2 0.5 convolution_minimum_fusion.4
  66.7 0.4 convolution_minimum_fusion.3
  67.1 0.4 convolution_minimum_fusion.2
  67.5 0.4 convolution_minimum_fusion.1
  67.9 0.4 convolution_minimum_fusion
  68.3 0.4 fusion.51
  68.7 0.8 constant_dynamic-slice_fusion
  69.5 0.9 constant_dynamic-slice_fusion.1
  70.4 0.3 fusion.48
  70.8 0.2 fusion.17
  71.0 0.1 squeeze_reshape.11
  71.1 0.1 squeeze_reshape.9
  71.2 0.3 convolution_bitcast_fusion
  71.5 28.4 %all-to-all-done = bf16[16,2,144,256]{3,2,1,0:T(8,128)(2,1)S(1)} async-done(((bf16[16,2,144,256]{3,2,1,0:T(8,128)(2,1)}), bf16[16,2,144,256]{3,2,1,0:T(8,128)(2,1)S(1)}, u32[]{:S(2)}, u32[]{:S(2)}) %all-to-all-start) | async-done | bytes 2359328 | tf_op jit(solution)/shard_map/all_to_all | solution.py:212
  99.9 0.1 fusion.47
  100.0 0.1 reshape.171
  100.1 0.1 fusion.32
  100.2 0.1 fusion.37
  100.2 0.1 reshape.162
  100.3 0.1 reshape.163
  100.4 0.1 reshape.167
  100.5 0.4 multiply_reduce_fusion
  100.9 0.1 copy.88
  101.1 0.3 fusion.14
  101.4 0.1 copy.98
  101.4 0.4 broadcast_in_dim.80
  101.8 32.4 %all_to_all.15 = bf16[16,16,32,128]{3,1,2,0:T(8,128)(2,1)S(1)} all-to-all(bf16[16,16,32,128]{3,1,2,0:T(8,128)(2,1)S(1)} %broadcast_in_dim.80), channel_id=1, replica_groups=mesh['heads'=4,'sx'=4,'sy'=4,'sc'=2] {'sx','sy'}, dimensions={0} | all-to-all | bytes 4194304 | tf_op jit(solution)/shard_map/all_to_all | solution.py:244
  134.2 0.0 collective-permute-start.1
  134.2 0.0 copy-start.4
  134.2 3.6 %fusion.4 = f32[16,16,512]{2,1,0:T(8,128)S(1)} fusion(bf16[16,16,32,128]{3,1,2,0:T(8,128)(2,1)S(1)} %all_to_all.15, bf16[32,128,512]{2,1,0:T(8,128)(2,1)} %param.21), kind=kOutput, calls=%fused_computation.9 | convolution fusion | flops 1073741824 | bytes 6815744 | tf_op jit(solution)/shard_map/xshd,hde->xse/dot_general | solution.py:246
  137.8 0.7 collective-permute-done.1
  138.5 0.0 copy-done.4
  138.5 2.9 %select_bitcast_fusion.1 = (f32[16,1,16,512]{3,2,0,1:T(8,128)S(1)}, f32[16,1,16,512]{3,2,0,1:T(8,128)S(1)}) fusion(f32[16,16,512]{2,1,0:T(8,128)S(1)} %fusion.4, pred[]{:T(512)S(6)} %eq.54, bf16[16,16,32,128]{3,1,2,0:T(8,128)(2,1)} %collective-permute-done.1, bf16[32,128,512]{2,1,0:T(8,128)(2,1)S(1)} %copy-done.4), kind=kOutput, calls=%fused_computation.23 | convolution fusion | flops 1074003968 | bytes 7864321 | tf_op jit(solution)/shard_map/xshd,hde->xse/dot_general | solution.py:247
  141.4 0.1 pad_maximum_fusion
  141.5 0.1 copy.99
  141.6 20.5 %all_to_all.16 = f32[4,2,64,512]{3,2,1,0:T(8,128)S(1)} all-to-all(f32[4,2,64,512]{3,2,1,0:T(8,128)S(1)} %bitcast.130), channel_id=1, replica_groups=mesh['heads'=4,'sx'=4,'sy'=4,'sc'=2] {'heads'}, dimensions={0} | all-to-all | bytes 2097152 | tf_op jit(solution)/shard_map/all_to_all | solution.py:253
  162.1 0.8 reduce_sum.39
  (17 shorter events, 0.3 us)
Async XLA Ops:
  0.0 6.2 %copy-start.1 = (bf16[6,128,2,128]{3,2,1,0:T(2,128)(2,1)S(1)}, bf16[6,128,2,128]{3,2,1,0:T(2,128)(2,1)}, u32[]{:S(2)}) copy-start(bf16[6,128,2,128]{3,2,1,0:T(2,128)(2,1)} %param.12) | copy-start | bytes 1179652
  0.0 7.0 %copy-start.2 = (bf16[6,128,2,128]{3,2,1,0:T(2,128)(2,1)S(1)}, bf16[6,128,2,128]{3,2,1,0:T(2,128)(2,1)}, u32[]{:S(2)}) copy-start(bf16[6,128,2,128]{3,2,1,0:T(2,128)(2,1)} %param.13) | copy-start | bytes 1179652
  0.0 8.1 %copy-start.5 = (s32[8]{0:T(128)S(1)}, s32[8]{0:T(128)}, u32[]{:S(2)}) copy-start(s32[8]{0:T(128)} %param.17) | copy-start | bytes 100
  48.2 4.7 %collective-permute-start = (bf16[16,2,144,256]{3,2,1,0:T(8,128)(2,1)}, bf16[16,2,144,256]{3,2,1,0:T(8,128)(2,1)S(1)}, u32[]{:S(2)}, u32[]{:S(2)}) collective-permute-start(bf16[16,2,144,256]{3,2,1,0:T(8,128)(2,1)} %get-tuple-element.10), channel_id=1, source_target_pairs={{0,1},{1,0},{2,3},{3,2},{4,5},{5,4},{6,7},{7,6},{8,9},{9,8},{10,11... | collective-permute-start | bytes 7077896 | tf_op jit(solution)/shard_map/ppermute | solution.py:192
  48.2 6.4 %copy-start = (bf16[2,8,2,2,144,256]{5,4,3,2,1,0:T(8,128)(2,1)S(1)}, bf16[2,8,2,2,144,256]{5,4,3,2,1,0:T(8,128)(2,1)}, u32[]{:S(2)}) copy-start(bf16[2,8,2,2,144,256]{5,4,3,2,1,0:T(8,128)(2,1)} %shard_map.109) | copy-start | bytes 14155780
  56.1 10.1 %copy-start.3 = (s32[8,64]{1,0:T(8,128)S(1)}, s32[8,64]{1,0:T(8,128)}, u32[]{:S(2)}) copy-start(s32[8,64]{1,0:T(8,128)} %param.20) | copy-start | bytes 6148
  59.0 40.9 %all-to-all-start = ((bf16[16,2,144,256]{3,2,1,0:T(8,128)(2,1)}), bf16[16,2,144,256]{3,2,1,0:T(8,128)(2,1)S(1)}, u32[]{:S(2)}, u32[]{:S(2)}) async-start(bf16[16,2,144,256]{3,2,1,0:T(8,128)(2,1)} %select_convert_fusion), calls=%async_computation | async-start | bytes 4718592 | tf_op jit(solution)/shard_map/all_to_all | solution.py:212
  134.2 4.3 %collective-permute-start.1 = (bf16[16,16,32,128]{3,1,2,0:T(8,128)(2,1)S(1)}, bf16[16,16,32,128]{3,1,2,0:T(8,128)(2,1)}, u32[]{:S(2)}, u32[]{:S(2)}) collective-permute-start(bf16[16,16,32,128]{3,1,2,0:T(8,128)(2,1)S(1)} %all_to_all.15), channel_id=1, source_target_pairs={{0,1},{1,0},{2,3},{3,2},{4,5},{5,4},{6,7},{7,6},{8,9},{9,8},{10,11... | collective-permute-start | bytes 6291464 | tf_op jit(solution)/shard_map/ppermute | solution.py:245
  134.2 4.3 %copy-start.4 = (bf16[32,128,512]{2,1,0:T(8,128)(2,1)S(1)}, bf16[32,128,512]{2,1,0:T(8,128)(2,1)}, u32[]{:S(2)}) copy-start(bf16[32,128,512]{2,1,0:T(8,128)(2,1)} %param.21) | copy-start | bytes 12582916

commit v11 on v10

--- a/solution.py
+++ b/solution.py
@@ -188,8 +188,8 @@
     width = chunk * group_size
     parts = acc.reshape(pair, seq_size // pair, kv_dev, head_dim + 16, width)
     keep = lax.dynamic_index_in_dim(parts, core, 0, keepdims=False)
-    send = lax.dynamic_index_in_dim(parts, pair - 1 - core, 0, keepdims=False)
-    recv = lax.ppermute(send, "sc", [(i, (i + 1) % pair) for i in range(pair)])
+    recv = lax.ppermute(parts, "sc", [(i, (i + 1) % pair) for i in range(pair)])
+    recv = lax.dynamic_index_in_dim(recv, core, 0, keepdims=False)
     keep = keep.astype(jnp.float32)
     recv = recv.astype(jnp.float32)
     keep_top = keep[:, :, head_dim : head_dim + 1]

time: 163 us -> 163 us (level)
    squeeze x1 -> x0, other arithmetic: 6.09 us -> none  [local(): send = lax.dynamic_index_in_dim(parts, pair - 1 - core, 0, keepdims=False)]
    convert_element_type x0 -> x1, other arithmetic: none -> 2.24 us  [local(): keep = keep.astype(jnp.float32)]
    convert_element_type x1, other arithmetic: 0.57 us -> 2.24 us  [local(): recv = recv.astype(jnp.float32)]
    add x1, other arithmetic: 1.17 us -> 2.84 us  [local(): keep * jnp.exp(keep_top - pair_top) + recv * jnp.exp(recv_top - pair_top)]
  transfers between devices with their start and end apart: 3 -> 3, of which waited for: 3 -> 3; matrix products, arithmetic and copies ran while one was open for 5% -> 7% of each run, Pallas kernels for 0% -> 0%
where the time goes in v11:
time: 163 us
  blocking collectives  52.9 us (32%)
  waiting for transfers between devices  35.1 us (22%)
  Pallas kernels  33.5 us (21%)
  other arithmetic  13.1 us (8%)
  local copies, waits for them, and re-layouts  11.2 us (7%)
  matrix products  9.4 us (6%)
  starting transfers between devices  7.16 us (4%)
    pallas_call x1, Pallas kernels, context_part(): pl.pallas_call(context_kernel, grid_spec=grid_spec, out_shape=jax.ShapeDt...  33.5 us
    all_to_all x1, blocking collectives, local(): attention = lax.all_to_all(attention, ('sx', 'sy'), 0, 0, tiled=True)  32.4 us
    all_to_all x1, waiting for transfers between devices, local(): got = lax.all_to_all(sent, ('sx', 'sy'), 0, 0, tiled=True)  28.4 us
    all_to_all x1, blocking collectives, local(): return jnp.sum(lax.all_to_all(partial, 'heads', 0, 0, tiled=True), axis=0)  20.5 us
    all_to_all x1, starting transfers between devices, local(): got = lax.all_to_all(sent, ('sx', 'sy'), 0, 0, tiled=True)  7.16 us
    unnamed x19, local copies, waits for them, and re-layouts  7.11 us
    ppermute x1, waiting for transfers between devices, local(): recv = lax.ppermute(parts, 'sc', [(i, (i + 1) % pair) for i in range(pair)])  5.95 us
    dot_general x1, matrix products, local(): jnp.einsum('xshd,hde->xse', attention, out_weight, preferred_element_type...  3.57 us
  transfers between devices with their start and end apart: 3, of which 3 were waited for; matrix products, arithmetic and copies ran while one was open for 7% of the time, Pallas kernels for 0%

profile of v11, /device:TPU:0, one launch (start us, length us, event | category | flops | bytes accessed | tf_op | source)
XLA Modules:
  0.0 162.7 jit_solution(1842048689358409998)
XLA Ops:
  0.0 0.0 copy-start.1
  0.0 0.0 copy-start.2
  0.0 0.0 copy-start.5
  0.0 2.5 %copy.139 = bf16[8,256,2,128]{3,1,2,0:T(8,128)(2,1)} copy(bf16[8,256,2,128]{3,2,1,0:T(2,128)(2,1)} %param.15) | data formatting | bytes 2097152 | tf_op args[4]
  2.5 3.6 %copy.86 = bf16[8,256,2,128]{1,3,2,0:T(8,128)(2,1)} copy(bf16[8,256,2,128]{3,2,1,0:T(2,128)(2,1)} %param.16) | data formatting | bytes 2097152 | tf_op args[5]
  6.2 0.0 copy-done.1
  6.2 0.8 copy.82
  7.0 0.0 copy-done.2
  7.0 1.1 copy.84
  8.1 0.0 copy-done.5
  8.1 0.5 subtract_clamp_fusion.len_ref
  8.6 33.5 %shard_map.109 = bf16[2,8,2,2,144,256]{5,4,3,2,1,0:T(8,128)(2,1)} custom-call(s32[8,6]{1,0:T(8,128)} %use_ref.1, s32[8]{0:T(128)} %subtract_clamp_fusion.len_ref, bf16[8,64,32,128]{3,2,1,0:T(8,128)(2,1)} %q_ref.1, bf16[2,768,128]{2,1,0:T(8,128)(2,1)} %bitcast.137, bf16[2,128,768]{2,1,0:T(8,128)(2,1)} %bitcast.138, bf16[8,2,256,128]{3,2,1,0:T(8,128)(2,1)} %bitcast.135, ...), custom_call_target="tpu_custom_call" | custom-call | tf_op jit(solution)/shard_map/pallas_call | solution.py:137
  42.1 0.0 collective-permute-start
  42.2 2.2 %bitcast_convert_fusion.1 = f32[16,2,144,256]{3,2,1,0:T(8,128)S(1)} fusion(bf16[2,16,2,144,256]{4,3,2,1,0:T(8,128)(2,1)} %bitcast.131, s32[]{:T(128)S(6)} %select_n.68), kind=kLoop, calls=%fused_computation.8 | loop fusion | flops 1179648 | bytes 7077892 | tf_op jit(solution)/shard_map/convert_element_type | solution.py:193
  44.4 0.0 copy-start
  44.4 6.0 %collective-permute-done = bf16[2,16,2,144,256]{4,3,2,1,0:T(8,128)(2,1)} collective-permute-done((bf16[2,16,2,144,256]{4,3,2,1,0:T(8,128)(2,1)}, bf16[2,16,2,144,256]{4,3,2,1,0:T(8,128)(2,1)}, u32[]{:S(2)}, u32[]{:S(2)}) %collective-permute-start) | collective-permute-done | bytes 4718624 | tf_op jit(solution)/shard_map/ppermute | solution.py:191
  50.4 2.2 %bitcast_convert_fusion = f32[16,2,144,256]{3,2,1,0:T(8,128)S(1)} fusion(bf16[2,16,2,144,256]{4,3,2,1,0:T(8,128)(2,1)} %collective-permute-done, s32[]{:T(128)S(6)} %select_n.68), kind=kLoop, calls=%fused_computation.7 | loop fusion | flops 1179648 | bytes 7077892 | tf_op jit(solution)/shard_map/convert_element_type | solution.py:194
  52.6 0.1 subtract_exponential_fusion.1
  52.7 0.1 subtract_exponential_fusion
  52.8 0.0 copy-done
  52.8 2.8 %multiply_add_fusion = f32[16,2,144,256]{3,2,1,0:T(8,128)S(1)} fusion(f32[16,2,256]{2,1,0:T(2,128)S(1)} %get-tuple-element.16, f32[16,2,256]{2,1,0:T(2,128)S(1)} %get-tuple-element.17, bf16[2,16,2,144,256]{4,3,2,1,0:T(8,128)(2,1)S(1)} %bitcast.132, s32[]{:T(128)S(6)} %select_n.68, bf16[2,16,2,144,256]{4,3,2,1,0:T(8,128)(2,1)} %collective-permute-done), kind=kLoop, calls=%fused_computation.1 | loop fusion | flops 5898240 | bytes 9502724 | tf_op jit(solution)/shard_map/add | solution.py:198
  55.7 0.1 fusion.39
  55.7 0.1 convert_convert_fusion
  55.9 0.0 copy-start.3
  55.9 3.0 %select_convert_fusion = bf16[16,2,144,256]{3,2,1,0:T(8,128)(2,1)} fusion(f32[16,2,144,256]{3,2,1,0:T(8,128)S(1)} %multiply_add_fusion, bf16[16,2,256]{2,1,0:T(2,128)(2,1)S(1)} %bitcast.144, bf16[16,2,256]{2,1,0:T(2,128)(2,1)S(1)} %bitcast.145, bf16[16,2,256]{2,1,0:T(2,128)(2,1)S(1)} %bitcast.143, pred[144]{0:T(512)(128)(4,1)S(1)} %get-tuple-element.18, ...), kind=kLoop, calls=%fused_computation | loop fusion | flops 4718592 | bytes 7127616 | tf_op jit(solution)/shard_map/convert_element_type | solution.py:211
  58.8 7.2 %all-to-all-start = ((bf16[16,2,144,256]{3,2,1,0:T(8,128)(2,1)}), bf16[16,2,144,256]{3,2,1,0:T(8,128)(2,1)S(1)}, u32[]{:S(2)}, u32[]{:S(2)}) async-start(bf16[16,2,144,256]{3,2,1,0:T(8,128)(2,1)} %select_convert_fusion), calls=%async_computation | async-start | bytes 4718592 | tf_op jit(solution)/shard_map/all_to_all | solution.py:212
  66.0 0.0 copy-done.3
  66.0 0.5 convolution_minimum_fusion.4
  66.5 0.4 convolution_minimum_fusion.3
  66.9 0.4 convolution_minimum_fusion.2
  67.3 0.4 convolution_minimum_fusion.1
  67.7 0.4 convolution_minimum_fusion
  68.1 0.4 fusion.51
  68.5 0.8 constant_dynamic-slice_fusion
  69.3 0.9 constant_dynamic-slice_fusion.1
  70.3 0.3 fusion.48
  70.6 0.2 fusion.17
  70.9 0.1 squeeze_reshape.11
  70.9 0.1 squeeze_reshape.9
  71.0 0.3 convolution_bitcast_fusion
  71.3 28.4 %all-to-all-done = bf16[16,2,144,256]{3,2,1,0:T(8,128)(2,1)S(1)} async-done(((bf16[16,2,144,256]{3,2,1,0:T(8,128)(2,1)}), bf16[16,2,144,256]{3,2,1,0:T(8,128)(2,1)S(1)}, u32[]{:S(2)}, u32[]{:S(2)}) %all-to-all-start) | async-done | bytes 2359328 | tf_op jit(solution)/shard_map/all_to_all | solution.py:212
  99.7 0.1 fusion.47
  99.8 0.1 reshape.174
  99.9 0.1 fusion.32
  100.0 0.1 fusion.37
  100.0 0.1 reshape.164
  100.1 0.1 reshape.165
  100.2 0.1 reshape.170
  100.3 0.4 multiply_reduce_fusion
  100.7 0.1 copy.88
  100.9 0.3 fusion.14
  101.2 0.1 copy.98
  101.2 0.4 broadcast_in_dim.80
  101.6 32.4 %all_to_all.15 = bf16[16,16,32,128]{3,1,2,0:T(8,128)(2,1)S(1)} all-to-all(bf16[16,16,32,128]{3,1,2,0:T(8,128)(2,1)S(1)} %broadcast_in_dim.80), channel_id=1, replica_groups=mesh['heads'=4,'sx'=4,'sy'=4,'sc'=2] {'sx','sy'}, dimensions={0} | all-to-all | bytes 4194304 | tf_op jit(solution)/shard_map/all_to_all | solution.py:244
  134.1 0.0 collective-permute-start.1
  134.1 0.0 copy-start.4
  134.1 3.6 %fusion.4 = f32[16,16,512]{2,1,0:T(8,128)S(1)} fusion(bf16[16,16,32,128]{3,1,2,0:T(8,128)(2,1)S(1)} %all_to_all.15, bf16[32,128,512]{2,1,0:T(8,128)(2,1)} %param.21), kind=kOutput, calls=%fused_computation.9 | convolution fusion | flops 1073741824 | bytes 6815744 | tf_op jit(solution)/shard_map/xshd,hde->xse/dot_general | solution.py:246
  137.6 0.7 collective-permute-done.1
  138.3 0.0 copy-done.4
  138.3 2.9 %select_bitcast_fusion.1 = (f32[16,1,16,512]{3,2,0,1:T(8,128)S(1)}, f32[16,1,16,512]{3,2,0,1:T(8,128)S(1)}) fusion(f32[16,16,512]{2,1,0:T(8,128)S(1)} %fusion.4, pred[]{:T(512)S(6)} %eq.54, bf16[16,16,32,128]{3,1,2,0:T(8,128)(2,1)} %collective-permute-done.1, bf16[32,128,512]{2,1,0:T(8,128)(2,1)S(1)} %copy-done.4), kind=kOutput, calls=%fused_computation.23 | convolution fusion | flops 1074003968 | bytes 7864321 | tf_op jit(solution)/shard_map/xshd,hde->xse/dot_general | solution.py:247
  141.2 0.1 pad_maximum_fusion
  141.3 0.1 copy.99
  141.4 20.5 %all_to_all.16 = f32[4,2,64,512]{3,2,1,0:T(8,128)S(1)} all-to-all(f32[4,2,64,512]{3,2,1,0:T(8,128)S(1)} %bitcast.134), channel_id=1, replica_groups=mesh['heads'=4,'sx'=4,'sy'=4,'sc'=2] {'heads'}, dimensions={0} | all-to-all | bytes 2097152 | tf_op jit(solution)/shard_map/all_to_all | solution.py:253
  161.9 0.8 reduce_sum.39
  (17 shorter events, 0.3 us)
Async XLA Ops:
  0.0 6.2 %copy-start.1 = (bf16[6,128,2,128]{3,2,1,0:T(2,128)(2,1)S(1)}, bf16[6,128,2,128]{3,2,1,0:T(2,128)(2,1)}, u32[]{:S(2)}) copy-start(bf16[6,128,2,128]{3,2,1,0:T(2,128)(2,1)} %param.12) | copy-start | bytes 1179652
  0.0 7.0 %copy-start.2 = (bf16[6,128,2,128]{3,2,1,0:T(2,128)(2,1)S(1)}, bf16[6,128,2,128]{3,2,1,0:T(2,128)(2,1)}, u32[]{:S(2)}) copy-start(bf16[6,128,2,128]{3,2,1,0:T(2,128)(2,1)} %param.13) | copy-start | bytes 1179652
  0.0 8.1 %copy-start.5 = (s32[8]{0:T(128)S(1)}, s32[8]{0:T(128)}, u32[]{:S(2)}) copy-start(s32[8]{0:T(128)} %param.17) | copy-start | bytes 100
  42.1 8.3 %collective-permute-start = (bf16[2,16,2,144,256]{4,3,2,1,0:T(8,128)(2,1)}, bf16[2,16,2,144,256]{4,3,2,1,0:T(8,128)(2,1)}, u32[]{:S(2)}, u32[]{:S(2)}) collective-permute-start(bf16[2,16,2,144,256]{4,3,2,1,0:T(8,128)(2,1)} %bitcast.130), channel_id=1, source_target_pairs={{0,1},{1,0},{2,3},{3,2},{4,5},{5,4},{6,7},{7,6},{8,9},{9,8},{10,11... | collective-permute-start | bytes 14155784 | tf_op jit(solution)/shard_map/ppermute | solution.py:191
  44.4 8.4 %copy-start = (bf16[2,8,2,2,144,256]{5,4,3,2,1,0:T(8,128)(2,1)S(1)}, bf16[2,8,2,2,144,256]{5,4,3,2,1,0:T(8,128)(2,1)}, u32[]{:S(2)}) copy-start(bf16[2,8,2,2,144,256]{5,4,3,2,1,0:T(8,128)(2,1)} %shard_map.109) | copy-start | bytes 14155780
  55.9 10.1 %copy-start.3 = (s32[8,64]{1,0:T(8,128)S(1)}, s32[8,64]{1,0:T(8,128)}, u32[]{:S(2)}) copy-start(s32[8,64]{1,0:T(8,128)} %param.20) | copy-start | bytes 6148
  58.8 40.9 %all-to-all-start = ((bf16[16,2,144,256]{3,2,1,0:T(8,128)(2,1)}), bf16[16,2,144,256]{3,2,1,0:T(8,128)(2,1)S(1)}, u32[]{:S(2)}, u32[]{:S(2)}) async-start(bf16[16,2,144,256]{3,2,1,0:T(8,128)(2,1)} %select_convert_fusion), calls=%async_computation | async-start | bytes 4718592 | tf_op jit(solution)/shard_map/all_to_all | solution.py:212
  134.1 4.3 %collective-permute-start.1 = (bf16[16,16,32,128]{3,1,2,0:T(8,128)(2,1)S(1)}, bf16[16,16,32,128]{3,1,2,0:T(8,128)(2,1)}, u32[]{:S(2)}, u32[]{:S(2)}) collective-permute-start(bf16[16,16,32,128]{3,1,2,0:T(8,128)(2,1)S(1)} %all_to_all.15), channel_id=1, source_target_pairs={{0,1},{1,0},{2,3},{3,2},{4,5},{5,4},{6,7},{7,6},{8,9},{9,8},{10,11... | collective-permute-start | bytes 6291464 | tf_op jit(solution)/shard_map/ppermute | solution.py:245
  134.1 4.3 %copy-start.4 = (bf16[32,128,512]{2,1,0:T(8,128)(2,1)S(1)}, bf16[32,128,512]{2,1,0:T(8,128)(2,1)}, u32[]{:S(2)}) copy-start(bf16[32,128,512]{2,1,0:T(8,128)(2,1)} %param.21) | copy-start | bytes 12582916

commit v12 on v7

--- a/solution.py
+++ b/solution.py
@@ -144,6 +144,52 @@
 
 
 SEQ = ("sx", "sy", "sc")
+
+
+def pair_kernel(core_ref, keep_ref, recv_ref, out_ref):
+    head_dim = out_ref.shape[-2] - 16
+    for i in range(out_ref.shape[0]):
+        for k in range(out_ref.shape[1]):
+            keep = keep_ref[0, i, k].astype(jnp.float32)
+            recv = recv_ref[0, i, k].astype(jnp.float32)
+            keep_top = keep[head_dim : head_dim + 1]
+            recv_top = recv[head_dim : head_dim + 1]
+            pair_top = jnp.maximum(keep_top, recv_top)
+            scaled = keep * jnp.exp(keep_top - pair_top) + recv * jnp.exp(recv_top - pair_top)
+            totals = scaled[head_dim + 1 : head_dim + 2] + scaled[head_dim + 2 : head_dim + 3]
+            high = totals.astype(jnp.bfloat16).astype(jnp.float32)
+            low = totals - high
+            row = lax.broadcasted_iota(jnp.int32, scaled.shape, 0)
+            sent = jnp.where(
+                row < head_dim,
+                scaled,
+                jnp.where(
+                    row == head_dim,
+                    pair_top,
+                    jnp.where(row == head_dim + 1, high, jnp.where(row == head_dim + 2, low, 0.0)),
+                ),
+            )
+            out_ref[i, k] = sent.astype(out_ref.dtype)
+
+
+def pair_combine(core, parts, recv, steps):
+    pair, chunks, kv_dev, rows, width = parts.shape
+    per = chunks // steps
+    block = (1, per, kv_dev, rows, width)
+    grid_spec = pltpu.PrefetchScalarGridSpec(
+        num_scalar_prefetch=1,
+        grid=(steps,),
+        in_specs=[
+            pl.BlockSpec(block, lambda g, c: (c[0], g, 0, 0, 0)),
+            pl.BlockSpec(block, lambda g, c: (c[0], g, 0, 0, 0)),
+        ],
+        out_specs=pl.BlockSpec((per, kv_dev, rows, width), lambda g, c: (g, 0, 0, 0)),
+    )
+    return pl.pallas_call(
+        pair_kernel,
+        grid_spec=grid_spec,
+        out_shape=jax.ShapeDtypeStruct((chunks, kv_dev, rows, width), parts.dtype),
+    )(core.reshape(1).astype(jnp.int32), parts, recv)
 
 
 def unpack(parts, head_dim, axis):
@@ -187,24 +233,8 @@
     )
     width = chunk * group_size
     parts = acc.reshape(pair, seq_size // pair, kv_dev, head_dim + 16, width)
-    parts = lax.all_to_all(parts, "sc", 0, 0, tiled=True).astype(jnp.float32)
-    part_top = parts[:, :, :, head_dim : head_dim + 1]
-    pair_top = jnp.max(part_top, axis=0)
-    factor = jnp.exp(part_top - pair_top[None])
-    scaled = jnp.sum(parts * factor, axis=0)
-    pair_totals = scaled[:, :, head_dim + 1 : head_dim + 2] + scaled[:, :, head_dim + 2 : head_dim + 3]
-    high = pair_totals.astype(jnp.bfloat16).astype(jnp.float32)
-    low = pair_totals - high
-    row = lax.broadcasted_iota(jnp.int32, scaled.shape, 2)
-    sent = jnp.where(
-        row < head_dim,
-        scaled,
-        jnp.where(
-            row == head_dim,
-            pair_top,
-            jnp.where(row == head_dim + 1, high, jnp.where(row == head_dim + 2, low, 0.0)),
-        ),
-    ).astype(jnp.bfloat16)
+    recv = lax.ppermute(parts, "sc", [(i, (i + 1) % pair) for i in range(pair)])
+    sent = pair_combine(core, parts, recv, 4)
     got = lax.all_to_all(sent, ("sx", "sy"), 0, 0, tiled=True)
     part_top, part_totals, part_weighted = unpack(got, head_dim, 0)
     top_all = jnp.max(part_top, axis=0)

time: 163 us -> 160 us (0.982)
  blocking collectives: 61.8 us -> 52.9 us
  waiting for transfers between devices: 29.1 us -> 37.4 us
  Pallas kernels: 33.5 us -> 38.3 us
  other arithmetic: 6.88 us -> 2.64 us
  local copies, waits for them, and re-layouts: 14.5 us -> 11.2 us
    all_to_all x1 -> x0, blocking collectives: 8.93 us -> none  [local(): parts = lax.all_to_all(parts, 'sc', 0, 0, tiled=True).astype(jnp.float32)]
    ppermute x0 -> x1, waiting for transfers between devices: none -> 8.24 us  [local(): recv = lax.ppermute(parts, 'sc', [(i, (i + 1) % pair) for i in range(pair)])]
    pallas_call x0 -> x1, Pallas kernels: none -> 4.76 us  [pair_combine(): pl.pallas_call(pair_kernel, grid_spec=grid_spec, out_shape=jax.ShapeDtype...]
    convert_element_type x1 -> x0, local copies, waits for them, and re-layouts: 3.54 us -> none  [local(): sent = jnp.where(row < head_dim, scaled, jnp.where(row == head_dim, pair_...]
    convert_element_type x3 -> x0, other arithmetic: 2.72 us -> none  [the longest x1 1.41 us: local(): sent = jnp.where(row < head_dim, scaled, jnp.where(row == head_dim, pair_...]
    unnamed x17 -> x11, local copies, waits for them, and re-layouts: 5.43 us -> 6.3 us
  transfers between devices with their start and end apart: 2 -> 3, of which waited for: 2 -> 3; matrix products, arithmetic and copies ran while one was open for 5% -> 6% of each run, Pallas kernels for 0% -> 0%
where the time goes in v12:
time: 160 us; the launch traced here: 159 us
  blocking collectives  52.9 us (33%)
  Pallas kernels  38.3 us (24%)
  waiting for transfers between devices  37.4 us (23%)
  local copies, waits for them, and re-layouts  11.2 us (7%)
  matrix products  9.41 us (6%)
  starting transfers between devices  7.28 us (5%)
  other arithmetic  2.64 us (2%)
    pallas_call x1, Pallas kernels, context_part(): pl.pallas_call(context_kernel, grid_spec=grid_spec, out_shape=jax.ShapeDt...  33.5 us
    all_to_all x1, blocking collectives, local(): attention = lax.all_to_all(attention, ('sx', 'sy'), 0, 0, tiled=True)  32.4 us
    all_to_all x1, waiting for transfers between devices, local(): got = lax.all_to_all(sent, ('sx', 'sy'), 0, 0, tiled=True)  28.4 us
    all_to_all x1, blocking collectives, local(): return jnp.sum(lax.all_to_all(partial, 'heads', 0, 0, tiled=True), axis=0)  20.5 us
    ppermute x1, waiting for transfers between devices, local(): recv = lax.ppermute(parts, 'sc', [(i, (i + 1) % pair) for i in range(pair)])  8.24 us
    all_to_all x1, starting transfers between devices, local(): got = lax.all_to_all(sent, ('sx', 'sy'), 0, 0, tiled=True)  7.27 us
    unnamed x11, local copies, waits for them, and re-layouts  6.3 us
    pallas_call x1, Pallas kernels, pair_combine(): pl.pallas_call(pair_kernel, grid_spec=grid_spec, out_shape=jax.ShapeDtype...  4.76 us
  transfers between devices with their start and end apart: 3, of which 3 were waited for; matrix products, arithmetic and copies ran while one was open for 6% of the time, Pallas kernels for 0%

profile of v12, /device:TPU:0, one launch (start us, length us, event | category | flops | bytes accessed | tf_op | source)
XLA Modules:
  0.0 159.4 jit_solution(14256306186709792222)
XLA Ops:
  0.0 0.0 copy-start
  0.0 1.9 %copy.66 = bf16[6,128,2,128]{3,1,0,2:T(8,128)(2,1)} copy(bf16[6,128,2,128]{3,2,1,0:T(2,128)(2,1)} %param.12) | data formatting | bytes 786432 | tf_op args[1]
  1.9 0.0 copy-start.3
  1.9 1.9 %copy.68 = bf16[768,2,128]{0,2,1:T(8,128)(2,1)} copy(bf16[768,2,128]{2,1,0:T(2,128)(2,1)} %bitcast.119) | data formatting | bytes 786432 | tf_op jit(solution)/shard_map/reshape | solution.py:119
  3.8 2.5 %copy.113 = bf16[8,256,2,128]{3,1,2,0:T(8,128)(2,1)} copy(bf16[8,256,2,128]{3,2,1,0:T(2,128)(2,1)} %param.15) | data formatting | bytes 2097152 | tf_op args[4]
  6.3 0.0 copy-done
  6.3 1.9 %copy.70 = bf16[8,256,2,128]{1,3,2,0:T(8,128)(2,1)} copy(bf16[8,256,2,128]{3,2,1,0:T(2,128)(2,1)S(1)} %copy-done) | data formatting | bytes 2097152 | tf_op args[5]
  8.2 0.0 copy-done.3
  8.2 0.6 subtract_clamp_fusion.len_ref
  8.8 33.5 %shard_map.109 = bf16[2,8,2,2,144,256]{5,4,3,2,1,0:T(8,128)(2,1)} custom-call(s32[8,6]{1,0:T(8,128)} %use_ref.1, s32[8]{0:T(128)} %subtract_clamp_fusion.len_ref, bf16[8,64,32,128]{3,2,1,0:T(8,128)(2,1)} %q_ref.1, bf16[2,768,128]{2,1,0:T(8,128)(2,1)} %bitcast.114, bf16[2,128,768]{2,1,0:T(8,128)(2,1)} %bitcast.115, bf16[8,2,256,128]{3,2,1,0:T(8,128)(2,1)} %bitcast.112, ...), custom_call_target="tpu_custom_call" | custom-call | tf_op jit(solution)/shard_map/pallas_call | solution.py:137
  42.4 0.0 collective-permute-start
  42.4 8.2 %collective-permute-done.recv_ref = bf16[2,16,2,144,256]{4,3,2,1,0:T(8,128)(2,1)} collective-permute-done((bf16[2,16,2,144,256]{4,3,2,1,0:T(8,128)(2,1)}, bf16[2,16,2,144,256]{4,3,2,1,0:T(8,128)(2,1)}, u32[]{:S(2)}, u32[]{:S(2)}) %collective-permute-start) | collective-permute-done | bytes 4718624 | tf_op jit(solution)/shard_map/ppermute | solution.py:236
  50.6 4.8 %shard_map.110 = bf16[16,2,144,256]{3,2,1,0:T(8,128)(2,1)} custom-call(s32[1]{0:T(128)} %bitcast.core_ref, bf16[2,16,2,144,256]{4,3,2,1,0:T(8,128)(2,1)} %bitcast.109, bf16[2,16,2,144,256]{4,3,2,1,0:T(8,128)(2,1)} %collective-permute-done.recv_ref), custom_call_target="tpu_custom_call" | custom-call | tf_op jit(solution)/shard_map/pallas_call | solution.py:188
  55.4 0.0 copy-start.1
  55.4 7.3 %all-to-all-start = ((bf16[16,2,144,256]{3,2,1,0:T(8,128)(2,1)}), bf16[16,2,144,256]{3,2,1,0:T(8,128)(2,1)S(1)}, u32[]{:S(2)}, u32[]{:S(2)}) async-start(bf16[16,2,144,256]{3,2,1,0:T(8,128)(2,1)} %shard_map.110), calls=%async_computation | async-start | bytes 4718592 | tf_op jit(solution)/shard_map/all_to_all | solution.py:238
  62.7 0.0 copy-done.1
  62.7 0.5 convolution_minimum_fusion.4
  63.2 0.4 convolution_minimum_fusion.3
  63.6 0.4 convolution_minimum_fusion.2
  64.0 0.4 convolution_minimum_fusion.1
  64.4 0.4 convolution_minimum_fusion
  64.8 0.4 fusion.50
  65.2 0.8 constant_dynamic-slice_fusion
  66.0 0.9 constant_dynamic-slice_fusion.1
  66.9 0.3 fusion.47
  67.2 0.3 convolution_bitcast_fusion
  67.5 0.2 fusion.17
  67.8 0.1 squeeze_reshape.11
  67.9 0.1 squeeze_reshape.9
  68.0 28.4 %all-to-all-done = bf16[16,2,144,256]{3,2,1,0:T(8,128)(2,1)S(1)} async-done(((bf16[16,2,144,256]{3,2,1,0:T(8,128)(2,1)}), bf16[16,2,144,256]{3,2,1,0:T(8,128)(2,1)S(1)}, u32[]{:S(2)}, u32[]{:S(2)}) %all-to-all-start) | async-done | bytes 2359328 | tf_op jit(solution)/shard_map/all_to_all | solution.py:238
  96.4 0.1 fusion.46
  96.5 0.1 reshape.172
  96.6 0.4 multiply_reduce_fusion
  97.0 0.1 copy.72
  97.2 0.1 fusion.32
  97.2 0.1 fusion.37
  97.3 0.1 reshape.164
  97.4 0.1 reshape.165
  97.5 0.1 reshape.168
  97.6 0.3 fusion.14
  97.8 0.1 copy.82
  97.9 0.4 broadcast_in_dim.42
  98.3 32.4 %all_to_all.15 = bf16[16,16,32,128]{3,1,2,0:T(8,128)(2,1)S(1)} all-to-all(bf16[16,16,32,128]{3,1,2,0:T(8,128)(2,1)S(1)} %broadcast_in_dim.42), channel_id=1, replica_groups=mesh['heads'=4,'sx'=4,'sy'=4,'sc'=2] {'sx','sy'}, dimensions={0} | all-to-all | bytes 4194304 | tf_op jit(solution)/shard_map/all_to_all | solution.py:270
  130.7 0.0 collective-permute-start.1
  130.7 0.0 copy-start.2
  130.7 3.6 %fusion.4 = f32[16,16,512]{2,1,0:T(8,128)S(1)} fusion(bf16[16,16,32,128]{3,1,2,0:T(8,128)(2,1)S(1)} %all_to_all.15, bf16[32,128,512]{2,1,0:T(8,128)(2,1)} %param.21), kind=kOutput, calls=%fused_computation.5 | convolution fusion | flops 1073741824 | bytes 6815744 | tf_op jit(solution)/shard_map/xshd,hde->xse/dot_general | solution.py:272
  134.3 0.7 collective-permute-done.1
  135.0 0.0 copy-done.2
  135.0 2.9 %select_bitcast_fusion.1 = (f32[16,1,16,512]{3,2,0,1:T(8,128)S(1)}, f32[16,1,16,512]{3,2,0,1:T(8,128)S(1)}) fusion(f32[16,16,512]{2,1,0:T(8,128)S(1)} %fusion.4, pred[]{:T(512)S(6)} %eq.36, bf16[16,16,32,128]{3,1,2,0:T(8,128)(2,1)} %collective-permute-done.1, bf16[32,128,512]{2,1,0:T(8,128)(2,1)S(1)} %copy-done.2), kind=kOutput, calls=%fused_computation.19 | convolution fusion | flops 1074003968 | bytes 7864321 | tf_op jit(solution)/shard_map/xshd,hde->xse/dot_general | solution.py:273
  137.9 0.1 pad_maximum_fusion
  138.0 0.1 copy.83
  138.1 20.5 %all_to_all.16 = f32[4,2,64,512]{3,2,1,0:T(8,128)S(1)} all-to-all(f32[4,2,64,512]{3,2,1,0:T(8,128)S(1)} %bitcast.111), channel_id=1, replica_groups=mesh['heads'=4,'sx'=4,'sy'=4,'sc'=2] {'heads'}, dimensions={0} | all-to-all | bytes 2097152 | tf_op jit(solution)/shard_map/all_to_all | solution.py:279
  158.6 0.8 reduce_sum.39
  (11 shorter events, 0.2 us)
Async XLA Ops:
  0.0 6.3 %copy-start = (bf16[8,256,2,128]{3,2,1,0:T(2,128)(2,1)S(1)}, bf16[8,256,2,128]{3,2,1,0:T(2,128)(2,1)}, u32[]{:S(2)}) copy-start(bf16[8,256,2,128]{3,2,1,0:T(2,128)(2,1)} %param.16) | copy-start | bytes 3145732
  1.9 6.3 %copy-start.3 = (s32[8]{0:T(128)S(1)}, s32[8]{0:T(128)}, u32[]{:S(2)}) copy-start(s32[8]{0:T(128)} %param.17) | copy-start | bytes 100
  42.4 8.3 %collective-permute-start = (bf16[2,16,2,144,256]{4,3,2,1,0:T(8,128)(2,1)}, bf16[2,16,2,144,256]{4,3,2,1,0:T(8,128)(2,1)}, u32[]{:S(2)}, u32[]{:S(2)}) collective-permute-start(bf16[2,16,2,144,256]{4,3,2,1,0:T(8,128)(2,1)} %bitcast.108), channel_id=1, source_target_pairs={{0,1},{1,0},{2,3},{3,2},{4,5},{5,4},{6,7},{7,6},{8,9},{9,8},{10,11... | collective-permute-start | bytes 14155784 | tf_op jit(solution)/shard_map/ppermute | solution.py:236
  55.4 7.3 %copy-start.1 = (s32[8,64]{1,0:T(8,128)S(1)}, s32[8,64]{1,0:T(8,128)}, u32[]{:S(2)}) copy-start(s32[8,64]{1,0:T(8,128)} %param.20) | copy-start | bytes 6148
  55.4 41.0 %all-to-all-start = ((bf16[16,2,144,256]{3,2,1,0:T(8,128)(2,1)}), bf16[16,2,144,256]{3,2,1,0:T(8,128)(2,1)S(1)}, u32[]{:S(2)}, u32[]{:S(2)}) async-start(bf16[16,2,144,256]{3,2,1,0:T(8,128)(2,1)} %shard_map.110), calls=%async_computation | async-start | bytes 4718592 | tf_op jit(solution)/shard_map/all_to_all | solution.py:238
  130.7 4.3 %collective-permute-start.1 = (bf16[16,16,32,128]{3,1,2,0:T(8,128)(2,1)S(1)}, bf16[16,16,32,128]{3,1,2,0:T(8,128)(2,1)}, u32[]{:S(2)}, u32[]{:S(2)}) collective-permute-start(bf16[16,16,32,128]{3,1,2,0:T(8,128)(2,1)S(1)} %all_to_all.15), channel_id=1, source_target_pairs={{0,1},{1,0},{2,3},{3,2},{4,5},{5,4},{6,7},{7,6},{8,9},{9,8},{10,11... | collective-permute-start | bytes 6291464 | tf_op jit(solution)/shard_map/ppermute | solution.py:271
  130.7 4.3 %copy-start.2 = (bf16[32,128,512]{2,1,0:T(8,128)(2,1)S(1)}, bf16[32,128,512]{2,1,0:T(8,128)(2,1)}, u32[]{:S(2)}) copy-start(bf16[32,128,512]{2,1,0:T(8,128)(2,1)} %param.21) | copy-start | bytes 12582916

commit v13 on v12

--- a/solution.py
+++ b/solution.py
@@ -58,7 +58,7 @@
     )
 
 
-def context_kernel(use_ref, len_ref, q_ref, kp_ref, vp_ref, ko_ref, vo_ref, acc_ref):
+def context_kernel(use_ref, len_ref, core_ref, q_ref, kp_ref, vp_ref, ko_ref, vo_ref, mine_ref, theirs_ref):
     r = pl.program_id(1)
     scaling = 1.0 / math.sqrt(q_ref.shape[-1])
     q = q_ref[0].reshape(-1, q_ref.shape[-1])
@@ -89,25 +89,27 @@
         vo_ref[0, 0], w_own.astype(jnp.bfloat16), preferred_element_type=jnp.float32
     )
     head_dim = acc.shape[0]
-    pieces = acc_ref.shape[0] * acc_ref.shape[2]
-    width = acc_ref.shape[-1]
-    extra = acc_ref.shape[-2] - head_dim
+    pair = 2
+    pieces = mine_ref.shape[1] * pair
+    width = mine_ref.shape[-1]
+    extra = mine_ref.shape[-2] - head_dim
     high = totals.astype(jnp.bfloat16).astype(jnp.float32)
     low = totals - high
     row_id = lax.broadcasted_iota(jnp.int32, (extra, totals.shape[1]), 0)
     stats = jnp.where(row_id == 0, top, jnp.where(row_id == 1, high, jnp.where(row_id == 2, low, 0.0)))
-    pair = acc_ref.shape[0]
+    core = core_ref[0]
     for c in range(pieces):
-        spot = (c % pair, 0, c // pair, 0)
-        acc_ref[spot + (slice(0, head_dim),)] = acc[:, c * width : (c + 1) * width].astype(
-            acc_ref.dtype
-        )
-        acc_ref[spot + (slice(head_dim, None),)] = stats[:, c * width : (c + 1) * width].astype(
-            acc_ref.dtype
-        )
-
-
-def context_part(queries, prefix_keys, prefix_values, use_rows, own_lengths, own_keys, own_values, pieces, pair):
+        body = acc[:, c * width : (c + 1) * width].astype(mine_ref.dtype)
+        tail = stats[:, c * width : (c + 1) * width].astype(mine_ref.dtype)
+        for half, ref in ((0, mine_ref), (1, theirs_ref)):
+
+            @pl.when((core == c % pair) == (half == 0))
+            def _():
+                ref[0, c // pair, 0, 0:head_dim, :] = body
+                ref[0, c // pair, 0, head_dim:, :] = tail
+
+
+def context_part(queries, prefix_keys, prefix_values, use_rows, own_lengths, own_keys, own_values, pieces, pair, core):
     requests, tree_size, heads_dev, head_dim = queries.shape
     block_count, block_len, kv_dev, _ = prefix_keys.shape
     group_size = heads_dev // kv_dev
@@ -120,76 +122,74 @@
     ko = jnp.transpose(own_keys, (0, 2, 1, 3))
     vo = jnp.transpose(own_values, (0, 2, 3, 1))
     grid_spec = pltpu.PrefetchScalarGridSpec(
-        num_scalar_prefetch=2,
+        num_scalar_prefetch=3,
         grid=(kv_dev, requests),
         in_specs=[
-            pl.BlockSpec((1, tree_size, group_size, head_dim), lambda k, r, u, n: (r, 0, k, 0)),
-            pl.BlockSpec((1, n_pre, head_dim), lambda k, r, u, n: (k, 0, 0)),
-            pl.BlockSpec((1, head_dim, n_pre), lambda k, r, u, n: (k, 0, 0)),
-            pl.BlockSpec((1, 1, private_dev, head_dim), lambda k, r, u, n: (r, k, 0, 0)),
-            pl.BlockSpec((1, 1, head_dim, private_dev), lambda k, r, u, n: (r, k, 0, 0)),
+            pl.BlockSpec((1, tree_size, group_size, head_dim), lambda k, r, u, n, c: (r, 0, k, 0)),
+            pl.BlockSpec((1, n_pre, head_dim), lambda k, r, u, n, c: (k, 0, 0)),
+            pl.BlockSpec((1, head_dim, n_pre), lambda k, r, u, n, c: (k, 0, 0)),
+            pl.BlockSpec((1, 1, private_dev, head_dim), lambda k, r, u, n, c: (r, k, 0, 0)),
+            pl.BlockSpec((1, 1, head_dim, private_dev), lambda k, r, u, n, c: (r, k, 0, 0)),
         ],
-        out_specs=pl.BlockSpec(
-            (pair, 1, pieces // pair, 1, head_dim + 16, width),
-            lambda k, r, u, n: (0, r, 0, k, 0, 0),
-        ),
+        out_specs=[
+            pl.BlockSpec((1, pieces // pair, 1, head_dim + 16, width), lambda k, r, u, n, c: (r, 0, k, 0, 0)),
+            pl.BlockSpec((1, pieces // pair, 1, head_dim + 16, width), lambda k, r, u, n, c: (r, 0, k, 0, 0)),
+        ],
     )
     return pl.pallas_call(
         context_kernel,
         grid_spec=grid_spec,
-        out_shape=jax.ShapeDtypeStruct(
-            (pair, requests, pieces // pair, kv_dev, head_dim + 16, width), jnp.bfloat16
-        ),
-    )(use_rows, own_lengths, queries, kp, vp, ko, vo)
+        out_shape=[
+            jax.ShapeDtypeStruct((requests, pieces // pair, kv_dev, head_dim + 16, width), jnp.bfloat16)
+        ]
+        * 2,
+    )(use_rows, own_lengths, core.reshape(1).astype(jnp.int32), queries, kp, vp, ko, vo)
 
 
 SEQ = ("sx", "sy", "sc")
 
 
-def pair_kernel(core_ref, keep_ref, recv_ref, out_ref):
+def pair_kernel(keep_ref, recv_ref, out_ref):
     head_dim = out_ref.shape[-2] - 16
     for i in range(out_ref.shape[0]):
         for k in range(out_ref.shape[1]):
-            keep = keep_ref[0, i, k].astype(jnp.float32)
-            recv = recv_ref[0, i, k].astype(jnp.float32)
+            keep = keep_ref[i, k].astype(jnp.float32)
+            recv = recv_ref[i, k].astype(jnp.float32)
             keep_top = keep[head_dim : head_dim + 1]
             recv_top = recv[head_dim : head_dim + 1]
             pair_top = jnp.maximum(keep_top, recv_top)
-            scaled = keep * jnp.exp(keep_top - pair_top) + recv * jnp.exp(recv_top - pair_top)
-            totals = scaled[head_dim + 1 : head_dim + 2] + scaled[head_dim + 2 : head_dim + 3]
+            keep_factor = jnp.exp(keep_top - pair_top)
+            recv_factor = jnp.exp(recv_top - pair_top)
+            out_ref[i, k, 0:head_dim] = (
+                keep[0:head_dim] * keep_factor + recv[0:head_dim] * recv_factor
+            ).astype(out_ref.dtype)
+            scaled = keep[head_dim:] * keep_factor + recv[head_dim:] * recv_factor
+            totals = scaled[1:2] + scaled[2:3]
             high = totals.astype(jnp.bfloat16).astype(jnp.float32)
             low = totals - high
             row = lax.broadcasted_iota(jnp.int32, scaled.shape, 0)
             sent = jnp.where(
-                row < head_dim,
-                scaled,
-                jnp.where(
-                    row == head_dim,
-                    pair_top,
-                    jnp.where(row == head_dim + 1, high, jnp.where(row == head_dim + 2, low, 0.0)),
-                ),
+                row == 0,
+                pair_top,
+                jnp.where(row == 1, high, jnp.where(row == 2, low, 0.0)),
             )
-            out_ref[i, k] = sent.astype(out_ref.dtype)
-
-
-def pair_combine(core, parts, recv, steps):
-    pair, chunks, kv_dev, rows, width = parts.shape
+            out_ref[i, k, head_dim:] = sent.astype(out_ref.dtype)
+
+
+def pair_combine(keep, recv, steps):
+    chunks, kv_dev, rows, width = keep.shape
     per = chunks // steps
-    block = (1, per, kv_dev, rows, width)
-    grid_spec = pltpu.PrefetchScalarGridSpec(
-        num_scalar_prefetch=1,
+    block = (per, kv_dev, rows, width)
+    return pl.pallas_call(
+        pair_kernel,
         grid=(steps,),
         in_specs=[
-            pl.BlockSpec(block, lambda g, c: (c[0], g, 0, 0, 0)),
-            pl.BlockSpec(block, lambda g, c: (c[0], g, 0, 0, 0)),
+            pl.BlockSpec(block, lambda g: (g, 0, 0, 0)),
+            pl.BlockSpec(block, lambda g: (g, 0, 0, 0)),
         ],
-        out_specs=pl.BlockSpec((per, kv_dev, rows, width), lambda g, c: (g, 0, 0, 0)),
-    )
-    return pl.pallas_call(
-        pair_kernel,
-        grid_spec=grid_spec,
-        out_shape=jax.ShapeDtypeStruct((chunks, kv_dev, rows, width), parts.dtype),
-    )(core.reshape(1).astype(jnp.int32), parts, recv)
+        out_specs=pl.BlockSpec(block, lambda g: (g, 0, 0, 0)),
+        out_shape=jax.ShapeDtypeStruct(keep.shape, keep.dtype),
+    )(keep, recv)
 
 
 def unpack(parts, head_dim, axis):
@@ -228,13 +228,15 @@
     pair = lax.axis_size("sc")
     core = lax.axis_index("sc")
     own_lengths = jnp.clip(private_lengths - shard_index * private_dev, 0, private_dev)
-    acc = context_part(
-        queries, prefix_keys, prefix_values, block_use, own_lengths, private_keys, private_values, pieces, pair
+    mine, theirs = context_part(
+        queries, prefix_keys, prefix_values, block_use, own_lengths, private_keys, private_values, pieces, pair, core
     )
     width = chunk * group_size
-    parts = acc.reshape(pair, seq_size // pair, kv_dev, head_dim + 16, width)
-    recv = lax.ppermute(parts, "sc", [(i, (i + 1) % pair) for i in range(pair)])
-    sent = pair_combine(core, parts, recv, 4)
+    keep = mine.reshape(seq_size // pair, kv_dev, head_dim + 16, width)
+    recv = lax.ppermute(
+        theirs.reshape(keep.shape), "sc", [(i, (i + 1) % pair) for i in range(pair)]
+    )
+    sent = pair_combine(keep, recv, 4)
     got = lax.all_to_all(sent, ("sx", "sy"), 0, 0, tiled=True)
     part_top, part_totals, part_weighted = unpack(got, head_dim, 0)
     top_all = jnp.max(part_top, axis=0)

time: 160 us -> 159 us (level)
  waiting for transfers between devices: 37.4 us -> 33.8 us
    ppermute x1, waiting for transfers between devices: 8.24 us -> 4.71 us  [local(): lax.ppermute(theirs.reshape(keep.shape), 'sc', [(i, (i + 1) % pair) for i...]
    unnamed x11 -> x13, local copies, waits for them, and re-layouts: 6.3 us -> 7.69 us
where the time goes in v13:
time: 159 us; the launch traced here: 158 us
  blocking collectives  52.9 us (33%)
  Pallas kernels  39.3 us (25%)
  waiting for transfers between devices  33.8 us (21%)
  local copies, waits for them, and re-layouts  12.6 us (8%)
  matrix products  9.42 us (6%)
  starting transfers between devices  7.28 us (5%)
  other arithmetic  2.64 us (2%)
    pallas_call x1, Pallas kernels, context_part(): pl.pallas_call(context_kernel, grid_spec=grid_spec, out_shape=[jax.ShapeD...  34.4 us
    all_to_all x1, blocking collectives, local(): attention = lax.all_to_all(attention, ('sx', 'sy'), 0, 0, tiled=True)  32.4 us
    all_to_all x1, waiting for transfers between devices, local(): got = lax.all_to_all(sent, ('sx', 'sy'), 0, 0, tiled=True)  28.4 us
    all_to_all x1, blocking collectives, local(): return jnp.sum(lax.all_to_all(partial, 'heads', 0, 0, tiled=True), axis=0)  20.5 us
    unnamed x13, local copies, waits for them, and re-layouts  7.69 us
    all_to_all x1, starting transfers between devices, local(): got = lax.all_to_all(sent, ('sx', 'sy'), 0, 0, tiled=True)  7.28 us
    pallas_call x1, Pallas kernels, pair_combine(): pl.pallas_call(pair_kernel, grid=(steps,), in_specs=[pl.BlockSpec(block,...  4.8 us
    ppermute x1, waiting for transfers between devices, local(): lax.ppermute(theirs.reshape(keep.shape), 'sc', [(i, (i + 1) % pair) for i...  4.71 us
  transfers between devices with their start and end apart: 3, of which 3 were waited for; matrix products, arithmetic and copies ran while one was open for 6% of the time, Pallas kernels for 0%

profile of v13, /device:TPU:0, one launch (start us, length us, event | category | flops | bytes accessed | tf_op | source)
XLA Modules:
  0.0 158.2 jit_solution(6673291091231222192)
XLA Ops:
  0.0 0.0 copy-start.1
  0.0 1.9 %copy.66 = bf16[6,128,2,128]{3,1,0,2:T(8,128)(2,1)} copy(bf16[6,128,2,128]{3,2,1,0:T(2,128)(2,1)} %param.12) | data formatting | bytes 786432 | tf_op args[1]
  1.9 0.0 copy-start.4
  1.9 1.9 %copy.68 = bf16[768,2,128]{0,2,1:T(8,128)(2,1)} copy(bf16[768,2,128]{2,1,0:T(2,128)(2,1)} %bitcast.119) | data formatting | bytes 786432 | tf_op jit(solution)/shard_map/reshape | solution.py:121
  3.8 2.5 %copy.113 = bf16[8,256,2,128]{3,1,2,0:T(8,128)(2,1)} copy(bf16[8,256,2,128]{3,2,1,0:T(2,128)(2,1)} %param.15) | data formatting | bytes 2097152 | tf_op args[4]
  6.3 0.0 copy-done.1
  6.3 1.9 %copy.70 = bf16[8,256,2,128]{1,3,2,0:T(8,128)(2,1)} copy(bf16[8,256,2,128]{3,2,1,0:T(2,128)(2,1)S(1)} %copy-done.1) | data formatting | bytes 2097152 | tf_op args[5]
  8.2 0.0 copy-done.4
  8.2 0.6 subtract_clamp_fusion.len_ref
  8.8 34.4 %shard_map.109 = (bf16[8,2,2,144,256]{4,3,2,1,0:T(8,128)(2,1)}, bf16[8,2,2,144,256]{4,3,2,1,0:T(8,128)(2,1)}) custom-call(s32[8,6]{1,0:T(8,128)} %use_ref.1, s32[8]{0:T(128)} %subtract_clamp_fusion.len_ref, s32[1]{0:T(128)} %bitcast.core_ref, bf16[8,64,32,128]{3,2,1,0:T(8,128)(2,1)} %q_ref.1, bf16[2,768,128]{2,1,0:T(8,128)(2,1)} %bitcast.114, ...), custom_call_target="tpu_custom_call" | custom-call | tf_op jit(solution)/shard_map/pallas_call | solution.py:139
  43.3 0.0 collective-permute-start
  43.3 4.7 %collective-permute-done.recv_ref = bf16[16,2,144,256]{3,2,1,0:T(8,128)(2,1)S(1)} collective-permute-done((bf16[16,2,144,256]{3,2,1,0:T(8,128)(2,1)}, bf16[16,2,144,256]{3,2,1,0:T(8,128)(2,1)S(1)}, u32[]{:S(2)}, u32[]{:S(2)}) %collective-permute-start) | collective-permute-done | bytes 2359328 | tf_op jit(solution)/shard_map/ppermute | solution.py:236
  48.0 0.0 copy-start
  48.0 1.4 copy-done
  49.4 4.8 %shard_map.110 = bf16[16,2,144,256]{3,2,1,0:T(8,128)(2,1)} custom-call(bf16[16,2,144,256]{3,2,1,0:T(8,128)(2,1)} %bitcast.113, bf16[16,2,144,256]{3,2,1,0:T(8,128)(2,1)} %copy-done), custom_call_target="tpu_custom_call" | custom-call | tf_op jit(solution)/shard_map/pallas_call | solution.py:183
  54.2 0.0 copy-start.2
  54.2 7.3 %all-to-all-start = ((bf16[16,2,144,256]{3,2,1,0:T(8,128)(2,1)}), bf16[16,2,144,256]{3,2,1,0:T(8,128)(2,1)S(1)}, u32[]{:S(2)}, u32[]{:S(2)}) async-start(bf16[16,2,144,256]{3,2,1,0:T(8,128)(2,1)} %shard_map.110), calls=%async_computation | async-start | bytes 4718592 | tf_op jit(solution)/shard_map/all_to_all | solution.py:240
  61.5 0.0 copy-done.2
  61.5 0.5 convolution_minimum_fusion.4
  62.0 0.4 convolution_minimum_fusion.3
  62.4 0.4 convolution_minimum_fusion.2
  62.8 0.4 convolution_minimum_fusion.1
  63.2 0.4 convolution_minimum_fusion
  63.6 0.4 fusion.50
  64.0 0.8 constant_dynamic-slice_fusion
  64.8 0.9 constant_dynamic-slice_fusion.1
  65.8 0.3 fusion.47
  66.1 0.3 convolution_bitcast_fusion
  66.4 0.2 fusion.17
  66.6 0.1 squeeze_reshape.11
  66.7 0.1 squeeze_reshape.9
  66.8 28.4 %all-to-all-done = bf16[16,2,144,256]{3,2,1,0:T(8,128)(2,1)S(1)} async-done(((bf16[16,2,144,256]{3,2,1,0:T(8,128)(2,1)}), bf16[16,2,144,256]{3,2,1,0:T(8,128)(2,1)S(1)}, u32[]{:S(2)}, u32[]{:S(2)}) %all-to-all-start) | async-done | bytes 2359328 | tf_op jit(solution)/shard_map/all_to_all | solution.py:240
  95.2 0.1 fusion.46
  95.3 0.1 reshape.176
  95.4 0.4 multiply_reduce_fusion
  95.8 0.1 copy.72
  96.0 0.1 fusion.32
  96.1 0.1 fusion.37
  96.1 0.1 reshape.168
  96.2 0.1 reshape.169
  96.3 0.1 reshape.172
  96.4 0.3 fusion.14
  96.7 0.1 copy.82
  96.7 0.4 broadcast_in_dim.42
  97.1 32.4 %all_to_all.15 = bf16[16,16,32,128]{3,1,2,0:T(8,128)(2,1)S(1)} all-to-all(bf16[16,16,32,128]{3,1,2,0:T(8,128)(2,1)S(1)} %broadcast_in_dim.42), channel_id=1, replica_groups=mesh['heads'=4,'sx'=4,'sy'=4,'sc'=2] {'sx','sy'}, dimensions={0} | all-to-all | bytes 4194304 | tf_op jit(solution)/shard_map/all_to_all | solution.py:272
  129.6 0.0 collective-permute-start.1
  129.6 0.0 copy-start.3
  129.6 3.6 %fusion.4 = f32[16,16,512]{2,1,0:T(8,128)S(1)} fusion(bf16[16,16,32,128]{3,1,2,0:T(8,128)(2,1)S(1)} %all_to_all.15, bf16[32,128,512]{2,1,0:T(8,128)(2,1)} %param.21), kind=kOutput, calls=%fused_computation.5 | convolution fusion | flops 1073741824 | bytes 6815744 | tf_op jit(solution)/shard_map/xshd,hde->xse/dot_general | solution.py:274
  133.1 0.7 collective-permute-done.1
  133.8 0.0 copy-done.3
  133.9 2.9 %select_bitcast_fusion.1 = (f32[16,1,16,512]{3,2,0,1:T(8,128)S(1)}, f32[16,1,16,512]{3,2,0,1:T(8,128)S(1)}) fusion(f32[16,16,512]{2,1,0:T(8,128)S(1)} %fusion.4, pred[]{:T(512)S(6)} %eq.36, bf16[16,16,32,128]{3,1,2,0:T(8,128)(2,1)} %collective-permute-done.1, bf16[32,128,512]{2,1,0:T(8,128)(2,1)S(1)} %copy-done.3), kind=kOutput, calls=%fused_computation.19 | convolution fusion | flops 1074003968 | bytes 7864321 | tf_op jit(solution)/shard_map/xshd,hde->xse/dot_general | solution.py:275
  136.7 0.1 pad_maximum_fusion
  136.8 0.1 copy.83
  136.9 20.5 %all_to_all.16 = f32[4,2,64,512]{3,2,1,0:T(8,128)S(1)} all-to-all(f32[4,2,64,512]{3,2,1,0:T(8,128)S(1)} %bitcast.112), channel_id=1, replica_groups=mesh['heads'=4,'sx'=4,'sy'=4,'sc'=2] {'heads'}, dimensions={0} | all-to-all | bytes 2097152 | tf_op jit(solution)/shard_map/all_to_all | solution.py:281
  157.4 0.8 reduce_sum.39
  (11 shorter events, 0.2 us)
Async XLA Ops:
  0.0 6.3 %copy-start.1 = (bf16[8,256,2,128]{3,2,1,0:T(2,128)(2,1)S(1)}, bf16[8,256,2,128]{3,2,1,0:T(2,128)(2,1)}, u32[]{:S(2)}) copy-start(bf16[8,256,2,128]{3,2,1,0:T(2,128)(2,1)} %param.16) | copy-start | bytes 3145732
  1.9 6.3 %copy-start.4 = (s32[8]{0:T(128)S(1)}, s32[8]{0:T(128)}, u32[]{:S(2)}) copy-start(s32[8]{0:T(128)} %param.17) | copy-start | bytes 100
  43.3 4.7 %collective-permute-start = (bf16[16,2,144,256]{3,2,1,0:T(8,128)(2,1)}, bf16[16,2,144,256]{3,2,1,0:T(8,128)(2,1)S(1)}, u32[]{:S(2)}, u32[]{:S(2)}) collective-permute-start(bf16[16,2,144,256]{3,2,1,0:T(8,128)(2,1)} %bitcast.122), channel_id=1, source_target_pairs={{0,1},{1,0},{2,3},{3,2},{4,5},{5,4},{6,7},{7,6},{8,9},{9,8},{10,11... | collective-permute-start | bytes 7077896 | tf_op jit(solution)/shard_map/ppermute | solution.py:236
  48.0 1.4 copy-start
  54.2 7.3 %copy-start.2 = (s32[8,64]{1,0:T(8,128)S(1)}, s32[8,64]{1,0:T(8,128)}, u32[]{:S(2)}) copy-start(s32[8,64]{1,0:T(8,128)} %param.20) | copy-start | bytes 6148
  54.2 41.0 %all-to-all-start = ((bf16[16,2,144,256]{3,2,1,0:T(8,128)(2,1)}), bf16[16,2,144,256]{3,2,1,0:T(8,128)(2,1)S(1)}, u32[]{:S(2)}, u32[]{:S(2)}) async-start(bf16[16,2,144,256]{3,2,1,0:T(8,128)(2,1)} %shard_map.110), calls=%async_computation | async-start | bytes 4718592 | tf_op jit(solution)/shard_map/all_to_all | solution.py:240
  129.6 4.3 %collective-permute-start.1 = (bf16[16,16,32,128]{3,1,2,0:T(8,128)(2,1)S(1)}, bf16[16,16,32,128]{3,1,2,0:T(8,128)(2,1)}, u32[]{:S(2)}, u32[]{:S(2)}) collective-permute-start(bf16[16,16,32,128]{3,1,2,0:T(8,128)(2,1)S(1)} %all_to_all.15), channel_id=1, source_target_pairs={{0,1},{1,0},{2,3},{3,2},{4,5},{5,4},{6,7},{7,6},{8,9},{9,8},{10,11... | collective-permute-start | bytes 6291464 | tf_op jit(solution)/shard_map/ppermute | solution.py:273
  129.6 4.3 %copy-start.3 = (bf16[32,128,512]{2,1,0:T(8,128)(2,1)S(1)}, bf16[32,128,512]{2,1,0:T(8,128)(2,1)}, u32[]{:S(2)}) copy-start(bf16[32,128,512]{2,1,0:T(8,128)(2,1)} %param.21) | copy-start | bytes 12582916

commit v14 on v13

--- a/solution.py
+++ b/solution.py
@@ -236,7 +236,7 @@
     recv = lax.ppermute(
         theirs.reshape(keep.shape), "sc", [(i, (i + 1) % pair) for i in range(pair)]
     )
-    sent = pair_combine(keep, recv, 4)
+    sent = pair_combine(keep, recv, 2)
     got = lax.all_to_all(sent, ("sx", "sy"), 0, 0, tiled=True)
     part_top, part_totals, part_weighted = unpack(got, head_dim, 0)
     top_all = jnp.max(part_top, axis=0)
@@ -273,9 +273,9 @@
     other = lax.ppermute(attention, "sc", [(i, (i + 1) % pair) for i in range(pair)])
     mine = jnp.einsum("xshd,hde->xse", attention, out_weight, preferred_element_type=jnp.float32)
     theirs = jnp.einsum("xshd,hde->xse", other, out_weight, preferred_element_type=jnp.float32)
-    first = jnp.where(core == 0, mine, theirs)
-    second = jnp.where(core == 0, theirs, mine)
-    partial = jnp.stack([first, second], 1)
+    partial = jnp.zeros((mine.shape[0], pair) + mine.shape[1:], mine.dtype)
+    partial = lax.dynamic_update_index_in_dim(partial, mine, core, 1)
+    partial = lax.dynamic_update_index_in_dim(partial, theirs, pair - 1 - core, 1)
     heads_size = lax.axis_size("heads")
     partial = partial.reshape(heads_size, requests // heads_size, tree_size, partial.shape[-1])
     return jnp.sum(lax.all_to_all(partial, "heads", 0, 0, tiled=True), axis=0)

time: 159 us -> 156 us (0.981)
  local copies, waits for them, and re-layouts: 12.6 us -> 10.8 us
    unnamed x13 -> x17, local copies, waits for them, and re-layouts: 7.69 us -> 6.75 us
where the time goes in v14:
time: 156 us; the launch traced here: 155 us
  blocking collectives  52.9 us (34%)
  Pallas kernels  38.4 us (25%)
  waiting for transfers between devices  33.7 us (22%)
  local copies, waits for them, and re-layouts  10.8 us (7%)
  matrix products  9.38 us (6%)
  starting transfers between devices  7.29 us (5%)
  other arithmetic  2.54 us (2%)
    pallas_call x1, Pallas kernels, context_part(): pl.pallas_call(context_kernel, grid_spec=grid_spec, out_shape=[jax.ShapeD...  34.4 us
    all_to_all x1, blocking collectives, local(): attention = lax.all_to_all(attention, ('sx', 'sy'), 0, 0, tiled=True)  32.4 us
    all_to_all x1, waiting for transfers between devices, local(): got = lax.all_to_all(sent, ('sx', 'sy'), 0, 0, tiled=True)  28.4 us
    all_to_all x1, blocking collectives, local(): return jnp.sum(lax.all_to_all(partial, 'heads', 0, 0, tiled=True), axis=0)  20.5 us
    all_to_all x1, starting transfers between devices, local(): got = lax.all_to_all(sent, ('sx', 'sy'), 0, 0, tiled=True)  7.28 us
    unnamed x17, local copies, waits for them, and re-layouts  6.75 us
    ppermute x1, waiting for transfers between devices, local(): lax.ppermute(theirs.reshape(keep.shape), 'sc', [(i, (i + 1) % pair) for i...  4.71 us
    pallas_call x1, Pallas kernels, pair_combine(): pl.pallas_call(pair_kernel, grid=(steps,), in_specs=[pl.BlockSpec(block,...  3.92 us
  transfers between devices with their start and end apart: 3, of which 3 were waited for; matrix products, arithmetic and copies ran while one was open for 6% of the time, Pallas kernels for 0%

profile of v14, /device:TPU:0, one launch (start us, length us, event | category | flops | bytes accessed | tf_op | source)
XLA Modules:
  0.0 155.3 jit_solution(10252858119122406383)
XLA Ops:
  0.0 0.0 copy-start.1
  0.0 0.0 copy-start.2
  0.0 0.0 copy-start.3
  0.0 2.6 %copy.117 = bf16[8,256,2,128]{3,1,2,0:T(8,128)(2,1)} copy(bf16[8,256,2,128]{3,2,1,0:T(2,128)(2,1)} %param.15) | data formatting | bytes 2097152 | tf_op args[4]
  2.6 0.0 copy-done.1
  2.6 0.0 copy-start.6
  2.6 1.9 %copy.73 = bf16[8,256,2,128]{1,3,2,0:T(8,128)(2,1)} copy(bf16[8,256,2,128]{3,2,1,0:T(2,128)(2,1)S(1)} %copy-done.1) | data formatting | bytes 2097152 | tf_op args[5]
  4.5 0.0 copy-done.2
  4.5 0.8 copy.69
  5.4 0.0 copy-done.3
  5.4 1.0 copy.71
  6.4 0.0 copy-done.6
  6.4 0.6 subtract_clamp_fusion.len_ref
  7.0 34.4 %shard_map.109 = (bf16[8,2,2,144,256]{4,3,2,1,0:T(8,128)(2,1)}, bf16[8,2,2,144,256]{4,3,2,1,0:T(8,128)(2,1)}) custom-call(s32[8,6]{1,0:T(8,128)} %use_ref.1, s32[8]{0:T(128)} %subtract_clamp_fusion.len_ref, s32[1]{0:T(128)} %bitcast.core_ref, bf16[8,64,32,128]{3,2,1,0:T(8,128)(2,1)} %q_ref.1, bf16[2,768,128]{2,1,0:T(8,128)(2,1)} %bitcast.120, ...), custom_call_target="tpu_custom_call" | custom-call | tf_op jit(solution)/shard_map/pallas_call | solution.py:139
  41.4 0.0 collective-permute-start
  41.5 4.7 %collective-permute-done.recv_ref = bf16[16,2,144,256]{3,2,1,0:T(8,128)(2,1)S(1)} collective-permute-done((bf16[16,2,144,256]{3,2,1,0:T(8,128)(2,1)}, bf16[16,2,144,256]{3,2,1,0:T(8,128)(2,1)S(1)}, u32[]{:S(2)}, u32[]{:S(2)}) %collective-permute-start) | collective-permute-done | bytes 2359328 | tf_op jit(solution)/shard_map/ppermute | solution.py:236
  46.2 0.0 copy-start
  46.2 1.4 copy-done
  47.6 3.9 %shard_map.110 = bf16[16,2,144,256]{3,2,1,0:T(8,128)(2,1)} custom-call(bf16[16,2,144,256]{3,2,1,0:T(8,128)(2,1)} %bitcast.119, bf16[16,2,144,256]{3,2,1,0:T(8,128)(2,1)} %copy-done), custom_call_target="tpu_custom_call" | custom-call | tf_op jit(solution)/shard_map/pallas_call | solution.py:183
  51.5 0.0 copy-start.4
  51.5 7.3 %all-to-all-start = ((bf16[16,2,144,256]{3,2,1,0:T(8,128)(2,1)}), bf16[16,2,144,256]{3,2,1,0:T(8,128)(2,1)S(1)}, u32[]{:S(2)}, u32[]{:S(2)}) async-start(bf16[16,2,144,256]{3,2,1,0:T(8,128)(2,1)} %shard_map.110), calls=%async_computation | async-start | bytes 4718592 | tf_op jit(solution)/shard_map/all_to_all | solution.py:240
  58.8 0.0 copy-done.4
  58.8 0.5 convolution_minimum_fusion.4
  59.3 0.4 convolution_minimum_fusion.3
  59.7 0.4 convolution_minimum_fusion.2
  60.1 0.4 convolution_minimum_fusion.1
  60.5 0.4 convolution_minimum_fusion
  60.9 0.4 fusion.54
  61.3 0.8 constant_dynamic-slice_fusion
  62.1 0.9 constant_dynamic-slice_fusion.1
  63.0 0.3 fusion.53
  63.3 0.2 fusion.23
  63.6 0.1 squeeze_reshape.11
  63.7 0.1 squeeze_reshape.9
  63.8 0.3 convolution_bitcast_fusion
  64.1 28.4 %all-to-all-done = bf16[16,2,144,256]{3,2,1,0:T(8,128)(2,1)S(1)} async-done(((bf16[16,2,144,256]{3,2,1,0:T(8,128)(2,1)}), bf16[16,2,144,256]{3,2,1,0:T(8,128)(2,1)S(1)}, u32[]{:S(2)}, u32[]{:S(2)}) %all-to-all-start) | async-done | bytes 2359328 | tf_op jit(solution)/shard_map/all_to_all | solution.py:240
  92.5 0.1 fusion.52
  92.6 0.1 reshape.176
  92.7 0.1 fusion.38
  92.7 0.1 fusion.43
  92.8 0.1 reshape.168
  92.9 0.1 reshape.169
  93.0 0.1 reshape.172
  93.1 0.4 multiply_reduce_fusion
  93.5 0.1 copy.75
  93.7 0.3 fusion.20
  93.9 0.1 copy.85
  94.0 0.4 broadcast_in_dim.53
  94.4 32.4 %all_to_all.15 = bf16[16,16,32,128]{3,1,2,0:T(8,128)(2,1)S(1)} all-to-all(bf16[16,16,32,128]{3,1,2,0:T(8,128)(2,1)S(1)} %broadcast_in_dim.53), channel_id=1, replica_groups=mesh['heads'=4,'sx'=4,'sy'=4,'sc'=2] {'sx','sy'}, dimensions={0} | all-to-all | bytes 4194304 | tf_op jit(solution)/shard_map/all_to_all | solution.py:272
  126.8 0.0 collective-permute-start.1
  126.8 0.1 broadcast_in_dim.48
  126.9 0.0 copy-start.5
  127.0 3.6 %fusion.7 = f32[16,2,16,512]{3,2,1,0:T(8,128)S(1)} fusion(f32[16,2,16,512]{3,2,1,0:T(8,128)S(1)} %broadcast_in_dim.48, s32[]{:T(128)S(6)} %select_n.51, bf16[16,16,32,128]{3,1,2,0:T(8,128)(2,1)S(1)} %all_to_all.15, bf16[32,128,512]{2,1,0:T(8,128)(2,1)} %param.21), kind=kOutput, calls=%fused_computation.6 | convolution fusion | flops 1073741824 | bytes 6815748 | tf_op jit(solution)/shard_map/xshd,hde->xse/dot_general | solution.py:274
  130.5 0.6 collective-permute-done.1
  131.1 0.0 copy-done.5
  131.1 2.8 %fusion.13 = f32[16,2,16,512]{3,2,1,0:T(8,128)S(1)} fusion(f32[16,2,16,512]{3,2,1,0:T(8,128)S(1)} %fusion.7, s32[]{:T(128)S(6)} %select_n.52, bf16[16,16,32,128]{3,1,2,0:T(8,128)(2,1)} %collective-permute-done.1, bf16[32,128,512]{2,1,0:T(8,128)(2,1)S(1)} %copy-done.5), kind=kOutput, calls=%fused_computation.8 | convolution fusion | flops 1073741824 | bytes 6815748 | tf_op jit(solution)/shard_map/xshd,hde->xse/dot_general | solution.py:275
  134.0 20.5 %all_to_all.16 = f32[4,2,64,512]{3,2,1,0:T(8,128)S(1)} all-to-all(f32[4,2,64,512]{3,2,1,0:T(8,128)S(1)} %bitcast.118), channel_id=1, replica_groups=mesh['heads'=4,'sx'=4,'sy'=4,'sc'=2] {'heads'}, dimensions={0} | all-to-all | bytes 2097152 | tf_op jit(solution)/shard_map/all_to_all | solution.py:281
  154.5 0.8 reduce_sum.39
  (11 shorter events, 0.2 us)
Async XLA Ops:
  0.0 2.6 %copy-start.1 = (bf16[8,256,2,128]{3,2,1,0:T(2,128)(2,1)S(1)}, bf16[8,256,2,128]{3,2,1,0:T(2,128)(2,1)}, u32[]{:S(2)}) copy-start(bf16[8,256,2,128]{3,2,1,0:T(2,128)(2,1)} %param.16) | copy-start | bytes 3145732
  0.0 4.5 %copy-start.2 = (bf16[6,128,2,128]{3,2,1,0:T(2,128)(2,1)S(1)}, bf16[6,128,2,128]{3,2,1,0:T(2,128)(2,1)}, u32[]{:S(2)}) copy-start(bf16[6,128,2,128]{3,2,1,0:T(2,128)(2,1)} %param.12) | copy-start | bytes 1179652
  0.0 5.4 %copy-start.3 = (bf16[6,128,2,128]{3,2,1,0:T(2,128)(2,1)S(1)}, bf16[6,128,2,128]{3,2,1,0:T(2,128)(2,1)}, u32[]{:S(2)}) copy-start(bf16[6,128,2,128]{3,2,1,0:T(2,128)(2,1)} %param.13) | copy-start | bytes 1179652
  2.6 3.8 %copy-start.6 = (s32[8]{0:T(128)S(1)}, s32[8]{0:T(128)}, u32[]{:S(2)}) copy-start(s32[8]{0:T(128)} %param.17) | copy-start | bytes 100
  41.4 4.7 %collective-permute-start = (bf16[16,2,144,256]{3,2,1,0:T(8,128)(2,1)}, bf16[16,2,144,256]{3,2,1,0:T(8,128)(2,1)S(1)}, u32[]{:S(2)}, u32[]{:S(2)}) collective-permute-start(bf16[16,2,144,256]{3,2,1,0:T(8,128)(2,1)} %bitcast.128), channel_id=1, source_target_pairs={{0,1},{1,0},{2,3},{3,2},{4,5},{5,4},{6,7},{7,6},{8,9},{9,8},{10,11... | collective-permute-start | bytes 7077896 | tf_op jit(solution)/shard_map/ppermute | solution.py:236
  46.2 1.4 copy-start
  51.5 7.3 %copy-start.4 = (s32[8,64]{1,0:T(8,128)S(1)}, s32[8,64]{1,0:T(8,128)}, u32[]{:S(2)}) copy-start(s32[8,64]{1,0:T(8,128)} %param.20) | copy-start | bytes 6148
  51.5 41.0 %all-to-all-start = ((bf16[16,2,144,256]{3,2,1,0:T(8,128)(2,1)}), bf16[16,2,144,256]{3,2,1,0:T(8,128)(2,1)S(1)}, u32[]{:S(2)}, u32[]{:S(2)}) async-start(bf16[16,2,144,256]{3,2,1,0:T(8,128)(2,1)} %shard_map.110), calls=%async_computation | async-start | bytes 4718592 | tf_op jit(solution)/shard_map/all_to_all | solution.py:240
  126.8 4.3 %collective-permute-start.1 = (bf16[16,16,32,128]{3,1,2,0:T(8,128)(2,1)S(1)}, bf16[16,16,32,128]{3,1,2,0:T(8,128)(2,1)}, u32[]{:S(2)}, u32[]{:S(2)}) collective-permute-start(bf16[16,16,32,128]{3,1,2,0:T(8,128)(2,1)S(1)} %all_to_all.15), channel_id=1, source_target_pairs={{0,1},{1,0},{2,3},{3,2},{4,5},{5,4},{6,7},{7,6},{8,9},{9,8},{10,11... | collective-permute-start | bytes 6291464 | tf_op jit(solution)/shard_map/ppermute | solution.py:273
  126.9 4.2 %copy-start.5 = (bf16[32,128,512]{2,1,0:T(8,128)(2,1)S(1)}, bf16[32,128,512]{2,1,0:T(8,128)(2,1)}, u32[]{:S(2)}) copy-start(bf16[32,128,512]{2,1,0:T(8,128)(2,1)} %param.21) | copy-start | bytes 12582916

commit v15 on v14

--- a/solution.py
+++ b/solution.py
@@ -236,7 +236,7 @@
     recv = lax.ppermute(
         theirs.reshape(keep.shape), "sc", [(i, (i + 1) % pair) for i in range(pair)]
     )
-    sent = pair_combine(keep, recv, 2)
+    sent = pair_combine(keep, recv, 1)
     got = lax.all_to_all(sent, ("sx", "sy"), 0, 0, tiled=True)
     part_top, part_totals, part_weighted = unpack(got, head_dim, 0)
     top_all = jnp.max(part_top, axis=0)

time: 156 us -> 157 us (level)
  no operation moved by 1% of the time
where the time goes in v15:
time: 157 us; the launch traced here: 156 us
  blocking collectives  52.9 us (34%)
  Pallas kernels  39.3 us (25%)
  waiting for transfers between devices  33.7 us (21%)
  local copies, waits for them, and re-layouts  10.8 us (7%)
  matrix products  9.39 us (6%)
  starting transfers between devices  7.29 us (5%)
  other arithmetic  2.54 us (2%)
    pallas_call x1, Pallas kernels, context_part(): pl.pallas_call(context_kernel, grid_spec=grid_spec, out_shape=[jax.ShapeD...  34.4 us
    all_to_all x1, blocking collectives, local(): attention = lax.all_to_all(attention, ('sx', 'sy'), 0, 0, tiled=True)  32.4 us
    all_to_all x1, waiting for transfers between devices, local(): got = lax.all_to_all(sent, ('sx', 'sy'), 0, 0, tiled=True)  28.4 us
    all_to_all x1, blocking collectives, local(): return jnp.sum(lax.all_to_all(partial, 'heads', 0, 0, tiled=True), axis=0)  20.5 us
    all_to_all x1, starting transfers between devices, local(): got = lax.all_to_all(sent, ('sx', 'sy'), 0, 0, tiled=True)  7.28 us
    unnamed x17, local copies, waits for them, and re-layouts  6.75 us
    pallas_call x1, Pallas kernels, pair_combine(): pl.pallas_call(pair_kernel, grid=(steps,), in_specs=[pl.BlockSpec(block,...  4.91 us
    ppermute x1, waiting for transfers between devices, local(): lax.ppermute(theirs.reshape(keep.shape), 'sc', [(i, (i + 1) % pair) for i...  4.71 us
  transfers between devices with their start and end apart: 3, of which 3 were waited for; matrix products, arithmetic and copies ran while one was open for 6% of the time, Pallas kernels for 0%

profile of v15, /device:TPU:0, one launch (start us, length us, event | category | flops | bytes accessed | tf_op | source)
XLA Modules:
  0.0 156.2 jit_solution(6992554360101541015)
XLA Ops:
  0.0 0.0 copy-start.1
  0.0 0.0 copy-start.2
  0.0 0.0 copy-start.3
  0.0 2.6 %copy.117 = bf16[8,256,2,128]{3,1,2,0:T(8,128)(2,1)} copy(bf16[8,256,2,128]{3,2,1,0:T(2,128)(2,1)} %param.15) | data formatting | bytes 2097152 | tf_op args[4]
  2.6 0.0 copy-done.1
  2.6 0.0 copy-start.6
  2.6 1.9 %copy.73 = bf16[8,256,2,128]{1,3,2,0:T(8,128)(2,1)} copy(bf16[8,256,2,128]{3,2,1,0:T(2,128)(2,1)S(1)} %copy-done.1) | data formatting | bytes 2097152 | tf_op args[5]
  4.5 0.0 copy-done.2
  4.5 0.8 copy.69
  5.4 0.0 copy-done.3
  5.4 1.0 copy.71
  6.4 0.0 copy-done.6
  6.4 0.6 subtract_clamp_fusion.len_ref
  7.0 34.4 %shard_map.109 = (bf16[8,2,2,144,256]{4,3,2,1,0:T(8,128)(2,1)}, bf16[8,2,2,144,256]{4,3,2,1,0:T(8,128)(2,1)}) custom-call(s32[8,6]{1,0:T(8,128)} %use_ref.1, s32[8]{0:T(128)} %subtract_clamp_fusion.len_ref, s32[1]{0:T(128)} %bitcast.core_ref, bf16[8,64,32,128]{3,2,1,0:T(8,128)(2,1)} %q_ref.1, bf16[2,768,128]{2,1,0:T(8,128)(2,1)} %bitcast.120, ...), custom_call_target="tpu_custom_call" | custom-call | tf_op jit(solution)/shard_map/pallas_call | solution.py:139
  41.4 0.0 collective-permute-start
  41.5 4.7 %collective-permute-done.recv_ref = bf16[16,2,144,256]{3,2,1,0:T(8,128)(2,1)S(1)} collective-permute-done((bf16[16,2,144,256]{3,2,1,0:T(8,128)(2,1)}, bf16[16,2,144,256]{3,2,1,0:T(8,128)(2,1)S(1)}, u32[]{:S(2)}, u32[]{:S(2)}) %collective-permute-start) | collective-permute-done | bytes 2359328 | tf_op jit(solution)/shard_map/ppermute | solution.py:236
  46.2 0.0 copy-start
  46.2 1.4 copy-done
  47.6 4.9 %shard_map.110 = bf16[16,2,144,256]{3,2,1,0:T(8,128)(2,1)} custom-call(bf16[16,2,144,256]{3,2,1,0:T(8,128)(2,1)} %bitcast.119, bf16[16,2,144,256]{3,2,1,0:T(8,128)(2,1)} %copy-done), custom_call_target="tpu_custom_call" | custom-call | tf_op jit(solution)/shard_map/pallas_call | solution.py:183
  52.5 0.0 copy-start.4
  52.5 7.3 %all-to-all-start = ((bf16[16,2,144,256]{3,2,1,0:T(8,128)(2,1)}), bf16[16,2,144,256]{3,2,1,0:T(8,128)(2,1)S(1)}, u32[]{:S(2)}, u32[]{:S(2)}) async-start(bf16[16,2,144,256]{3,2,1,0:T(8,128)(2,1)} %shard_map.110), calls=%async_computation | async-start | bytes 4718592 | tf_op jit(solution)/shard_map/all_to_all | solution.py:240
  59.8 0.0 copy-done.4
  59.8 0.5 convolution_minimum_fusion.4
  60.3 0.4 convolution_minimum_fusion.3
  60.7 0.4 convolution_minimum_fusion.2
  61.1 0.4 convolution_minimum_fusion.1
  61.5 0.4 convolution_minimum_fusion
  61.9 0.4 fusion.54
  62.3 0.8 constant_dynamic-slice_fusion
  63.1 0.9 constant_dynamic-slice_fusion.1
  64.0 0.3 fusion.53
  64.3 0.2 fusion.23
  64.6 0.1 squeeze_reshape.11
  64.7 0.1 squeeze_reshape.9
  64.8 0.3 convolution_bitcast_fusion
  65.1 28.4 %all-to-all-done = bf16[16,2,144,256]{3,2,1,0:T(8,128)(2,1)S(1)} async-done(((bf16[16,2,144,256]{3,2,1,0:T(8,128)(2,1)}), bf16[16,2,144,256]{3,2,1,0:T(8,128)(2,1)S(1)}, u32[]{:S(2)}, u32[]{:S(2)}) %all-to-all-start) | async-done | bytes 2359328 | tf_op jit(solution)/shard_map/all_to_all | solution.py:240
  93.5 0.1 fusion.52
  93.6 0.1 reshape.176
  93.7 0.1 fusion.38
  93.7 0.1 fusion.43
  93.8 0.1 reshape.168
  93.9 0.1 reshape.169
  94.0 0.1 reshape.172
  94.1 0.4 multiply_reduce_fusion
  94.5 0.1 copy.75
  94.7 0.3 fusion.20
  94.9 0.1 copy.85
  95.0 0.4 broadcast_in_dim.53
  95.4 32.4 %all_to_all.15 = bf16[16,16,32,128]{3,1,2,0:T(8,128)(2,1)S(1)} all-to-all(bf16[16,16,32,128]{3,1,2,0:T(8,128)(2,1)S(1)} %broadcast_in_dim.53), channel_id=1, replica_groups=mesh['heads'=4,'sx'=4,'sy'=4,'sc'=2] {'sx','sy'}, dimensions={0} | all-to-all | bytes 4194304 | tf_op jit(solution)/shard_map/all_to_all | solution.py:272
  127.8 0.0 collective-permute-start.1
  127.8 0.1 broadcast_in_dim.48
  127.9 0.0 copy-start.5
  127.9 3.6 %fusion.7 = f32[16,2,16,512]{3,2,1,0:T(8,128)S(1)} fusion(f32[16,2,16,512]{3,2,1,0:T(8,128)S(1)} %broadcast_in_dim.48, s32[]{:T(128)S(6)} %select_n.51, bf16[16,16,32,128]{3,1,2,0:T(8,128)(2,1)S(1)} %all_to_all.15, bf16[32,128,512]{2,1,0:T(8,128)(2,1)} %param.21), kind=kOutput, calls=%fused_computation.6 | convolution fusion | flops 1073741824 | bytes 6815748 | tf_op jit(solution)/shard_map/xshd,hde->xse/dot_general | solution.py:274
  131.5 0.6 collective-permute-done.1
  132.1 0.0 copy-done.5
  132.1 2.8 %fusion.13 = f32[16,2,16,512]{3,2,1,0:T(8,128)S(1)} fusion(f32[16,2,16,512]{3,2,1,0:T(8,128)S(1)} %fusion.7, s32[]{:T(128)S(6)} %select_n.52, bf16[16,16,32,128]{3,1,2,0:T(8,128)(2,1)} %collective-permute-done.1, bf16[32,128,512]{2,1,0:T(8,128)(2,1)S(1)} %copy-done.5), kind=kOutput, calls=%fused_computation.8 | convolution fusion | flops 1073741824 | bytes 6815748 | tf_op jit(solution)/shard_map/xshd,hde->xse/dot_general | solution.py:275
  134.9 20.5 %all_to_all.16 = f32[4,2,64,512]{3,2,1,0:T(8,128)S(1)} all-to-all(f32[4,2,64,512]{3,2,1,0:T(8,128)S(1)} %bitcast.118), channel_id=1, replica_groups=mesh['heads'=4,'sx'=4,'sy'=4,'sc'=2] {'heads'}, dimensions={0} | all-to-all | bytes 2097152 | tf_op jit(solution)/shard_map/all_to_all | solution.py:281
  155.5 0.8 reduce_sum.39
  (11 shorter events, 0.2 us)
Async XLA Ops:
  0.0 2.6 %copy-start.1 = (bf16[8,256,2,128]{3,2,1,0:T(2,128)(2,1)S(1)}, bf16[8,256,2,128]{3,2,1,0:T(2,128)(2,1)}, u32[]{:S(2)}) copy-start(bf16[8,256,2,128]{3,2,1,0:T(2,128)(2,1)} %param.16) | copy-start | bytes 3145732
  0.0 4.5 %copy-start.2 = (bf16[6,128,2,128]{3,2,1,0:T(2,128)(2,1)S(1)}, bf16[6,128,2,128]{3,2,1,0:T(2,128)(2,1)}, u32[]{:S(2)}) copy-start(bf16[6,128,2,128]{3,2,1,0:T(2,128)(2,1)} %param.12) | copy-start | bytes 1179652
  0.0 5.4 %copy-start.3 = (bf16[6,128,2,128]{3,2,1,0:T(2,128)(2,1)S(1)}, bf16[6,128,2,128]{3,2,1,0:T(2,128)(2,1)}, u32[]{:S(2)}) copy-start(bf16[6,128,2,128]{3,2,1,0:T(2,128)(2,1)} %param.13) | copy-start | bytes 1179652
  2.6 3.8 %copy-start.6 = (s32[8]{0:T(128)S(1)}, s32[8]{0:T(128)}, u32[]{:S(2)}) copy-start(s32[8]{0:T(128)} %param.17) | copy-start | bytes 100
  41.4 4.7 %collective-permute-start = (bf16[16,2,144,256]{3,2,1,0:T(8,128)(2,1)}, bf16[16,2,144,256]{3,2,1,0:T(8,128)(2,1)S(1)}, u32[]{:S(2)}, u32[]{:S(2)}) collective-permute-start(bf16[16,2,144,256]{3,2,1,0:T(8,128)(2,1)} %bitcast.128), channel_id=1, source_target_pairs={{0,1},{1,0},{2,3},{3,2},{4,5},{5,4},{6,7},{7,6},{8,9},{9,8},{10,11... | collective-permute-start | bytes 7077896 | tf_op jit(solution)/shard_map/ppermute | solution.py:236
  46.2 1.4 copy-start
  52.5 7.3 %copy-start.4 = (s32[8,64]{1,0:T(8,128)S(1)}, s32[8,64]{1,0:T(8,128)}, u32[]{:S(2)}) copy-start(s32[8,64]{1,0:T(8,128)} %param.20) | copy-start | bytes 6148
  52.5 41.0 %all-to-all-start = ((bf16[16,2,144,256]{3,2,1,0:T(8,128)(2,1)}), bf16[16,2,144,256]{3,2,1,0:T(8,128)(2,1)S(1)}, u32[]{:S(2)}, u32[]{:S(2)}) async-start(bf16[16,2,144,256]{3,2,1,0:T(8,128)(2,1)} %shard_map.110), calls=%async_computation | async-start | bytes 4718592 | tf_op jit(solution)/shard_map/all_to_all | solution.py:240
  127.8 4.3 %collective-permute-start.1 = (bf16[16,16,32,128]{3,1,2,0:T(8,128)(2,1)S(1)}, bf16[16,16,32,128]{3,1,2,0:T(8,128)(2,1)}, u32[]{:S(2)}, u32[]{:S(2)}) collective-permute-start(bf16[16,16,32,128]{3,1,2,0:T(8,128)(2,1)S(1)} %all_to_all.15), channel_id=1, source_target_pairs={{0,1},{1,0},{2,3},{3,2},{4,5},{5,4},{6,7},{7,6},{8,9},{9,8},{10,11... | collective-permute-start | bytes 6291464 | tf_op jit(solution)/shard_map/ppermute | solution.py:273
  127.9 4.2 %copy-start.5 = (bf16[32,128,512]{2,1,0:T(8,128)(2,1)S(1)}, bf16[32,128,512]{2,1,0:T(8,128)(2,1)}, u32[]{:S(2)}) copy-start(bf16[32,128,512]{2,1,0:T(8,128)(2,1)} %param.21) | copy-start | bytes 12582916

commit v16 on v14

--- a/solution.py
+++ b/solution.py
@@ -273,8 +273,7 @@
     other = lax.ppermute(attention, "sc", [(i, (i + 1) % pair) for i in range(pair)])
     mine = jnp.einsum("xshd,hde->xse", attention, out_weight, preferred_element_type=jnp.float32)
     theirs = jnp.einsum("xshd,hde->xse", other, out_weight, preferred_element_type=jnp.float32)
-    partial = jnp.zeros((mine.shape[0], pair) + mine.shape[1:], mine.dtype)
-    partial = lax.dynamic_update_index_in_dim(partial, mine, core, 1)
+    partial = jnp.broadcast_to(mine[:, None], (mine.shape[0], pair) + mine.shape[1:])
     partial = lax.dynamic_update_index_in_dim(partial, theirs, pair - 1 - core, 1)
     heads_size = lax.axis_size("heads")
     partial = partial.reshape(heads_size, requests // heads_size, tree_size, partial.shape[-1])

time: 156 us -> 158 us (1.013)
  local copies, waits for them, and re-layouts: 10.8 us -> 12.6 us
    unnamed x17 -> x13, local copies, waits for them, and re-layouts: 6.75 us -> 7.69 us
where the time goes in v16:
time: 158 us; the launch traced here: 157 us
  blocking collectives  52.9 us (33%)
  Pallas kernels  38.4 us (24%)
  waiting for transfers between devices  33.8 us (21%)
  local copies, waits for them, and re-layouts  12.6 us (8%)
  matrix products  9.39 us (6%)
  starting transfers between devices  7.28 us (5%)
  other arithmetic  2.56 us (2%)
    pallas_call x1, Pallas kernels, context_part(): pl.pallas_call(context_kernel, grid_spec=grid_spec, out_shape=[jax.ShapeD...  34.4 us
    all_to_all x1, blocking collectives, local(): attention = lax.all_to_all(attention, ('sx', 'sy'), 0, 0, tiled=True)  32.4 us
    all_to_all x1, waiting for transfers between devices, local(): got = lax.all_to_all(sent, ('sx', 'sy'), 0, 0, tiled=True)  28.4 us
    all_to_all x1, blocking collectives, local(): return jnp.sum(lax.all_to_all(partial, 'heads', 0, 0, tiled=True), axis=0)  20.5 us
    unnamed x13, local copies, waits for them, and re-layouts  7.69 us
    all_to_all x1, starting transfers between devices, local(): got = lax.all_to_all(sent, ('sx', 'sy'), 0, 0, tiled=True)  7.28 us
    ppermute x1, waiting for transfers between devices, local(): lax.ppermute(theirs.reshape(keep.shape), 'sc', [(i, (i + 1) % pair) for i...  4.71 us
    pallas_call x1, Pallas kernels, pair_combine(): pl.pallas_call(pair_kernel, grid=(steps,), in_specs=[pl.BlockSpec(block,...  3.92 us
  transfers between devices with their start and end apart: 3, of which 3 were waited for; matrix products, arithmetic and copies ran while one was open for 6% of the time, Pallas kernels for 0%

profile of v16, /device:TPU:0, one launch (start us, length us, event | category | flops | bytes accessed | tf_op | source)
XLA Modules:
  0.0 157.3 jit_solution(12520032985542839469)
XLA Ops:
  0.0 0.0 copy-start.1
  0.0 1.9 %copy.66 = bf16[6,128,2,128]{3,1,0,2:T(8,128)(2,1)} copy(bf16[6,128,2,128]{3,2,1,0:T(2,128)(2,1)} %param.12) | data formatting | bytes 786432 | tf_op args[1]
  1.9 0.0 copy-start.4
  1.9 1.9 %copy.68 = bf16[768,2,128]{0,2,1:T(8,128)(2,1)} copy(bf16[768,2,128]{2,1,0:T(2,128)(2,1)} %bitcast.118) | data formatting | bytes 786432 | tf_op jit(solution)/shard_map/reshape | solution.py:121
  3.8 2.5 %copy.113 = bf16[8,256,2,128]{3,1,2,0:T(8,128)(2,1)} copy(bf16[8,256,2,128]{3,2,1,0:T(2,128)(2,1)} %param.15) | data formatting | bytes 2097152 | tf_op args[4]
  6.3 0.0 copy-done.1
  6.3 1.9 %copy.70 = bf16[8,256,2,128]{1,3,2,0:T(8,128)(2,1)} copy(bf16[8,256,2,128]{3,2,1,0:T(2,128)(2,1)S(1)} %copy-done.1) | data formatting | bytes 2097152 | tf_op args[5]
  8.2 0.0 copy-done.4
  8.2 0.6 subtract_clamp_fusion.len_ref
  8.8 34.4 %shard_map.109 = (bf16[8,2,2,144,256]{4,3,2,1,0:T(8,128)(2,1)}, bf16[8,2,2,144,256]{4,3,2,1,0:T(8,128)(2,1)}) custom-call(s32[8,6]{1,0:T(8,128)} %use_ref.1, s32[8]{0:T(128)} %subtract_clamp_fusion.len_ref, s32[1]{0:T(128)} %bitcast.core_ref, bf16[8,64,32,128]{3,2,1,0:T(8,128)(2,1)} %q_ref.1, bf16[2,768,128]{2,1,0:T(8,128)(2,1)} %bitcast.113, ...), custom_call_target="tpu_custom_call" | custom-call | tf_op jit(solution)/shard_map/pallas_call | solution.py:139
  43.3 0.0 collective-permute-start
  43.3 4.7 %collective-permute-done.recv_ref = bf16[16,2,144,256]{3,2,1,0:T(8,128)(2,1)S(1)} collective-permute-done((bf16[16,2,144,256]{3,2,1,0:T(8,128)(2,1)}, bf16[16,2,144,256]{3,2,1,0:T(8,128)(2,1)S(1)}, u32[]{:S(2)}, u32[]{:S(2)}) %collective-permute-start) | collective-permute-done | bytes 2359328 | tf_op jit(solution)/shard_map/ppermute | solution.py:236
  48.0 0.0 copy-start
  48.0 1.4 copy-done
  49.4 3.9 %shard_map.110 = bf16[16,2,144,256]{3,2,1,0:T(8,128)(2,1)} custom-call(bf16[16,2,144,256]{3,2,1,0:T(8,128)(2,1)} %bitcast.112, bf16[16,2,144,256]{3,2,1,0:T(8,128)(2,1)} %copy-done), custom_call_target="tpu_custom_call" | custom-call | tf_op jit(solution)/shard_map/pallas_call | solution.py:183
  53.3 0.0 copy-start.2
  53.3 7.3 %all-to-all-start = ((bf16[16,2,144,256]{3,2,1,0:T(8,128)(2,1)}), bf16[16,2,144,256]{3,2,1,0:T(8,128)(2,1)S(1)}, u32[]{:S(2)}, u32[]{:S(2)}) async-start(bf16[16,2,144,256]{3,2,1,0:T(8,128)(2,1)} %shard_map.110), calls=%async_computation | async-start | bytes 4718592 | tf_op jit(solution)/shard_map/all_to_all | solution.py:240
  60.6 0.0 copy-done.2
  60.6 0.5 convolution_minimum_fusion.4
  61.1 0.4 convolution_minimum_fusion.3
  61.5 0.4 convolution_minimum_fusion.2
  61.9 0.4 convolution_minimum_fusion.1
  62.3 0.4 convolution_minimum_fusion
  62.7 0.4 fusion.51
  63.1 0.8 constant_dynamic-slice_fusion
  63.9 0.9 constant_dynamic-slice_fusion.1
  64.9 0.3 fusion.50
  65.2 0.3 convolution_bitcast_fusion
  65.5 0.2 fusion.20
  65.7 0.1 squeeze_reshape.11
  65.8 0.1 squeeze_reshape.9
  65.9 28.4 %all-to-all-done = bf16[16,2,144,256]{3,2,1,0:T(8,128)(2,1)S(1)} async-done(((bf16[16,2,144,256]{3,2,1,0:T(8,128)(2,1)}), bf16[16,2,144,256]{3,2,1,0:T(8,128)(2,1)S(1)}, u32[]{:S(2)}, u32[]{:S(2)}) %all-to-all-start) | async-done | bytes 2359328 | tf_op jit(solution)/shard_map/all_to_all | solution.py:240
  94.3 0.1 fusion.49
  94.4 0.1 reshape.177
  94.5 0.4 multiply_reduce_fusion
  94.9 0.1 copy.72
  95.1 0.1 fusion.35
  95.2 0.1 fusion.40
  95.2 0.1 reshape.169
  95.3 0.1 reshape.170
  95.4 0.1 reshape.173
  95.5 0.3 fusion.17
  95.8 0.1 copy.82
  95.8 0.4 broadcast_in_dim.52
  96.3 32.4 %all_to_all.15 = bf16[16,16,32,128]{3,1,2,0:T(8,128)(2,1)S(1)} all-to-all(bf16[16,16,32,128]{3,1,2,0:T(8,128)(2,1)S(1)} %broadcast_in_dim.52), channel_id=1, replica_groups=mesh['heads'=4,'sx'=4,'sy'=4,'sc'=2] {'sx','sy'}, dimensions={0} | all-to-all | bytes 4194304 | tf_op jit(solution)/shard_map/all_to_all | solution.py:272
  128.7 0.0 collective-permute-start.1
  128.7 0.0 copy-start.3
  128.7 3.6 %fusion.4 = f32[16,16,512]{2,1,0:T(8,128)S(1)} fusion(bf16[16,16,32,128]{3,1,2,0:T(8,128)(2,1)S(1)} %all_to_all.15, bf16[32,128,512]{2,1,0:T(8,128)(2,1)} %param.21), kind=kOutput, calls=%fused_computation.5 | convolution fusion | flops 1073741824 | bytes 6815744 | tf_op jit(solution)/shard_map/xshd,hde->xse/dot_general | solution.py:274
  132.3 0.7 collective-permute-done.1
  133.0 0.1 broadcast_in_dim.53
  133.1 0.0 copy-done.3
  133.1 2.8 %fusion.10 = f32[16,2,16,512]{3,2,1,0:T(8,128)S(1)} fusion(f32[16,2,16,512]{3,2,1,0:T(8,128)S(1)} %broadcast_in_dim.53, s32[]{:T(128)S(6)} %select_n.48, bf16[16,16,32,128]{3,1,2,0:T(8,128)(2,1)} %collective-permute-done.1, bf16[32,128,512]{2,1,0:T(8,128)(2,1)S(1)} %copy-done.3), kind=kOutput, calls=%fused_computation.7 | convolution fusion | flops 1073741824 | bytes 6815748 | tf_op jit(solution)/shard_map/xshd,hde->xse/dot_general | solution.py:275
  136.0 20.5 %all_to_all.16 = f32[4,2,64,512]{3,2,1,0:T(8,128)S(1)} all-to-all(f32[4,2,64,512]{3,2,1,0:T(8,128)S(1)} %bitcast.111), channel_id=1, replica_groups=mesh['heads'=4,'sx'=4,'sy'=4,'sc'=2] {'heads'}, dimensions={0} | all-to-all | bytes 2097152 | tf_op jit(solution)/shard_map/all_to_all | solution.py:280
  156.5 0.8 reduce_sum.39
  (11 shorter events, 0.2 us)
Async XLA Ops:
  0.0 6.3 %copy-start.1 = (bf16[8,256,2,128]{3,2,1,0:T(2,128)(2,1)S(1)}, bf16[8,256,2,128]{3,2,1,0:T(2,128)(2,1)}, u32[]{:S(2)}) copy-start(bf16[8,256,2,128]{3,2,1,0:T(2,128)(2,1)} %param.16) | copy-start | bytes 3145732
  1.9 6.3 %copy-start.4 = (s32[8]{0:T(128)S(1)}, s32[8]{0:T(128)}, u32[]{:S(2)}) copy-start(s32[8]{0:T(128)} %param.17) | copy-start | bytes 100
  43.3 4.7 %collective-permute-start = (bf16[16,2,144,256]{3,2,1,0:T(8,128)(2,1)}, bf16[16,2,144,256]{3,2,1,0:T(8,128)(2,1)S(1)}, u32[]{:S(2)}, u32[]{:S(2)}) collective-permute-start(bf16[16,2,144,256]{3,2,1,0:T(8,128)(2,1)} %bitcast.121), channel_id=1, source_target_pairs={{0,1},{1,0},{2,3},{3,2},{4,5},{5,4},{6,7},{7,6},{8,9},{9,8},{10,11... | collective-permute-start | bytes 7077896 | tf_op jit(solution)/shard_map/ppermute | solution.py:236
  48.0 1.4 copy-start
  53.3 7.3 %copy-start.2 = (s32[8,64]{1,0:T(8,128)S(1)}, s32[8,64]{1,0:T(8,128)}, u32[]{:S(2)}) copy-start(s32[8,64]{1,0:T(8,128)} %param.20) | copy-start | bytes 6148
  53.3 41.0 %all-to-all-start = ((bf16[16,2,144,256]{3,2,1,0:T(8,128)(2,1)}), bf16[16,2,144,256]{3,2,1,0:T(8,128)(2,1)S(1)}, u32[]{:S(2)}, u32[]{:S(2)}) async-start(bf16[16,2,144,256]{3,2,1,0:T(8,128)(2,1)} %shard_map.110), calls=%async_computation | async-start | bytes 4718592 | tf_op jit(solution)/shard_map/all_to_all | solution.py:240
  128.7 4.3 %collective-permute-start.1 = (bf16[16,16,32,128]{3,1,2,0:T(8,128)(2,1)S(1)}, bf16[16,16,32,128]{3,1,2,0:T(8,128)(2,1)}, u32[]{:S(2)}, u32[]{:S(2)}) collective-permute-start(bf16[16,16,32,128]{3,1,2,0:T(8,128)(2,1)S(1)} %all_to_all.15), channel_id=1, source_target_pairs={{0,1},{1,0},{2,3},{3,2},{4,5},{5,4},{6,7},{7,6},{8,9},{9,8},{10,11... | collective-permute-start | bytes 6291464 | tf_op jit(solution)/shard_map/ppermute | solution.py:273
  128.7 4.4 %copy-start.3 = (bf16[32,128,512]{2,1,0:T(8,128)(2,1)S(1)}, bf16[32,128,512]{2,1,0:T(8,128)(2,1)}, u32[]{:S(2)}) copy-start(bf16[32,128,512]{2,1,0:T(8,128)(2,1)} %param.21) | copy-start | bytes 12582916
